TPU v7x, 32 devices: a whole 2x2x4 slice. The times are simulated.
32 devices in a mesh: dp: 8 (over z, y), tensor: 4 (over x, core).
Axes of the slice: x: 2, y: 2, z: 4, core: 2. Of those that a mesh axis runs over, the one named last changes fastest.
Arguments:
- hidden_in: bfloat16 [4096, 768], P('dp'), may hold values from -6 to 6
- out_cotangent: bfloat16 [4096, 768], P('dp'), may hold values from -6 to 6
- class_label: int32 [16], replicated, may hold values from 0 to 1000
- time_step: int32 [16], replicated, may hold values from 0 to 999
- modulation_weight: bfloat16 [768, 4608], P(None, 'tensor'), may hold values from -0.21875 to 0.21875
- modulation_bias: bfloat16 [4608], P('tensor'), may hold values from -3 to 3
- heads_weight: bfloat16 [768, 3, 768], P(None, None, 'tensor'), may hold values from -0.15625 to 0.15625
- heads_bias: bfloat16 [2, 768], P(None, 'tensor'), may hold values from -3 to 3
- mixing_weight: bfloat16 [768, 768], P('tensor'), may hold values from -1.25 to 1.25
- mixing_bias: bfloat16 [768], replicated, may hold values from -3 to 3
- up_weight: bfloat16 [768, 3072], P(None, 'tensor'), may hold values from -0.15625 to 0.15625
- up_bias: bfloat16 [3072], P('tensor'), may hold values from -3 to 3
- down_weight: bfloat16 [3072, 768], P('tensor'), may hold values from -0.109375 to 0.109375
- down_bias: bfloat16 [768], replicated, may hold values from -3 to 3
- class_table: bfloat16 [1001, 768], P(None, 'tensor'), may hold values from -6 to 6
- time_table: bfloat16 [1000, 768], P(None, 'tensor'), may hold values from -6 to 6
Outputs:
- block_out: bfloat16 [4096, 768], P('dp')
- input_grad: float32 [4096, 768], P('dp')
- modulation_weight_grad: float32 [768, 4608], P(None, 'tensor')
- modulation_bias_grad: float32 [4608], P('tensor')
- heads_weight_grad: float32 [768, 3, 768], P(None, None, 'tensor')
- heads_bias_grad: float32 [2, 768], P(None, 'tensor')
- mixing_weight_grad: float32 [768, 768], P('tensor')
- mixing_bias_grad: float32 [768], replicated
- up_weight_grad: float32 [768, 3072], P(None, 'tensor')
- up_bias_grad: float32 [3072], P('tensor')
- down_weight_grad: float32 [3072, 768], P('tensor')
- down_bias_grad: float32 [768], replicated
- class_table_grad: float32 [1001, 768], P(None, 'tensor')
- time_table_grad: float32 [1000, 768], P(None, 'tensor')
All inputs are finite; a program needn't handle non-finite values.
Results may differ from a plain program's by a relative error of at most 0.023.
Values sent between devices are 32-bit elements; how exact they have to be, the bound alone decides.
No kernel may reach another device: no remote copies, remote signals or barrier semaphores. Data moves between devices by JAX's collectives and lax.ppermute only.
A program may use at most 128 MiB of HBM per device.

v0:
```python
import jax
import jax.numpy as jnp
from jax import lax
from jax.sharding import PartitionSpec as P

SEQ = 256
HEAD_DIM = 64


def layer_norm(values):
    centered = values - jnp.mean(values, axis=-1, keepdims=True)
    variance = jnp.mean(centered * centered, axis=-1, keepdims=True)
    inverse = lax.rsqrt(variance + 1e-06)
    return (centered * inverse, inverse)


def norm_back(upstream, normed, inverse):
    mean_grad = jnp.mean(upstream, axis=-1, keepdims=True)
    mean_proj = jnp.mean(upstream * normed, axis=-1, keepdims=True)
    return inverse * (upstream - mean_grad - normed * mean_proj)


def gelu_tanh(values):
    return jax.nn.gelu(values, approximate=True)


def on_device(
    hidden_in,
    out_cotangent,
    class_label,
    time_step,
    modulation_weight,
    modulation_bias,
    heads_weight,
    heads_bias,
    mixing_weight,
    mixing_bias,
    up_weight,
    up_bias,
    down_weight,
    down_bias,
    class_table,
    time_table,
):
    model_width = hidden_in.shape[1]
    own_latents = hidden_in.shape[0] // SEQ
    tok_rows = own_latents * SEQ
    heads_here = heads_weight.shape[2] // HEAD_DIM
    score_scale = HEAD_DIM ** (-0.5)
    lat_first = lax.axis_index("dp") * own_latents
    my_labels = lax.dynamic_slice_in_dim(class_label, lat_first, own_latents)
    my_steps = lax.dynamic_slice_in_dim(time_step, lat_first, own_latents)
    cond_part = jnp.take(class_table, my_labels, axis=0).astype(jnp.float32) + jnp.take(
        time_table, my_steps, axis=0
    ).astype(jnp.float32)
    condition = lax.all_gather(cond_part, "tensor", axis=1, tiled=True)
    silu_cond = jax.nn.silu(condition).astype(jnp.bfloat16)
    mod_part = jnp.dot(
        silu_cond, modulation_weight, preferred_element_type=jnp.float32
    ) + modulation_bias.astype(jnp.float32)
    modulation = lax.all_gather(mod_part, "tensor", axis=1, tiled=True)
    pieces = [
        modulation[:, number * model_width : (number + 1) * model_width][:, None, :]
        for number in range(6)
    ]
    shift_one, scale_one, gate_one, shift_two, scale_two, gate_two = pieces
    states = hidden_in.astype(jnp.float32).reshape(own_latents, SEQ, model_width)
    normed_one, inverse_one = layer_norm(states)
    heads_in = (normed_one * (1.0 + scale_one) + shift_one).astype(jnp.bfloat16)
    projected = jnp.einsum(
        "bsd,dce->bsce", heads_in, heads_weight, preferred_element_type=jnp.float32
    )
    head_terms = heads_bias.astype(jnp.float32)
    shape_heads = (own_latents, SEQ, heads_here, HEAD_DIM)
    queries = (projected[:, :, 0] + head_terms[0]).astype(jnp.bfloat16).reshape(shape_heads)
    key_rows = projected[:, :, 1].astype(jnp.bfloat16).reshape(shape_heads)
    value_rows = (projected[:, :, 2] + head_terms[1]).astype(jnp.bfloat16).reshape(shape_heads)
    scores = (
        jnp.einsum("bqhe,bkhe->bhqk", queries, key_rows, preferred_element_type=jnp.float32)
        * score_scale
    )
    row_max = jnp.max(scores, axis=-1, keepdims=True)
    exp_terms = jnp.exp(scores - row_max)
    row_total = jnp.sum(exp_terms, axis=-1, keepdims=True)
    log_total = row_max + jnp.log(row_total)
    weights_low = (exp_terms / row_total).astype(jnp.bfloat16)
    attended = (
        jnp.einsum("bhqk,bkhe->bqhe", weights_low, value_rows, preferred_element_type=jnp.float32)
        .astype(jnp.bfloat16)
        .reshape(tok_rows, heads_here * HEAD_DIM)
    )
    attn_part = jnp.dot(attended, mixing_weight, preferred_element_type=jnp.float32)
    attn_out = (lax.psum(attn_part, "tensor") + mixing_bias.astype(jnp.float32)).reshape(
        own_latents, SEQ, model_width
    )
    middle = states + gate_one * attn_out
    normed_two, inverse_two = layer_norm(middle)
    mlp_in = (
        (normed_two * (1.0 + scale_two) + shift_two)
        .astype(jnp.bfloat16)
        .reshape(tok_rows, model_width)
    )
    pre_act = jnp.dot(mlp_in, up_weight, preferred_element_type=jnp.float32) + up_bias.astype(
        jnp.float32
    )
    activated = gelu_tanh(pre_act).astype(jnp.bfloat16)
    mlp_part = jnp.dot(activated, down_weight, preferred_element_type=jnp.float32)
    mlp_out = (lax.psum(mlp_part, "tensor") + down_bias.astype(jnp.float32)).reshape(
        own_latents, SEQ, model_width
    )
    result = middle + gate_two * mlp_out
    block_out = result.reshape(tok_rows, model_width).astype(jnp.bfloat16)
    upstream = out_cotangent.astype(jnp.float32).reshape(own_latents, SEQ, model_width)
    d_gate_two = jnp.sum(upstream * mlp_out, axis=1)
    d_mlp = (upstream * gate_two).astype(jnp.bfloat16).reshape(tok_rows, model_width)
    d_down_weight = jnp.einsum("tf,td->fd", activated, d_mlp, preferred_element_type=jnp.float32)
    d_down_bias = jnp.sum(d_mlp.astype(jnp.float32), axis=0)
    d_act = jnp.einsum("td,fd->tf", d_mlp, down_weight, preferred_element_type=jnp.float32)
    unused_out, gelu_pull = jax.vjp(gelu_tanh, pre_act)
    d_pre = gelu_pull(d_act)[0].astype(jnp.bfloat16)
    d_up_weight = jnp.einsum("td,tf->df", mlp_in, d_pre, preferred_element_type=jnp.float32)
    d_up_bias = jnp.sum(d_pre.astype(jnp.float32), axis=0)
    up_weight_sum, up_bias_sum, down_weight_sum, down_bias_sum = (
        d_up_weight,
        d_up_bias,
        d_down_weight,
        d_down_bias,
    )
    d_mlp_part = jnp.einsum("tf,df->td", d_pre, up_weight, preferred_element_type=jnp.float32)
    d_mlp_in = lax.psum(d_mlp_part, "tensor").reshape(own_latents, SEQ, model_width)
    d_shift_two = jnp.sum(d_mlp_in, axis=1)
    d_scale_two = jnp.sum(d_mlp_in * normed_two, axis=1)
    d_middle = upstream + norm_back(d_mlp_in * (1.0 + scale_two), normed_two, inverse_two)
    d_gate_one = jnp.sum(d_middle * attn_out, axis=1)
    d_attn = (d_middle * gate_one).astype(jnp.bfloat16).reshape(tok_rows, model_width)
    d_mixing_weight = jnp.einsum("te,td->ed", attended, d_attn, preferred_element_type=jnp.float32)
    d_mixing_bias = jnp.sum(d_attn.astype(jnp.float32), axis=0)
    d_attended = (
        jnp.einsum("td,ed->te", d_attn, mixing_weight, preferred_element_type=jnp.float32)
        .astype(jnp.bfloat16)
        .reshape(shape_heads)
    )
    scores_again = (
        jnp.einsum("bqhe,bkhe->bhqk", queries, key_rows, preferred_element_type=jnp.float32)
        * score_scale
    )
    weights_full = jnp.exp(scores_again - log_total)
    weights_back = weights_full.astype(jnp.bfloat16)
    d_weights = jnp.einsum(
        "bqhe,bkhe->bhqk", d_attended, value_rows, preferred_element_type=jnp.float32
    )
    row_dots = jnp.sum(weights_full * d_weights, axis=-1, keepdims=True)
    d_scores = (weights_full * (d_weights - row_dots)).astype(jnp.bfloat16)
    flat_heads = (own_latents, SEQ, heads_here * HEAD_DIM)
    d_queries = (
        (
            jnp.einsum("bhqk,bkhe->bqhe", d_scores, key_rows, preferred_element_type=jnp.float32)
            * score_scale
        )
        .astype(jnp.bfloat16)
        .reshape(flat_heads)
    )
    d_keys = (
        (
            jnp.einsum("bhqk,bqhe->bkhe", d_scores, queries, preferred_element_type=jnp.float32)
            * score_scale
        )
        .astype(jnp.bfloat16)
        .reshape(flat_heads)
    )
    d_values = (
        jnp.einsum("bhqk,bqhe->bkhe", weights_back, d_attended, preferred_element_type=jnp.float32)
        .astype(jnp.bfloat16)
        .reshape(flat_heads)
    )
    d_stack = jnp.stack([d_queries, d_keys, d_values], axis=2)
    d_heads_weight = jnp.einsum(
        "bsd,bsce->dce", heads_in, d_stack, preferred_element_type=jnp.float32
    )
    d_heads_bias = jnp.stack(
        [
            jnp.sum(d_queries.astype(jnp.float32), axis=(0, 1)),
            jnp.sum(d_values.astype(jnp.float32), axis=(0, 1)),
        ]
    )
    d_heads_part = jnp.einsum(
        "bsce,dce->bsd", d_stack, heads_weight, preferred_element_type=jnp.float32
    )
    d_heads_in = lax.psum(d_heads_part, "tensor")
    d_shift_one = jnp.sum(d_heads_in, axis=1)
    d_scale_one = jnp.sum(d_heads_in * normed_one, axis=1)
    input_grad = (
        d_middle + norm_back(d_heads_in * (1.0 + scale_one), normed_one, inverse_one)
    ).reshape(tok_rows, model_width)
    d_modulation = jnp.concatenate(
        [d_shift_one, d_scale_one, d_gate_one, d_shift_two, d_scale_two, d_gate_two], axis=1
    )
    own_cols = modulation_weight.shape[1]
    own_mods = lax.dynamic_slice_in_dim(
        d_modulation, lax.axis_index("tensor") * own_cols, own_cols, 1
    ).astype(jnp.bfloat16)
    d_mod_weight = jnp.einsum("ld,lc->dc", silu_cond, own_mods, preferred_element_type=jnp.float32)
    d_mod_bias = jnp.sum(own_mods.astype(jnp.float32), axis=0)
    d_silu_part = jnp.einsum(
        "lc,dc->ld", own_mods, modulation_weight, preferred_element_type=jnp.float32
    )
    d_silu_own = lax.psum_scatter(d_silu_part, "tensor", scatter_dimension=1, tiled=True)
    sigmoid_part = jax.nn.sigmoid(cond_part)
    d_condition = d_silu_own * sigmoid_part * (1.0 + cond_part * (1.0 - sigmoid_part))
    class_rows = class_table.shape[0]
    time_rows = time_table.shape[0]
    every_cond = lax.all_gather(d_condition, "dp", axis=0, tiled=True)
    class_sum = jax.ops.segment_sum(every_cond, class_label, num_segments=class_rows)
    time_sum = jax.ops.segment_sum(every_cond, time_step, num_segments=time_rows)
    (
        mod_weight_sum,
        mod_bias_sum,
        heads_weight_sum,
        heads_bias_sum,
        mixing_weight_sum,
        mixing_bias_sum,
        up_weight_sum,
        up_bias_sum,
        down_weight_sum,
        down_bias_sum,
    ) = lax.psum(
        (
            d_mod_weight,
            d_mod_bias,
            d_heads_weight,
            d_heads_bias,
            d_mixing_weight,
            d_mixing_bias,
            up_weight_sum,
            up_bias_sum,
            down_weight_sum,
            down_bias_sum,
        ),
        "dp",
    )
    return (
        block_out,
        input_grad,
        mod_weight_sum,
        mod_bias_sum,
        heads_weight_sum,
        heads_bias_sum,
        mixing_weight_sum,
        mixing_bias_sum,
        up_weight_sum,
        up_bias_sum,
        down_weight_sum,
        down_bias_sum,
        class_sum,
        time_sum,
    )


def solution(mesh):
    in_specs = (
        P("dp", None),
        P("dp", None),
        P(),
        P(),
        P(None, "tensor"),
        P("tensor"),
        P(None, None, "tensor"),
        P(None, "tensor"),
        P("tensor", None),
        P(),
        P(None, "tensor"),
        P("tensor"),
        P("tensor", None),
        P(),
        P(None, "tensor"),
        P(None, "tensor"),
    )
    out_specs = (
        P("dp", None),
        P("dp", None),
        P(None, "tensor"),
        P("tensor"),
        P(None, None, "tensor"),
        P(None, "tensor"),
        P("tensor", None),
        P(),
        P(None, "tensor"),
        P("tensor"),
        P("tensor", None),
        P(),
        P(None, "tensor"),
        P(None, "tensor"),
    )
    return jax.shard_map(
        on_device, mesh=mesh, in_specs=in_specs, out_specs=out_specs, check_vma=False
    )
```

profile of v0, /device:TPU:0, one launch (start us, length us, event | category | flops | bytes accessed | tf_op | source)
XLA Modules:
  0.0 601.4 jit_solution(7812551976983866752)
XLA Ops:
  7.3 1.5 convert_reduce_fusion.3
  8.8 1.5 multiply_reduce_fusion.7
  12.2 1.7 gather_fusion.1
  14.0 6.1 %all-gather = f32[4,192,2]{1,2,0:T(2,128)S(1)} all-gather(f32[1,192,2]{1,2,0:T(2,128)S(1)} %fusion.37), channel_id=1, replica_groups=mesh['dp'=8,'tensor'=4] {'tensor'}, dimensions={0}, use_global_device_ids=true | all-gather | bytes 7680 | tf_op jit(solution)/shard_map/all_gather | solution.py:56
  21.1 5.4 all_gather.10
  26.7 2.0 fusion.22
  32.2 1.6 fusion.55
  35.6 2.0 fusion.56
  37.6 40.8 %all-reduce.8.cloned.1.call-done = f32[512,768]{1,0:T(8,128)} async-done(((f32[512,768]{1,0:T(8,128)}), f32[512,768]{1,0:T(8,128)}) %all-reduce.8.cloned.1.call-update) | async-done | bytes 1572880 | tf_op jit(solution)/shard_map/psum | solution.py:93
  78.3 3.1 fusion.50
  83.2 3.4 convert_reduce_fusion.1
  87.5 2.0 fusion.57
  90.3 4.0 fusion.46
  94.2 38.3 %all-reduce.10.cloned.1.call-done = f32[512,768]{1,0:T(8,128)} async-done(((f32[512,768]{1,0:T(8,128)}), f32[512,768]{1,0:T(8,128)}) %all-reduce.10.cloned.1.call-update) | async-done | bytes 1572880 | tf_op jit(solution)/shard_map/psum | solution.py:130
  132.5 2.1 fusion.16
  139.0 2.6 convert_reduce_fusion.4
  145.2 2.0 convolution_bitcast_fusion.1
  149.7 3.7 fusion.59
  153.4 2.4 fusion.45
  158.2 2.4 fusion.58
  160.7 2.7 convolution_bitcast_fusion
  163.5 52.6 %all-reduce.14.cloned.1.call-done = (f32[512,768]{1,0:T(8,128)}, f32[2,256,768]{2,1,0:T(8,128)}) async-done(((f32[512,768]{1,0:T(8,128)}, f32[2,256,768]{2,1,0:T(8,128)}), (f32[512,768]{1,0:T(8,128)}, f32[2,256,768]{2,1,0:T(8,128)})) %all-reduce.14.cloned.1.call-update) | async-done | bytes 3145744 | tf_op jit(solution)/shard_map/psum | solution.py:108
  216.1 6.4 %multiply_reduce_fusion.8 = (f32[2,256]{1,0:T(2,128)S(1)}, f32[2,256]{1,0:T(2,128)S(1)}, bf16[2,768]{1,0:T(2,128)(2,1)S(1)}, bf16[2,768]{1,0:T(2,128)(2,1)S(1)},...) fusion(f32[2,256,768]{2,1,0:T(8,128)} %get-tuple-element.82, ...), kind=kLoop, calls=%fused_computation.58 | loop fusion | flops 12572672 | bytes 10279936 | tf_op jit(solution)/shard_map/reduce_sum | solution.py:18
  224.0 2.5 fusion.42
  227.4 2.5 fusion.10
  229.9 38.1 %all-reduce = (f32[1152]{0:T(1024)}, f32[2,192]{1,0:T(2,128)}, f32[768]{0:T(1024)}, f32[768]{0:T(1024)}, f32[768]{0:T(1024)}) all-reduce(f32[1152]{0:T(1024)S(1)} %get-tuple-element.89, f32[2,192]{1,0:T(2,128)S(1)} %pad_maximum_fusion.3, f32[768]{0:T(1024)S(1)} %copy-done.61, ...), channel_id=1, replica_groups=mesh['dp'=8,'tensor'=4] {'dp'}, use_global_device_ids=true, to_apply=%region_23.24 | all-reduce | flops 3840 | bytes 30720 | tf_op jit(solution)/shard_map/psum | solution.py:226
  268.1 4.3 multiply_add_fusion
  273.5 28.0 %all-gather.1 = f32[8,2,192]{2,1,0:T(2,128)S(1)} all-gather(f32[1,2,192]{2,1,0:T(2,128)S(1)} %multiply_bitcast_fusion), channel_id=1, replica_groups=mesh['dp'=8,'tensor'=4] {'dp'}, dimensions={0}, use_global_device_ids=true | all-gather | bytes 13824 | tf_op jit(solution)/shard_map/all_gather | solution.py:212
  302.5 1.8 scatter_custom_fusion.1
  305.4 2.4 copy.92
  307.9 276.3 %all-reduce.12.cloned.1.call-done = (f32[768,1152]{1,0:T(8,128)}, f32[768,3,192]{0,2,1:T(8,128)}, f32[192,768]{1,0:T(8,128)}, f32[768,768]{1,0:T(8,128)}, f32[768,768]{1,0:T(8,128)}) async-done(((f32[768,1152]{1,0:T(8,128)}, f32[768,3,192]{0,2,1:T(8,128)}, f32[192,768]{1,0:T(8,128)}, f32[768,768]{1,0:T(8,128)}, f32[768,768]{1,0:T(8,128)}), (f32[768,1152]{1,0:T(8,128)}, f32[768,3,192]{0,2,1:T(8,128)}, ...) | async-done | bytes 10616848 | tf_op jit(solution)/shard_map/psum | solution.py:226
  584.2 4.2 copy.125
  (258 shorter events, 36.8 us)
Async XLA Ops:
  7.2 13.6 %copy-start = (bf16[768,1152]{1,0:T(8,128)(2,1)S(1)}, bf16[768,1152]{1,0:T(8,128)(2,1)}, u32[]{:S(2)}) copy-start(bf16[768,1152]{1,0:T(8,128)(2,1)} %param.20) | copy-start | bytes 5308420
  7.3 71.1 %all-reduce.8.cloned.1.call-start = ((), (), s32[]{:S(2)}) async-start(), calls=%async_computation.1 | async-start | bytes 3145728 | tf_op jit(solution)/shard_map/psum | solution.py:93
  10.3 16.4 %copy-start.47 = (f32[2,256]{1,0:T(2,128)}, f32[2,256]{1,0:T(2,128)S(1)}, u32[]{:S(2)}) copy-start(f32[2,256]{1,0:T(2,128)S(1)} %div.49) | copy-start | bytes 6148
  10.5 16.1 %copy-start.3 = (bf16[512,768]{1,0:T(8,128)(2,1)S(1)}, bf16[512,768]{1,0:T(8,128)(2,1)}, u32[]{:S(2)}) copy-start(bf16[512,768]{1,0:T(8,128)(2,1)} %param.16) | copy-start | bytes 2359300
  10.6 10.5 %copy-start.71 = (pred[2]{0:T(512)(128)(4,1)}, pred[2]{0:T(512)(128)(4,1)S(1)}, u32[]{:S(2)}) copy-start(pred[2]{0:T(512)(128)(4,1)S(1)} %get-tuple-element.95) | copy-start | bytes 10
  10.6 18.0 %copy-start.73 = (pred[2]{0:T(512)(128)(4,1)}, pred[2]{0:T(512)(128)(4,1)S(1)}, u32[]{:S(2)}) copy-start(pred[2]{0:T(512)(128)(4,1)S(1)} %get-tuple-element.116) | copy-start | bytes 10
  12.2 16.5 %copy-start.62 = (bf16[2,192]{1,0:T(2,128)(2,1)}, bf16[2,192]{1,0:T(2,128)(2,1)S(1)}, u32[]{:S(2)}) copy-start(bf16[2,192]{1,0:T(2,128)(2,1)S(1)} %gather_fusion) | copy-start | bytes 2308
  13.9 14.8 %copy-start.64 = (bf16[2,192]{1,0:T(2,128)(2,1)}, bf16[2,192]{1,0:T(2,128)(2,1)S(1)}, u32[]{:S(2)}) copy-start(bf16[2,192]{1,0:T(2,128)(2,1)S(1)} %gather_fusion.1) | copy-start | bytes 2308
  26.6 7.3 %copy-start.41 = (f32[2,768]{1,0:T(2,128)}, f32[2,768]{1,0:T(2,128)S(1)}, u32[]{:S(2)}) copy-start(f32[2,768]{1,0:T(2,128)S(1)} %get-tuple-element.101) | copy-start | bytes 18436
  33.8 98.7 %all-reduce.10.cloned.1.call-start = ((), (), s32[]{:S(2)}) async-start(), calls=%async_computation.2 | async-start | bytes 3145728 | tf_op jit(solution)/shard_map/psum | solution.py:130
  81.4 53.3 %copy-start.36 = (f32[512]{0:T(512)}, f32[512]{0:T(512)S(1)}, u32[]{:S(2)}) copy-start(f32[512]{0:T(512)S(1)} %broadcast_multiply_fusion.4) | copy-start | bytes 6148
  81.7 52.9 %copy-start.45 = (f32[512]{0:T(512)}, f32[512]{0:T(512)S(1)}, u32[]{:S(2)}) copy-start(f32[512]{0:T(512)S(1)} %add_rsqrt_fusion) | copy-start | bytes 6148
  89.4 126.6 %all-reduce.14.cloned.1.call-start = ((), (), s32[]{:S(2)}) async-start(), calls=%async_computation.5 | async-start | bytes 6291456 | tf_op jit(solution)/shard_map/psum | solution.py:108
  141.6 3.5 copy-start.29
  147.2 125.2 %reduce-scatter.4.cloned.1.call-start = ((), (), s32[]{:S(2)}) async-start(), calls=%async_computation.3 | async-start | bytes 491520
  149.7 3.7 copy-start.24
  149.7 3.7 copy-start.87
  153.4 4.8 copy-start.18
  160.6 55.4 %copy-start.40 = (f32[2,768]{1,0:T(2,128)S(1)}, f32[2,768]{1,0:T(2,128)}, u32[]{:S(2)}) copy-start(f32[2,768]{1,0:T(2,128)} %copy-done.38) | copy-start | bytes 18436
  160.7 55.4 %copy-start.48 = (f32[2,256]{1,0:T(2,128)S(1)}, f32[2,256]{1,0:T(2,128)}, u32[]{:S(2)}) copy-start(f32[2,256]{1,0:T(2,128)} %copy-done.47) | copy-start | bytes 6148
  160.7 55.4 %copy-start.50 = (f32[2,256]{1,0:T(2,128)S(1)}, f32[2,256]{1,0:T(2,128)}, u32[]{:S(2)}) copy-start(f32[2,256]{1,0:T(2,128)} %copy-done.49) | copy-start | bytes 6148
  160.7 55.4 %copy-start.51 = (f32[2,256]{1,0:T(2,128)S(1)}, f32[2,256]{1,0:T(2,128)}, u32[]{:S(2)}) copy-start(f32[2,256]{1,0:T(2,128)} %div.57) | copy-start | bytes 6148
  160.7 55.4 %copy-start.52 = (f32[2,256]{1,0:T(2,128)S(1)}, f32[2,256]{1,0:T(2,128)}, u32[]{:S(2)}) copy-start(f32[2,256]{1,0:T(2,128)} %rsqrt.26) | copy-start | bytes 6148
  160.7 55.4 %copy-start.53 = (f32[2,256]{1,0:T(2,128)S(1)}, f32[2,256]{1,0:T(2,128)}, u32[]{:S(2)}) copy-start(f32[2,256]{1,0:T(2,128)} %div.59) | copy-start | bytes 6148
  160.7 55.4 %copy-start.54 = (f32[2,256]{1,0:T(2,128)S(1)}, f32[2,256]{1,0:T(2,128)}, u32[]{:S(2)}) copy-start(f32[2,256]{1,0:T(2,128)} %div.56) | copy-start | bytes 6148
  160.7 55.4 %copy-start.59 = (f32[768]{0:T(1024)S(1)}, f32[768]{0:T(1024)}, u32[]{:S(2)}) copy-start(f32[768]{0:T(1024)} %convert_element_type.143) | copy-start | bytes 9220
  224.0 360.2 %all-reduce.12.cloned.1.call-start = ((), (), s32[]{:S(2)}) async-start(), calls=%async_computation.4 | async-start | bytes 21233664 | tf_op jit(solution)/shard_map/psum | solution.py:226
  268.1 5.3 copy-start.63
  268.1 5.3 copy-start.65
  268.1 5.3 copy-start.72
  268.1 5.3 copy-start.74
  584.2 4.2 copy-start.16
  (61 other events, 109.4 us)
Sparse Core Ops, SparseCore 0:
  33.9 44.3 all-reduce.7
  89.6 42.8 all-reduce.9
  147.3 68.6 all-reduce.13
  224.1 20.9 reduce-scatter.3
  250.9 333.2 all-reduce.11
where the time goes:
time: 602 us; the launch traced here: 601 us
  waiting for transfers between devices  408 us (68%)
  blocking collectives  77.6 us (13%)
  matrix products  39.2 us (7%)
  local copies, waits for them, and re-layouts  32.5 us (5%)
  other arithmetic  29 us (5%)
  between operations  14.7 us (2%)
    psum x1, waiting for transfers between devices, on_device(): lax.psum((d_mod_weight, d_mod_bias, d_heads_weight, d_heads_bias, d_mixin...  276 us
    psum x1, waiting for transfers between devices, on_device(): lax.psum(mlp_part, 'tensor') + down_bias.astype(jnp.float32)  52.6 us
    psum x1, waiting for transfers between devices, on_device(): lax.psum(attn_part, 'tensor') + mixing_bias.astype(jnp.float32)  40.8 us
    psum x1, waiting for transfers between devices, on_device(): lax.psum(d_mlp_part, 'tensor').reshape(own_latents, SEQ, model_width)  38.3 us
    psum x1, blocking collectives, on_device(): lax.psum((d_mod_weight, d_mod_bias, d_heads_weight, d_heads_bias, d_mixin...  38.1 us
    all_gather x1, blocking collectives, on_device(): every_cond = lax.all_gather(d_condition, 'dp', axis=0, tiled=True)  28 us
    unnamed x194, local copies, waits for them, and re-layouts  25 us
  transfers between devices with their start and end apart: 5, of which 4 were waited for; matrix products, arithmetic and copies ran while one was open for 7% of the time, Pallas kernels for 0%

commit v1 on v0

v1 whole, which is shorter than its diff:
```python
import jax
import jax.numpy as jnp
from jax import lax
from jax.experimental import pallas as pl
from jax.experimental.pallas import tpu as pltpu
from jax.sharding import PartitionSpec as P

SEQ = 256
HEAD_DIM = 64
F32 = jnp.float32
BF16 = jnp.bfloat16


def layer_norm(values):
    centered = values - jnp.mean(values, axis=-1, keepdims=True)
    variance = jnp.mean(centered * centered, axis=-1, keepdims=True)
    inverse = lax.rsqrt(variance + 1e-06)
    return (centered * inverse, inverse)


def norm_back(upstream, normed, inverse):
    mean_grad = jnp.mean(upstream, axis=-1, keepdims=True)
    mean_proj = jnp.mean(upstream * normed, axis=-1, keepdims=True)
    return inverse * (upstream - mean_grad - normed * mean_proj)


def gelu_tanh(values):
    return jax.nn.gelu(values, approximate=True)


def swap(values, size, bit):
    return lax.ppermute(values, "tensor", [(at, at ^ bit) for at in range(size)])


def chip_pair(own, size, axis):
    far = lax.axis_index("tensor") >= 2
    across = swap(own, size, 2)
    return jnp.concatenate(
        [jnp.where(far, across, own), jnp.where(far, own, across)], axis=axis
    )


VMEM_LIMIT = 48 * 1024 * 1024
IN_VMEM = pl.BlockSpec(memory_space=pltpu.VMEM)
IN_SMEM = pl.BlockSpec(memory_space=pltpu.SMEM)


def call(kernel, out_shape, operands, scalars=1):
    return pl.pallas_call(
        kernel,
        out_shape=out_shape,
        in_specs=[IN_SMEM] * scalars + [IN_VMEM] * (len(operands) - scalars),
        out_specs=jax.tree.map(lambda leaf: IN_VMEM, out_shape),
        compiler_params=pltpu.CompilerParams(vmem_limit_bytes=VMEM_LIMIT),
    )(*operands)


def join_rows_kernel(odd_ref, own_ref, beside_ref, out_ref):
    half = own_ref.shape[0]
    odd = odd_ref[0] == 1
    own = own_ref[...].astype(BF16)
    beside = beside_ref[...].astype(BF16)
    out_ref[0:half, :] = jnp.where(odd, beside, own)
    out_ref[half : 2 * half, :] = jnp.where(odd, own, beside)


def mixing_kernel(odd_ref, own_ref, beside_ref, weight_ref, bias_ref, out_ref):
    half = own_ref.shape[1]
    odd = odd_ref[0] == 1
    own = own_ref[...].astype(BF16)
    beside = beside_ref[...].astype(BF16)
    low = jnp.where(odd, beside, own)
    high = jnp.where(odd, own, beside)
    out_ref[...] = (
        jnp.dot(low, weight_ref[0:half, :], preferred_element_type=F32)
        + jnp.dot(high, weight_ref[half : 2 * half, :], preferred_element_type=F32)
        + bias_ref[...].astype(F32)
    )


def modulation_grad_kernel(mods_ref, silu_ref, weight_ref, weight_grad_ref, bias_grad_ref, silu_grad_ref):
    mods = mods_ref[...].astype(BF16)
    weight_grad_ref[...] = lax.dot_general(
        silu_ref[...], mods, (((0,), (0,)), ((), ())), preferred_element_type=F32
    )
    bias_grad_ref[...] = jnp.sum(mods.astype(F32), axis=0, keepdims=True)
    silu_grad_ref[...] = lax.dot_general(
        mods, weight_ref[...], (((1,), (1,)), ((), ())), preferred_element_type=F32
    )


def reduce_rows(part, size):
    odd = lax.axis_index("tensor") % 2
    half = part.shape[0] // 2
    mine = lax.dynamic_slice_in_dim(part, odd * half, half)
    theirs = lax.dynamic_slice_in_dim(part, (1 - odd) * half, half)
    chip_sum = mine + swap(theirs, size, 1)
    full = chip_sum + swap(chip_sum, size, 2)
    other = swap(full, size, 1)
    flip = odd == 1
    return jnp.concatenate([jnp.where(flip, other, full), jnp.where(flip, full, other)], axis=0)


def on_device(
    tensor_size,
    dp_size,
    hidden_in,
    out_cotangent,
    class_label,
    time_step,
    modulation_weight,
    modulation_bias,
    heads_weight,
    heads_bias,
    mixing_weight,
    mixing_bias,
    up_weight,
    up_bias,
    down_weight,
    down_bias,
    class_table,
    time_table,
):
    model_width = hidden_in.shape[1]
    own_latents = hidden_in.shape[0] // SEQ
    tok_rows = own_latents * SEQ
    heads_here = heads_weight.shape[2] // HEAD_DIM
    score_scale = HEAD_DIM ** (-0.5)
    lat_first = lax.axis_index("dp") * own_latents

    cond_part = jnp.take(class_table, class_label, axis=0).astype(F32) + jnp.take(
        time_table, time_step, axis=0
    ).astype(F32)
    condition = lax.all_gather(cond_part, "tensor", axis=1, tiled=True)
    silu_all = jax.nn.silu(condition).astype(BF16)
    silu_own = lax.dynamic_slice_in_dim(silu_all, lat_first, own_latents)
    mod_part = jnp.dot(silu_own, modulation_weight, preferred_element_type=F32) + modulation_bias.astype(F32)
    modulation = lax.all_gather(mod_part, "tensor", axis=1, tiled=True)
    pieces = [
        modulation[:, number * model_width : (number + 1) * model_width][:, None, :]
        for number in range(6)
    ]
    shift_one, scale_one, gate_one, shift_two, scale_two, gate_two = pieces

    odd_flag = (lax.axis_index("tensor") % 2).reshape(1)
    mixing_pair = chip_pair(mixing_weight.astype(F32), tensor_size, 0)
    mixing_full = call(
        join_rows_kernel,
        jax.ShapeDtypeStruct((model_width, model_width), BF16),
        (odd_flag, mixing_pair, swap(mixing_pair, tensor_size, 1)),
    )

    states = hidden_in.astype(F32).reshape(own_latents, SEQ, model_width)
    normed_one, inverse_one = layer_norm(states)
    heads_in = (normed_one * (1.0 + scale_one) + shift_one).astype(BF16)
    projected = jnp.einsum("bsd,dce->bsce", heads_in, heads_weight, preferred_element_type=F32)
    head_terms = heads_bias.astype(F32)
    shape_heads = (own_latents, SEQ, heads_here, HEAD_DIM)
    queries = (projected[:, :, 0] + head_terms[0]).astype(BF16).reshape(shape_heads)
    key_rows = projected[:, :, 1].astype(BF16).reshape(shape_heads)
    value_rows = (projected[:, :, 2] + head_terms[1]).astype(BF16).reshape(shape_heads)
    scores = jnp.einsum("bqhe,bkhe->bhqk", queries, key_rows, preferred_element_type=F32) * score_scale
    row_max = jnp.max(scores, axis=-1, keepdims=True)
    exp_terms = jnp.exp(scores - row_max)
    row_total = jnp.sum(exp_terms, axis=-1, keepdims=True)
    weights_full = exp_terms / row_total
    weights_low = weights_full.astype(BF16)
    attended = (
        jnp.einsum("bhqk,bkhe->bqhe", weights_low, value_rows, preferred_element_type=F32)
        .astype(BF16)
        .reshape(tok_rows, heads_here * HEAD_DIM)
    )
    attended_pair = chip_pair(attended.astype(F32), tensor_size, 1)
    attn_out = call(
        mixing_kernel,
        jax.ShapeDtypeStruct((tok_rows, model_width), F32),
        (
            odd_flag,
            attended_pair,
            swap(attended_pair, tensor_size, 1),
            mixing_full,
            mixing_bias.reshape(1, model_width),
        ),
    ).reshape(own_latents, SEQ, model_width)
    middle = states + gate_one * attn_out
    normed_two, inverse_two = layer_norm(middle)
    mlp_in = (normed_two * (1.0 + scale_two) + shift_two).astype(BF16).reshape(tok_rows, model_width)
    pre_act = jnp.dot(mlp_in, up_weight, preferred_element_type=F32) + up_bias.astype(F32)
    upstream = out_cotangent.astype(F32).reshape(own_latents, SEQ, model_width)
    d_mlp = (upstream * gate_two).astype(BF16).reshape(tok_rows, model_width)
    d_act = jnp.einsum("td,fd->tf", d_mlp, down_weight, preferred_element_type=F32)
    activated, gelu_pull = jax.vjp(gelu_tanh, pre_act)
    activated = activated.astype(BF16)
    d_pre = gelu_pull(d_act)[0].astype(BF16)
    d_mlp_part = jnp.einsum("tf,df->td", d_pre, up_weight, preferred_element_type=F32)
    d_mlp_in = reduce_rows(d_mlp_part, tensor_size).reshape(own_latents, SEQ, model_width)

    mlp_part = jnp.dot(activated, down_weight, preferred_element_type=F32)
    mlp_out = (reduce_rows(mlp_part, tensor_size) + down_bias.astype(F32)).reshape(
        own_latents, SEQ, model_width
    )
    d_down_weight = jnp.einsum("tf,td->fd", activated, d_mlp, preferred_element_type=F32)
    d_up_weight = jnp.einsum("td,tf->df", mlp_in, d_pre, preferred_element_type=F32)
    d_down_bias = jnp.sum(d_mlp.astype(F32), axis=0)
    d_up_bias = jnp.sum(d_pre.astype(F32), axis=0)
    up_weight_sum, down_weight_sum = lax.psum((d_up_weight, d_down_weight), "dp")

    d_shift_two = jnp.sum(d_mlp_in, axis=1)
    d_scale_two = jnp.sum(d_mlp_in * normed_two, axis=1)
    d_middle = upstream + norm_back(d_mlp_in * (1.0 + scale_two), normed_two, inverse_two)
    d_gate_one = jnp.sum(d_middle * attn_out, axis=1)
    d_attn = (d_middle * gate_one).astype(BF16).reshape(tok_rows, model_width)
    d_mixing_weight = jnp.einsum("te,td->ed", attended, d_attn, preferred_element_type=F32)
    d_mixing_bias = jnp.sum(d_attn.astype(F32), axis=0)
    d_attended = (
        jnp.einsum("td,ed->te", d_attn, mixing_weight, preferred_element_type=F32)
        .astype(BF16)
        .reshape(shape_heads)
    )
    d_weights = jnp.einsum("bqhe,bkhe->bhqk", d_attended, value_rows, preferred_element_type=F32)
    row_dots = jnp.sum(weights_full * d_weights, axis=-1, keepdims=True)
    d_scores = (weights_full * (d_weights - row_dots)).astype(BF16)
    flat_heads = (own_latents, SEQ, heads_here * HEAD_DIM)
    d_queries = (
        (jnp.einsum("bhqk,bkhe->bqhe", d_scores, key_rows, preferred_element_type=F32) * score_scale)
        .astype(BF16)
        .reshape(flat_heads)
    )
    d_keys = (
        (jnp.einsum("bhqk,bqhe->bkhe", d_scores, queries, preferred_element_type=F32) * score_scale)
        .astype(BF16)
        .reshape(flat_heads)
    )
    d_values = (
        jnp.einsum("bhqk,bqhe->bkhe", weights_low, d_attended, preferred_element_type=F32)
        .astype(BF16)
        .reshape(flat_heads)
    )
    d_stack = jnp.stack([d_queries, d_keys, d_values], axis=2)
    d_heads_weight = jnp.einsum("bsd,bsce->dce", heads_in, d_stack, preferred_element_type=F32)
    d_heads_bias = jnp.stack(
        [jnp.sum(d_queries.astype(F32), axis=(0, 1)), jnp.sum(d_values.astype(F32), axis=(0, 1))]
    )
    d_heads_part = jnp.einsum("bsce,dce->bsd", d_stack, heads_weight, preferred_element_type=F32)
    d_heads_in = reduce_rows(d_heads_part.reshape(tok_rows, model_width), tensor_size).reshape(
        own_latents, SEQ, model_width
    )
    heads_weight_sum, mixing_weight_sum = lax.psum((d_heads_weight, d_mixing_weight), "dp")
    heads_bias_sum, mixing_bias_sum, up_bias_sum, down_bias_sum = lax.psum(
        (d_heads_bias, d_mixing_bias, d_up_bias, d_down_bias), "dp"
    )
    block_out = (middle + gate_two * mlp_out).reshape(tok_rows, model_width).astype(BF16)
    d_gate_two = jnp.sum(upstream * mlp_out, axis=1)

    d_shift_one = jnp.sum(d_heads_in, axis=1)
    d_scale_one = jnp.sum(d_heads_in * normed_one, axis=1)
    input_grad = (
        d_middle + norm_back(d_heads_in * (1.0 + scale_one), normed_one, inverse_one)
    ).reshape(tok_rows, model_width)
    d_modulation = jnp.concatenate(
        [d_shift_one, d_scale_one, d_gate_one, d_shift_two, d_scale_two, d_gate_two], axis=1
    )
    own_cols = modulation_weight.shape[1]
    own_mods = lax.dynamic_slice_in_dim(d_modulation, lax.axis_index("tensor") * own_cols, own_cols, 1)
    all_mods = lax.all_gather(own_mods, "dp", axis=0, tiled=True)
    mod_weight_sum, mod_bias_row, d_silu_part = call(
        modulation_grad_kernel,
        (
            jax.ShapeDtypeStruct((model_width, own_cols), F32),
            jax.ShapeDtypeStruct((1, own_cols), F32),
            jax.ShapeDtypeStruct((all_mods.shape[0], model_width), F32),
        ),
        (all_mods, silu_all, modulation_weight),
        scalars=0,
    )
    mod_bias_sum = mod_bias_row.reshape(own_cols)
    d_silu_own = lax.psum_scatter(d_silu_part, "tensor", scatter_dimension=1, tiled=True)
    sigmoid_part = jax.nn.sigmoid(cond_part)
    d_condition = d_silu_own * sigmoid_part * (1.0 + cond_part * (1.0 - sigmoid_part))
    class_sum = jax.ops.segment_sum(d_condition, class_label, num_segments=class_table.shape[0])
    time_sum = jax.ops.segment_sum(d_condition, time_step, num_segments=time_table.shape[0])
    return (
        block_out,
        input_grad,
        mod_weight_sum,
        mod_bias_sum,
        heads_weight_sum,
        heads_bias_sum,
        mixing_weight_sum,
        mixing_bias_sum,
        up_weight_sum,
        up_bias_sum,
        down_weight_sum,
        down_bias_sum,
        class_sum,
        time_sum,
    )


def solution(mesh):
    in_specs = (
        P("dp", None),
        P("dp", None),
        P(),
        P(),
        P(None, "tensor"),
        P("tensor"),
        P(None, None, "tensor"),
        P(None, "tensor"),
        P("tensor", None),
        P(),
        P(None, "tensor"),
        P("tensor"),
        P("tensor", None),
        P(),
        P(None, "tensor"),
        P(None, "tensor"),
    )
    out_specs = (
        P("dp", None),
        P("dp", None),
        P(None, "tensor"),
        P("tensor"),
        P(None, None, "tensor"),
        P(None, "tensor"),
        P("tensor", None),
        P(),
        P(None, "tensor"),
        P("tensor"),
        P("tensor", None),
        P(),
        P(None, "tensor"),
        P(None, "tensor"),
    )

    def run(*args):
        return on_device(mesh.shape["tensor"], mesh.shape["dp"], *args)

    return jax.shard_map(run, mesh=mesh, in_specs=in_specs, out_specs=out_specs, check_vma=False)
```

time: 602 us -> 463 us (0.77)
  waiting for transfers between devices: 408 us -> 253 us
  matrix products: 39.2 us -> 26.5 us
  starting transfers between devices: 0.39 us -> 10.3 us
  other arithmetic: 29 us -> 35.7 us
  Pallas kernels: 0 us -> 6.2 us
    psum x4 -> x1, waiting for transfers between devices: 408 us -> 189 us  [on_device(): lax.psum((d_heads_weight, d_mixing_weight), 'dp')]
    ppermute x0 -> x13, waiting for transfers between devices: none -> 64 us  [swap(): lax.ppermute(values, 'tensor', [(at, at ^ bit) for at in range(size)])]
    ppermute x0 -> x13, starting transfers between devices: none -> 10.3 us  [swap(): lax.ppermute(values, 'tensor', [(at, at ^ bit) for at in range(size)])]
    dot_general x15 -> x12, matrix products: 31.3 us -> 21.4 us  [the longest x1 3.39 us: on_device(): jnp.dot(mlp_in, up_weight, preferred_element_type=F32) + up_bias.astype(F32)]
    reduce_sum x2, other arithmetic: 8.46 us -> 0.36 us  [norm_back(): mean_grad = jnp.mean(upstream, axis=-1, keepdims=True)]
    select_n x0 -> x6, other arithmetic: none -> 6.25 us  [the longest x3 3.31 us: reduce_rows(): jnp.where(flip, other, full)]
    pallas_call x0 -> x3, Pallas kernels: none -> 6.2 us  [call(): pl.pallas_call(kernel, out_shape=out_shape, in_specs=[IN_SMEM] * scalars...]
    unnamed x194 -> x229, local copies, waits for them, and re-layouts: 25 us -> 25.1 us
  transfers between devices with their start and end apart: 5 -> 15, of which waited for: 4 -> 6; matrix products, arithmetic and copies ran while one was open for 7% -> 11% of each run, Pallas kernels for 0% -> 0%
where the time goes in v1:
time: 463 us; the launch traced here: 462 us
  waiting for transfers between devices  253 us (55%)
  blocking collectives  81.1 us (18%)
  other arithmetic  35.7 us (8%)
  local copies, waits for them, and re-layouts  31.6 us (7%)
  matrix products  26.5 us (6%)
  between operations  16.8 us (4%)
  starting transfers between devices  10.3 us (2%)
  Pallas kernels  6.2 us (1%)
    psum x1, waiting for transfers between devices, on_device(): lax.psum((d_heads_weight, d_mixing_weight), 'dp')  189 us
    ppermute x13, waiting for transfers between devices, swap(): lax.ppermute(values, 'tensor', [(at, at ^ bit) for at in range(size)])  64 us
    psum x1, blocking collectives, on_device(): lax.psum((d_heads_bias, d_mixing_bias, d_up_bias, d_down_bias), 'dp')  39.5 us
    all_gather x1, blocking collectives, on_device(): all_mods = lax.all_gather(own_mods, 'dp', axis=0, tiled=True)  31.1 us
    unnamed x229, local copies, waits for them, and re-layouts  25.1 us
    ppermute x13, starting transfers between devices, swap(): lax.ppermute(values, 'tensor', [(at, at ^ bit) for at in range(size)])  10.3 us
  transfers between devices with their start and end apart: 15, of which 6 were waited for; matrix products, arithmetic and copies ran while one was open for 11% of the time, Pallas kernels for 0%

profile of v1, /device:TPU:0, one launch (start us, length us, event | category | flops | bytes accessed | tf_op | source)
XLA Modules:
  0.0 461.5 jit_solution(5944145948109910248)
XLA Ops:
  8.1 1.9 convert_element_type.134
  10.0 2.9 collective-permute-start.2
  20.1 1.7 gather_fusion.1
  22.5 5.3 %all-gather = f32[4,192,16]{1,2,0:T(8,128)S(1)} all-gather(f32[1,192,16]{1,2,0:T(8,128)S(1)} %fusion.40), channel_id=1, replica_groups=mesh['dp'=8,'tensor'=4] {'tensor'}, dimensions={0}, use_global_device_ids=true | all-gather | bytes 61440 | tf_op jit(solution)/shard_map/all_gather | solution.py:134
  28.3 5.3 %all_gather.10 = f32[2,4608]{1,0:T(2,128)S(1)} all-gather(f32[2,1152]{1,0:T(2,128)S(1)} %convolution_add_fusion), channel_id=1, replica_groups=mesh['dp'=8,'tensor'=4] {'tensor'}, dimensions={1}, use_global_device_ids=true | all-gather | bytes 46080 | tf_op jit(solution)/shard_map/all_gather | solution.py:138
  39.9 1.7 collective-permute-start
  43.0 11.2 %collective-permute-done = f32[512,192]{1,0:T(8,128)} collective-permute-done((f32[512,192]{1,0:T(8,128)S(1)}, f32[512,192]{1,0:T(8,128)}, u32[]{:S(2)}, u32[]{:S(2)}) %collective-permute-start) | collective-permute-done | bytes 393248 | tf_op jit(solution)/shard_map/ppermute | solution.py:32
  57.6 2.1 convert_reduce_fusion
  62.1 2.2 shard_map.264
  65.7 3.4 convert_reduce_fusion.1
  71.8 2.8 fusion.51
  76.1 1.7 collective-permute-start.8
  78.8 17.7 %collective-permute-done.8 = f32[256,768]{1,0:T(8,128)S(1)} collective-permute-done((f32[256,768]{1,0:T(8,128)S(1)}, f32[256,768]{1,0:T(8,128)S(1)}, u32[]{:S(2)}, u32[]{:S(2)}) %collective-permute-start.8) | collective-permute-done | bytes 786464 | tf_op jit(solution)/shard_map/ppermute | solution.py:32
  96.8 15.8 %collective-permute-done.5 = f32[256,768]{1,0:T(8,128)} collective-permute-done((f32[256,768]{1,0:T(8,128)S(1)}, f32[256,768]{1,0:T(8,128)}, u32[]{:S(2)}, u32[]{:S(2)}) %collective-permute-start.5) | collective-permute-done | bytes 786464 | tf_op jit(solution)/shard_map/ppermute | solution.py:32
  118.3 3.3 convert_reduce_fusion.2
  123.0 2.6 convert_reduce_fusion.4
  129.9 2.1 collective-permute-done.10
  132.9 1.7 collective-permute-start.11
  135.7 17.2 %collective-permute-done.11 = f32[256,768]{1,0:T(8,128)} collective-permute-done((f32[256,768]{1,0:T(8,128)}, f32[256,768]{1,0:T(8,128)}, u32[]{:S(2)}, u32[]{:S(2)}) %collective-permute-start.11) | collective-permute-done | bytes 786464 | tf_op jit(solution)/shard_map/ppermute | solution.py:32
  152.9 2.3 add.258
  155.2 2.2 fusion.64
  157.5 2.4 fusion.50
  160.5 3.0 convolution_bitcast_fusion
  163.5 1.6 broadcast_select_fusion.1
  165.8 2.3 fusion.17
  168.3 31.1 %all-gather.1 = f32[8,2,1152]{2,1,0:T(2,128)S(1)} all-gather(f32[1,2,1152]{2,1,0:T(2,128)S(1)} %dynamic-slice_bitcast_fusion), channel_id=1, replica_groups=mesh['dp'=8,'tensor'=4] {'dp'}, dimensions={0}, use_global_device_ids=true | all-gather | bytes 82944 | tf_op jit(solution)/shard_map/all_gather | solution.py:265
  200.9 2.6 shard_map.265
  204.5 2.3 fusion.63
  207.7 39.5 %all-reduce = (f32[2,192]{1,0:T(2,128)}, f32[768]{0:T(1024)}, f32[768]{0:T(1024)}, f32[768]{0:T(1024)}) all-reduce(f32[2,192]{1,0:T(2,128)S(1)} %pad_maximum_fusion.8, f32[768]{0:T(1024)S(1)} %copy-done.71, f32[768]{0:T(1024)S(1)} %copy-done.92, f32[768]{0:T(1024)S(1)} %copy-done.70), channel_id=1, replica_groups=mesh['dp'=8,'tensor'=4] {'dp'}, use_global_device_ids=true, to_apply=%region_20.21 | all-reduce | flops 2688 | bytes 21504 | tf_op jit(solution)/shard_map/psum | solution.py:249
  248.5 3.1 multiply_add_fusion
  257.3 189.1 %all-reduce.4.cloned.1.call-done = (f32[768,3,192]{0,2,1:T(8,128)}, f32[192,768]{1,0:T(8,128)}, f32[768,768]{1,0:T(8,128)}, f32[768,768]{1,0:T(8,128)}) async-done(((f32[768,3,192]{0,2,1:T(8,128)}, f32[192,768]{1,0:T(8,128)}, f32[768,768]{1,0:T(8,128)}, f32[768,768]{1,0:T(8,128)}), (f32[768,3,192]{0,2,1:T(8,128)}, f32[192,768]{1,0:T(8,128)}, f32[768,768]{1,0:T(8,128)}, ...) | async-done | bytes 7077904 | tf_op jit(solution)/shard_map/psum | solution.py:248
  446.4 2.9 copy.107
  (329 shorter events, 57.7 us)
Async XLA Ops:
  8.0 57.7 %copy-start = (bf16[768,768]{1,0:T(8,128)(2,1)S(1)}, bf16[768,768]{1,0:T(8,128)(2,1)}, u32[]{:S(2)}) copy-start(bf16[768,768]{1,0:T(8,128)(2,1)} %param.26) | copy-start | bytes 3538948
  8.1 243.6 %reduce-scatter.4.cloned.1.call-start = ((), (), s32[]{:S(2)}) async-start(), calls=%async_computation.1 | async-start | bytes 491520
  10.0 31.7 %collective-permute-start.2 = (f32[192,768]{1,0:T(8,128)}, f32[192,768]{1,0:T(8,128)}, u32[]{:S(2)}, u32[]{:S(2)}) collective-permute-start(f32[192,768]{1,0:T(8,128)} %convert_element_type.134), channel_id=1, source_target_pairs={{0,2},{1,3},{2,0},{3,1},{4,6},{5,7},{6,4},{7,5},{8,10},{9,11},{10,... | collective-permute-start | bytes 1769480 | tf_op jit(solution)/shard_map/ppermute | solution.py:32
  15.7 18.6 %copy-start.83 = (f32[2,256]{1,0:T(2,128)}, f32[2,256]{1,0:T(2,128)S(1)}, u32[]{:S(2)}) copy-start(f32[2,256]{1,0:T(2,128)S(1)} %div.51) | copy-start | bytes 6148
  15.7 12.3 %copy-start.2 = (bf16[768,1152]{1,0:T(8,128)(2,1)S(1)}, bf16[768,1152]{1,0:T(8,128)(2,1)}, u32[]{:S(2)}) copy-start(bf16[768,1152]{1,0:T(8,128)(2,1)} %weight_ref.1) | copy-start | bytes 5308420
  17.4 16.9 %copy-start.85 = (f32[2,256]{1,0:T(2,128)}, f32[2,256]{1,0:T(2,128)S(1)}, u32[]{:S(2)}) copy-start(f32[2,256]{1,0:T(2,128)S(1)} %rsqrt.25) | copy-start | bytes 6148
  21.8 13.4 %copy-start.50 = (bf16[16,192]{1,0:T(8,128)(2,1)}, bf16[16,192]{1,0:T(8,128)(2,1)S(1)}, u32[]{:S(2)}) copy-start(bf16[16,192]{1,0:T(8,128)(2,1)S(1)} %gather_fusion.1) | copy-start | bytes 18436
  22.4 12.8 %copy-start.52 = (bf16[16,192]{1,0:T(8,128)(2,1)}, bf16[16,192]{1,0:T(8,128)(2,1)S(1)}, u32[]{:S(2)}) copy-start(bf16[16,192]{1,0:T(8,128)(2,1)S(1)} %gather_fusion) | copy-start | bytes 18436
  39.9 14.3 %collective-permute-start = (f32[512,192]{1,0:T(8,128)S(1)}, f32[512,192]{1,0:T(8,128)}, u32[]{:S(2)}, u32[]{:S(2)}) collective-permute-start(f32[512,192]{1,0:T(8,128)S(1)} %convert_element_type.133), channel_id=1, source_target_pairs={{0,2},{1,3},{2,0},{3,1},{4,6},{5,7},{6,4},{7,5},{8,10},{9,11},{10,... | collective-permute-start | bytes 1179656 | tf_op jit(solution)/shard_map/ppermute | solution.py:32
  42.9 17.7 %collective-permute-start.3 = (f32[384,768]{1,0:T(8,128)S(1)}, f32[384,768]{1,0:T(8,128)}, u32[]{:S(2)}, u32[]{:S(2)}) collective-permute-start(f32[384,768]{1,0:T(8,128)S(1)} %pad_maximum_fusion.3.own_ref), channel_id=1, source_target_pairs={{0,1},{1,0},{2,3},{3,2},{4,5},{5,4},{6,7},{7,6},{8,9},{9,8},{10,11... | collective-permute-start | bytes 3538952 | tf_op jit(solution)/shard_map/ppermute | solution.py:32
  55.6 6.5 %collective-permute-start.1 = (f32[512,384]{1,0:T(8,128)S(1)}, f32[512,384]{1,0:T(8,128)}, u32[]{:S(2)}, u32[]{:S(2)}) collective-permute-start(f32[512,384]{1,0:T(8,128)S(1)} %pad_maximum_fusion.4.own_ref), channel_id=1, source_target_pairs={{0,1},{1,0},{2,3},{3,2},{4,5},{5,4},{6,7},{7,6},{8,9},{9,8},{10,11... | collective-permute-start | bytes 2359304 | tf_op jit(solution)/shard_map/ppermute | solution.py:32
  71.2 3.5 collective-permute-start.7
  74.7 3.1 collective-permute-start.4
  76.1 20.5 %collective-permute-start.8 = (f32[256,768]{1,0:T(8,128)S(1)}, f32[256,768]{1,0:T(8,128)S(1)}, u32[]{:S(2)}, u32[]{:S(2)}) collective-permute-start(f32[256,768]{1,0:T(8,128)S(1)} %dynamic-slice_add_fusion.1), channel_id=1, source_target_pairs={{0,2},{1,3},{2,0},{3,1},{4,6},{5,7},{6,4},{7,5},{8,10},{9,11},{10,... | collective-permute-start | bytes 2359304 | tf_op jit(solution)/shard_map/ppermute | solution.py:32
  77.9 18.8 %copy-start.94 = (bf16[768]{0:T(1024)(128)(2,1)S(1)}, bf16[768]{0:T(1024)(128)(2,1)}, u32[]{:S(2)}) copy-start(bf16[768]{0:T(1024)(128)(2,1)} %param.29) | copy-start | bytes 4612
  77.9 34.7 %collective-permute-start.5 = (f32[256,768]{1,0:T(8,128)S(1)}, f32[256,768]{1,0:T(8,128)}, u32[]{:S(2)}, u32[]{:S(2)}) collective-permute-start(f32[256,768]{1,0:T(8,128)S(1)} %dynamic-slice_add_fusion.2), channel_id=1, source_target_pairs={{0,2},{1,3},{2,0},{3,1},{4,6},{5,7},{6,4},{7,5},{8,10},{9,11},{10,... | collective-permute-start | bytes 2359304 | tf_op jit(solution)/shard_map/ppermute | solution.py:32
  96.6 17.3 %copy-start.26 = (f32[256,768]{1,0:T(8,128)}, f32[256,768]{1,0:T(8,128)S(1)}, u32[]{:S(2)}) copy-start(f32[256,768]{1,0:T(8,128)S(1)} %add.255) | copy-start | bytes 2359300
  96.7 17.3 %collective-permute-start.9 = (f32[256,768]{1,0:T(8,128)S(1)}, f32[256,768]{1,0:T(8,128)}, u32[]{:S(2)}, u32[]{:S(2)}) collective-permute-start(f32[256,768]{1,0:T(8,128)S(1)} %add.255), channel_id=1, source_target_pairs={{0,1},{1,0},{2,3},{3,2},{4,5},{5,4},{6,7},{7,6},{8,9},{9,8},{10,11... | collective-permute-start | bytes 2359304 | tf_op jit(solution)/shard_map/ppermute | solution.py:32
  96.8 20.4 %copy-start.63 = (f32[768]{0:T(1024)}, f32[768]{0:T(1024)S(1)}, u32[]{:S(2)}) copy-start(f32[768]{0:T(1024)S(1)} %convert_element_type.138) | copy-start | bytes 9220
  113.8 3.2 collective-permute-start.6
  129.6 2.4 collective-permute-start.10
  132.9 22.3 %copy-start.25 = (bf16[512,768]{1,0:T(8,128)(2,1)S(1)}, bf16[512,768]{1,0:T(8,128)(2,1)}, u32[]{:S(2)}) copy-start(bf16[512,768]{1,0:T(8,128)(2,1)} %copy-done.24) | copy-start | bytes 2359300
  132.9 20.0 %collective-permute-start.11 = (f32[256,768]{1,0:T(8,128)}, f32[256,768]{1,0:T(8,128)}, u32[]{:S(2)}, u32[]{:S(2)}) collective-permute-start(f32[256,768]{1,0:T(8,128)} %dynamic-slice_add_fusion), channel_id=1, source_target_pairs={{0,2},{1,3},{2,0},{3,1},{4,6},{5,7},{6,4},{7,5},{8,10},{9,11},{10,... | collective-permute-start | bytes 2359304 | tf_op jit(solution)/shard_map/ppermute | solution.py:32
  135.7 19.5 %copy-start.44 = (bf16[512,768]{1,0:T(8,128)(2,1)S(1)}, bf16[512,768]{1,0:T(8,128)(2,1)}, u32[]{:S(2)}) copy-start(bf16[512,768]{1,0:T(8,128)(2,1)} %copy-done.43) | copy-start | bytes 2359300
  155.2 8.3 %collective-permute-start.12 = (f32[256,768]{1,0:T(8,128)}, f32[256,768]{1,0:T(8,128)}, u32[]{:S(2)}, u32[]{:S(2)}) collective-permute-start(f32[256,768]{1,0:T(8,128)} %add.258), channel_id=1, source_target_pairs={{0,1},{1,0},{2,3},{3,2},{4,5},{5,4},{6,7},{7,6},{8,9},{9,8},{10,11... | collective-permute-start | bytes 2359304 | tf_op jit(solution)/shard_map/ppermute | solution.py:32
  165.8 33.6 %copy-start.5 = (bf16[16,768]{1,0:T(8,128)(2,1)S(1)}, bf16[16,768]{1,0:T(8,128)(2,1)}, u32[]{:S(2)}) copy-start(bf16[16,768]{1,0:T(8,128)(2,1)} %copy-done.4) | copy-start | bytes 73732
  168.2 36.3 %copy-start.32 = (bf16[24,8,2,256]{3,1,2,0:T(8,128)(2,1)S(1)}, bf16[24,8,2,256]{3,1,2,0:T(8,128)(2,1)}, u32[]{:S(2)}) copy-start(bf16[24,8,2,256]{3,1,2,0:T(8,128)(2,1)} %copy-done.31) | copy-start | bytes 589828
  204.4 242.0 %all-reduce.4.cloned.1.call-start = ((), (), s32[]{:S(2)}) async-start(), calls=%async_computation.2 | async-start | bytes 14155776 | tf_op jit(solution)/shard_map/psum | solution.py:248
  206.8 40.3 %copy-start.14 = (f32[256,768]{1,0:T(8,128)S(1)}, f32[256,768]{1,0:T(8,128)}, u32[]{:S(2)}) copy-start(f32[256,768]{1,0:T(8,128)} %copy-done.13) | copy-start | bytes 2359300
  206.8 40.3 %copy-start.16 = (f32[256,768]{1,0:T(8,128)S(1)}, f32[256,768]{1,0:T(8,128)}, u32[]{:S(2)}) copy-start(f32[256,768]{1,0:T(8,128)} %copy-done.15) | copy-start | bytes 2359300
  206.8 40.3 %copy-start.55 = (f32[2,768]{1,0:T(2,128)S(1)}, f32[2,768]{1,0:T(2,128)}, u32[]{:S(2)}) copy-start(f32[2,768]{1,0:T(2,128)} %copy-done.54) | copy-start | bytes 18436
  206.8 40.3 %copy-start.66 = (f32[512]{0:T(512)S(1)}, f32[512]{0:T(512)}, u32[]{:S(2)}) copy-start(f32[512]{0:T(512)} %copy-done.65) | copy-start | bytes 6148
  (87 other events, 258.0 us)
Sparse Core Ops, SparseCore 0:
  204.6 21.6 reduce-scatter.3
Sparse Core Ops, SparseCore 1:
  210.5 235.8 all-reduce.3

commit v2 on v1

--- a/solution.py
+++ b/solution.py
@@ -1,3 +1,5 @@
+import functools
+
 import jax
 import jax.numpy as jnp
 from jax import lax
@@ -40,7 +42,40 @@
     )
 
 
-VMEM_LIMIT = 48 * 1024 * 1024
+def ring_place(size):
+    order = list(range(0, size, 2)) + list(range(size - 1, 0, -2))
+    index = lax.axis_index("dp")
+    place = jnp.where(index % 2 == 0, index // 2, size - 1 - index // 2)
+    return order, place
+
+
+def gather_latents(own, size):
+    if size % 2 or size > 16:
+        return lax.all_gather(own, "dp", axis=0, tiled=True)
+    rows = own.shape[0]
+    index = lax.axis_index("dp")
+    other = lax.ppermute(own, "dp", [(at, at ^ 1) for at in range(size)])
+    odd = index % 2 == 1
+    pair = jnp.concatenate([jnp.where(odd, other, own), jnp.where(odd, own, other)], axis=0)
+    out = jnp.zeros((size * rows, own.shape[1]), own.dtype)
+    out = lax.dynamic_update_slice_in_dim(out, pair, (index // 2) * 2 * rows, 0)
+    for step in range(2, size, 2):
+        got = lax.ppermute(pair, "dp", [(at, (at + step) % size) for at in range(size)])
+        out = lax.dynamic_update_slice_in_dim(out, got, (((index - step) % size) // 2) * 2 * rows, 0)
+    return out
+
+
+def scatter_features(part, size):
+    index = lax.axis_index("tensor")
+    columns = part.shape[1] // size
+    block = lambda at: lax.dynamic_slice_in_dim(part, at * columns, columns, 1)
+    total = block(index)
+    for bit in range(1, size):
+        total = total + swap(block(index ^ bit), size, bit)
+    return total
+
+
+VMEM_LIMIT = 20 * 1024 * 1024
 IN_VMEM = pl.BlockSpec(memory_space=pltpu.VMEM)
 IN_SMEM = pl.BlockSpec(memory_space=pltpu.SMEM)
 
@@ -50,9 +85,129 @@
         kernel,
         out_shape=out_shape,
         in_specs=[IN_SMEM] * scalars + [IN_VMEM] * (len(operands) - scalars),
-        out_specs=jax.tree.map(lambda leaf: IN_VMEM, out_shape),
+        out_specs=[IN_VMEM] * len(out_shape) if isinstance(out_shape, tuple) else IN_VMEM,
         compiler_params=pltpu.CompilerParams(vmem_limit_bytes=VMEM_LIMIT),
     )(*operands)
+
+
+def natural(blocks):
+    index = lax.axis_index("tensor")
+    low, high = index % 2 == 1, index >= 2
+    return [
+        jnp.where(
+            high,
+            jnp.where(low, blocks[at ^ 3], blocks[at ^ 2]),
+            jnp.where(low, blocks[at ^ 1], blocks[at]),
+        )
+        for at in range(4)
+    ]
+
+
+def join_columns(own, size):
+    blocks = [own] + [swap(own, size, bit) for bit in range(1, size)]
+    return jnp.concatenate(natural(blocks), axis=1)
+
+
+def place_kernel(count, spots_ref, *refs):
+    pieces, out_ref, sems = refs[:count], refs[count], refs[count + 1]
+    rows = pieces[0].shape[0]
+    copies = []
+    for at in range(count):
+        start = pl.multiple_of(spots_ref[at] * rows, 8)
+        copies.append(
+            pltpu.make_async_copy(pieces[at], out_ref.at[pl.ds(start, rows), :], sems.at[at])
+        )
+    for copy in copies:
+        copy.start()
+    for copy in copies:
+        copy.wait()
+
+
+def place_rows(pieces, spots):
+    count = len(pieces)
+    rows, columns = pieces[0].shape
+    return pl.pallas_call(
+        functools.partial(place_kernel, count),
+        out_shape=jax.ShapeDtypeStruct((count * rows, columns), F32),
+        in_specs=[IN_SMEM] + [IN_VMEM] * count,
+        out_specs=pl.BlockSpec(memory_space=pl.ANY),
+        scratch_shapes=[pltpu.SemaphoreType.DMA((count,))],
+        compiler_params=pltpu.CompilerParams(vmem_limit_bytes=VMEM_LIMIT),
+    )(jnp.stack(spots).astype(jnp.int32), *(in_vmem(piece) for piece in pieces))
+
+
+def in_vmem(values):
+    return pltpu.with_memory_space_constraint(values, pltpu.VMEM)
+
+
+def add_kernel(spots_ref, *refs):
+    count = len(refs) // 3
+    for at in range(count):
+        moved_ref, part_ref, out_ref = refs[at], refs[count + at], refs[2 * count + at]
+        rows = moved_ref.shape[0]
+        start = pl.multiple_of(spots_ref[at] * rows, 8)
+        out_ref[...] = moved_ref[...] + part_ref[pl.ds(start, rows), :]
+
+
+def add_pieces(moving, parts, spots):
+    return call(
+        add_kernel,
+        tuple(pltpu.VMEM(held.shape, F32) for held in moving),
+        (jnp.stack(spots).astype(jnp.int32), *(in_vmem(held) for held in moving), *(in_vmem(part) for part in parts)),
+    )
+
+
+def ring_spots(ways, size):
+    order, place = ring_place(size)
+    return lambda steps: [(place - way * steps) % size for way in ways]
+
+
+class Ring:
+    def __init__(self, parts, firsts, ways, size):
+        order, place = ring_place(size)
+        self.perms = [[(order[at], order[(at + way) % size]) for at in range(size)] for way in ways]
+        self.spots = ring_spots(ways, size)
+        self.parts, self.size, self.count = parts, size, 0
+        self.moving = list(firsts)
+        self.pieces = []
+
+    def step(self, gate=None):
+        if self.count == 2 * self.size - 2:
+            return self.moving[0]
+        self.count += 1
+        self.moving = [lax.ppermute(held, "dp", perm) for held, perm in zip(self.moving, self.perms)]
+        if gate is not None:
+            self.moving = after(self.moving, gate)
+        if self.count < self.size:
+            self.moving = add_pieces(self.moving, self.parts, self.spots(self.count))
+        if self.count >= self.size - 1:
+            self.pieces.append(self.moving)
+        return self.moving[0]
+
+    def finish(self):
+        while self.count < 2 * self.size - 2:
+            self.step()
+        last = [self.spots(self.size - 1 + step) for step in range(self.size)]
+        return [
+            place_rows(kept, [spots[at] for spots in last])
+            for at, kept in enumerate(zip(*self.pieces))
+        ]
+
+
+class Plain:
+    def __init__(self, parts):
+        self.parts = parts
+
+    def step(self, gate=None):
+        return self.parts[0]
+
+    def finish(self):
+        return lax.psum(self.parts, "dp")
+
+
+def start_sum(parts, firsts, ways, size):
+    whole = all(part.shape[0] % (8 * size) == 0 for part in parts)
+    return Ring(parts, firsts, ways, size) if whole and size <= 16 else Plain(parts)
 
 
 def join_rows_kernel(odd_ref, own_ref, beside_ref, out_ref):
@@ -78,6 +233,61 @@
     )
 
 
+def column_sums(values):
+    return jnp.sum(values.astype(F32), axis=0, keepdims=True)
+
+
+def over_tokens(left, right):
+    return lax.dot_general(left, right, (((0,), (0,)), ((), ())), preferred_element_type=F32)
+
+
+def copy_block(spots_ref, at, part_ref, first_ref):
+    rows = first_ref.shape[0]
+    first_ref[...] = part_ref[pl.ds(pl.multiple_of(spots_ref[at] * rows, 8), rows), :]
+
+
+def mlp_grads_kernel(
+    spots_ref, mlp_in_ref, d_pre_ref, activated_ref, d_mlp_ref, up_ref, down_ref, bias_ref, up_first_ref, down_first_ref
+):
+    up_ref[...] = over_tokens(mlp_in_ref[...], d_pre_ref[...])
+    down_ref[...] = over_tokens(activated_ref[...], d_mlp_ref[...])
+    bias_ref[0:1, :] = column_sums(d_pre_ref[...])
+    bias_ref[1:2, :] = column_sums(d_mlp_ref[...])
+    copy_block(spots_ref, 0, up_ref, up_first_ref)
+    copy_block(spots_ref, 1, down_ref, down_first_ref)
+
+
+def attention_grads_kernel(
+    spots_ref,
+    heads_in_ref,
+    d_queries_ref,
+    d_keys_ref,
+    d_values_ref,
+    attended_ref,
+    d_attn_ref,
+    bias_ref,
+    upper_ref,
+    lower_ref,
+    upper_first_ref,
+    lower_first_ref,
+):
+    feats = d_queries_ref.shape[1]
+    width = heads_in_ref.shape[1]
+    heads_in = heads_in_ref[...]
+    upper_ref[0:feats, :] = over_tokens(d_queries_ref[...], heads_in)
+    upper_ref[feats : 2 * feats, :] = over_tokens(d_keys_ref[...], heads_in)
+    lower_ref[0:feats, :] = over_tokens(d_values_ref[...], heads_in)
+    lower_ref[feats : 2 * feats, :] = over_tokens(attended_ref[...], d_attn_ref[...])
+    base = 2 * feats
+    lower_ref[base:, :] = jnp.zeros((lower_ref.shape[0] - base, width), F32)
+    lower_ref[base : base + 2, :] = bias_ref[...]
+    lower_ref[base + 2 : base + 3, :] = column_sums(d_attn_ref[...])
+    lower_ref[base + 3 : base + 4, 0:feats] = column_sums(d_queries_ref[...])
+    lower_ref[base + 4 : base + 5, 0:feats] = column_sums(d_values_ref[...])
+    copy_block(spots_ref, 0, upper_ref, upper_first_ref)
+    copy_block(spots_ref, 1, lower_ref, lower_first_ref)
+
+
 def modulation_grad_kernel(mods_ref, silu_ref, weight_ref, weight_grad_ref, bias_grad_ref, silu_grad_ref):
     mods = mods_ref[...].astype(BF16)
     weight_grad_ref[...] = lax.dot_general(
@@ -89,15 +299,22 @@
     )
 
 
-def reduce_rows(part, size):
+def after(values, gate):
+    flat, tree = jax.tree.flatten(values)
+    return jax.tree.unflatten(tree, lax.optimization_barrier((*flat, gate))[:-1])
+
+
+def chip_rows(part, size):
     odd = lax.axis_index("tensor") % 2
     half = part.shape[0] // 2
     mine = lax.dynamic_slice_in_dim(part, odd * half, half)
     theirs = lax.dynamic_slice_in_dim(part, (1 - odd) * half, half)
-    chip_sum = mine + swap(theirs, size, 1)
-    full = chip_sum + swap(chip_sum, size, 2)
+    return mine + swap(theirs, size, 1)
+
+
+def whole_rows(full, size):
     other = swap(full, size, 1)
-    flip = odd == 1
+    flip = lax.axis_index("tensor") % 2 == 1
     return jnp.concatenate([jnp.where(flip, other, full), jnp.where(flip, full, other)], axis=0)
 
 
@@ -128,14 +345,16 @@
     score_scale = HEAD_DIM ** (-0.5)
     lat_first = lax.axis_index("dp") * own_latents
 
-    cond_part = jnp.take(class_table, class_label, axis=0).astype(F32) + jnp.take(
-        time_table, time_step, axis=0
-    ).astype(F32)
-    condition = lax.all_gather(cond_part, "tensor", axis=1, tiled=True)
+    class_pick = jax.nn.one_hot(class_label, class_table.shape[0], dtype=BF16)
+    time_pick = jax.nn.one_hot(time_step, time_table.shape[0], dtype=BF16)
+    cond_part = jnp.dot(class_pick, class_table, preferred_element_type=F32) + jnp.dot(
+        time_pick, time_table, preferred_element_type=F32
+    )
+    condition = join_columns(cond_part, tensor_size)
     silu_all = jax.nn.silu(condition).astype(BF16)
     silu_own = lax.dynamic_slice_in_dim(silu_all, lat_first, own_latents)
     mod_part = jnp.dot(silu_own, modulation_weight, preferred_element_type=F32) + modulation_bias.astype(F32)
-    modulation = lax.all_gather(mod_part, "tensor", axis=1, tiled=True)
+    modulation = join_columns(mod_part, tensor_size)
     pieces = [
         modulation[:, number * model_width : (number + 1) * model_width][:, None, :]
         for number in range(6)
@@ -143,7 +362,7 @@
     shift_one, scale_one, gate_one, shift_two, scale_two, gate_two = pieces
 
     odd_flag = (lax.axis_index("tensor") % 2).reshape(1)
-    mixing_pair = chip_pair(mixing_weight.astype(F32), tensor_size, 0)
+    mixing_pair = chip_pair(after(mixing_weight, cond_part).astype(F32), tensor_size, 0)
     mixing_full = call(
         join_rows_kernel,
         jax.ShapeDtypeStruct((model_width, model_width), BF16),
@@ -170,7 +389,11 @@
         .astype(BF16)
         .reshape(tok_rows, heads_here * HEAD_DIM)
     )
+    upstream = out_cotangent.astype(F32).reshape(own_latents, SEQ, model_width)
+    d_mlp = (upstream * gate_two).astype(BF16).reshape(tok_rows, model_width)
+    d_act = jnp.einsum("td,fd->tf", d_mlp, down_weight, preferred_element_type=F32)
     attended_pair = chip_pair(attended.astype(F32), tensor_size, 1)
+    attended_pair, mixing_full, d_act = lax.optimization_barrier((attended_pair, mixing_full, d_act))
     attn_out = call(
         mixing_kernel,
         jax.ShapeDtypeStruct((tok_rows, model_width), F32),
@@ -186,40 +409,52 @@
     normed_two, inverse_two = layer_norm(middle)
     mlp_in = (normed_two * (1.0 + scale_two) + shift_two).astype(BF16).reshape(tok_rows, model_width)
     pre_act = jnp.dot(mlp_in, up_weight, preferred_element_type=F32) + up_bias.astype(F32)
-    upstream = out_cotangent.astype(F32).reshape(own_latents, SEQ, model_width)
-    d_mlp = (upstream * gate_two).astype(BF16).reshape(tok_rows, model_width)
-    d_act = jnp.einsum("td,fd->tf", d_mlp, down_weight, preferred_element_type=F32)
     activated, gelu_pull = jax.vjp(gelu_tanh, pre_act)
     activated = activated.astype(BF16)
     d_pre = gelu_pull(d_act)[0].astype(BF16)
     d_mlp_part = jnp.einsum("tf,df->td", d_pre, up_weight, preferred_element_type=F32)
-    d_mlp_in = reduce_rows(d_mlp_part, tensor_size).reshape(own_latents, SEQ, model_width)
+    chip_two = chip_rows(d_mlp_part, tensor_size)
 
     mlp_part = jnp.dot(activated, down_weight, preferred_element_type=F32)
-    mlp_out = (reduce_rows(mlp_part, tensor_size) + down_bias.astype(F32)).reshape(
+    activated, d_pre = after((activated, d_pre), chip_two)
+    ways = (1, -1)
+    first_spots = jnp.stack(ring_spots(ways, dp_size)(0)).astype(jnp.int32)
+    up_part, down_part, mlp_bias, up_first, down_first = call(
+        mlp_grads_kernel,
+        (
+            pltpu.VMEM((model_width, d_pre.shape[1]), F32),
+            pltpu.VMEM((activated.shape[1], model_width), F32),
+            pltpu.VMEM((2, model_width), F32),
+            pltpu.VMEM((model_width // dp_size, d_pre.shape[1]), F32),
+            pltpu.VMEM((activated.shape[1] // dp_size, model_width), F32),
+        ),
+        (first_spots, mlp_in, d_pre, activated, d_mlp),
+    )
+    mlp_ring = start_sum((up_part, down_part), (up_first, down_first), ways, dp_size)
+    across_two = after(swap(chip_two, tensor_size, 2), mlp_ring.step())
+    full_two = chip_two + across_two
+    d_mlp_in = whole_rows(full_two, tensor_size).reshape(own_latents, SEQ, model_width)
+    d_mlp_in = after(d_mlp_in, mlp_ring.step(full_two))
+    chip_out = after(chip_rows(mlp_part, tensor_size), full_two)
+    full_out = chip_out + swap(chip_out, tensor_size, 2)
+    mlp_out = (whole_rows(full_out, tensor_size) + down_bias.astype(F32)).reshape(
         own_latents, SEQ, model_width
     )
-    d_down_weight = jnp.einsum("tf,td->fd", activated, d_mlp, preferred_element_type=F32)
-    d_up_weight = jnp.einsum("td,tf->df", mlp_in, d_pre, preferred_element_type=F32)
-    d_down_bias = jnp.sum(d_mlp.astype(F32), axis=0)
-    d_up_bias = jnp.sum(d_pre.astype(F32), axis=0)
-    up_weight_sum, down_weight_sum = lax.psum((d_up_weight, d_down_weight), "dp")
-
     d_shift_two = jnp.sum(d_mlp_in, axis=1)
     d_scale_two = jnp.sum(d_mlp_in * normed_two, axis=1)
     d_middle = upstream + norm_back(d_mlp_in * (1.0 + scale_two), normed_two, inverse_two)
     d_gate_one = jnp.sum(d_middle * attn_out, axis=1)
     d_attn = (d_middle * gate_one).astype(BF16).reshape(tok_rows, model_width)
-    d_mixing_weight = jnp.einsum("te,td->ed", attended, d_attn, preferred_element_type=F32)
-    d_mixing_bias = jnp.sum(d_attn.astype(F32), axis=0)
     d_attended = (
         jnp.einsum("td,ed->te", d_attn, mixing_weight, preferred_element_type=F32)
         .astype(BF16)
         .reshape(shape_heads)
     )
+    d_attended = after(d_attended, mlp_ring.step(d_attended))
     d_weights = jnp.einsum("bqhe,bkhe->bhqk", d_attended, value_rows, preferred_element_type=F32)
     row_dots = jnp.sum(weights_full * d_weights, axis=-1, keepdims=True)
     d_scores = (weights_full * (d_weights - row_dots)).astype(BF16)
+    d_scores = after(d_scores, mlp_ring.step(d_scores))
     flat_heads = (own_latents, SEQ, heads_here * HEAD_DIM)
     d_queries = (
         (jnp.einsum("bhqk,bkhe->bqhe", d_scores, key_rows, preferred_element_type=F32) * score_scale)
@@ -237,18 +472,40 @@
         .reshape(flat_heads)
     )
     d_stack = jnp.stack([d_queries, d_keys, d_values], axis=2)
-    d_heads_weight = jnp.einsum("bsd,bsce->dce", heads_in, d_stack, preferred_element_type=F32)
-    d_heads_bias = jnp.stack(
-        [jnp.sum(d_queries.astype(F32), axis=(0, 1)), jnp.sum(d_values.astype(F32), axis=(0, 1))]
-    )
     d_heads_part = jnp.einsum("bsce,dce->bsd", d_stack, heads_weight, preferred_element_type=F32)
-    d_heads_in = reduce_rows(d_heads_part.reshape(tok_rows, model_width), tensor_size).reshape(
-        own_latents, SEQ, model_width
-    )
-    heads_weight_sum, mixing_weight_sum = lax.psum((d_heads_weight, d_mixing_weight), "dp")
-    heads_bias_sum, mixing_bias_sum, up_bias_sum, down_bias_sum = lax.psum(
-        (d_heads_bias, d_mixing_bias, d_up_bias, d_down_bias), "dp"
-    )
+    chip_one = after(
+        chip_rows(d_heads_part.reshape(tok_rows, model_width), tensor_size), full_out
+    )
+    own_feats = heads_here * HEAD_DIM
+    d_queries, d_keys, d_values = after((d_queries, d_keys, d_values), chip_one)
+    upper_rows, lower_rows = 2 * own_feats, 2 * own_feats + 8 * dp_size
+    upper_part, lower_part, upper_first, lower_first = call(
+        attention_grads_kernel,
+        (
+            pltpu.VMEM((upper_rows, model_width), F32),
+            pltpu.VMEM((lower_rows, model_width), F32),
+            pltpu.VMEM((upper_rows // dp_size, model_width), F32),
+            pltpu.VMEM((lower_rows // dp_size, model_width), F32),
+        ),
+        (
+            first_spots,
+            heads_in.reshape(tok_rows, model_width),
+            d_queries.reshape(tok_rows, own_feats),
+            d_keys.reshape(tok_rows, own_feats),
+            d_values.reshape(tok_rows, own_feats),
+            attended,
+            d_attn,
+            mlp_bias,
+        ),
+    )
+    heads_ring = start_sum((upper_part, lower_part), (upper_first, lower_first), ways, dp_size)
+    gate = mlp_ring.step(upper_first)
+    gate = heads_ring.step(gate)
+    gate = mlp_ring.step(gate)
+    across_one = after(swap(chip_one, tensor_size, 2), gate)
+    full_one = chip_one + across_one
+    d_heads_in = whole_rows(full_one, tensor_size).reshape(own_latents, SEQ, model_width)
+    d_heads_in = after(d_heads_in, heads_ring.step(full_one))
     block_out = (middle + gate_two * mlp_out).reshape(tok_rows, model_width).astype(BF16)
     d_gate_two = jnp.sum(upstream * mlp_out, axis=1)
 
@@ -262,7 +519,19 @@
     )
     own_cols = modulation_weight.shape[1]
     own_mods = lax.dynamic_slice_in_dim(d_modulation, lax.axis_index("tensor") * own_cols, own_cols, 1)
-    all_mods = lax.all_gather(own_mods, "dp", axis=0, tiled=True)
+    mlp_ring.step(own_mods)
+    heads_ring.step(own_mods)
+    up_weight_sum, down_weight_sum = mlp_ring.finish()
+    upper, lower = heads_ring.finish()
+    heads_weight_sum = (
+        jnp.concatenate([upper, lower[:own_feats]], axis=0)
+        .reshape(3, own_feats, model_width)
+        .transpose(2, 0, 1)
+    )
+    mixing_weight_sum = lower[own_feats : 2 * own_feats]
+    up_bias_sum, down_bias_sum, mixing_bias_sum = (lower[2 * own_feats + row] for row in range(3))
+    heads_bias_sum = lower[2 * own_feats + 3 : 2 * own_feats + 5, :own_feats]
+    all_mods = gather_latents(own_mods, dp_size)
     mod_weight_sum, mod_bias_row, d_silu_part = call(
         modulation_grad_kernel,
         (
@@ -274,11 +543,12 @@
         scalars=0,
     )
     mod_bias_sum = mod_bias_row.reshape(own_cols)
-    d_silu_own = lax.psum_scatter(d_silu_part, "tensor", scatter_dimension=1, tiled=True)
+    d_silu_own = scatter_features(d_silu_part, tensor_size)
     sigmoid_part = jax.nn.sigmoid(cond_part)
     d_condition = d_silu_own * sigmoid_part * (1.0 + cond_part * (1.0 - sigmoid_part))
-    class_sum = jax.ops.segment_sum(d_condition, class_label, num_segments=class_table.shape[0])
-    time_sum = jax.ops.segment_sum(d_condition, time_step, num_segments=time_table.shape[0])
+    exact = dict(preferred_element_type=F32, precision=lax.Precision.HIGHEST)
+    class_sum = jnp.einsum("lk,lf->kf", class_pick.astype(F32), d_condition, **exact)
+    time_sum = jnp.einsum("lk,lf->kf", time_pick.astype(F32), d_condition, **exact)
     return (
         block_out,
         input_grad,

time: 463 us -> 312 us (0.67)
  waiting for transfers between devices: 253 us -> 82.7 us
  blocking collectives: 81.1 us -> 0 us
  starting transfers between devices: 10.3 us -> 78.6 us
  Pallas kernels: 6.2 us -> 33.9 us
  between operations: 16.8 us -> 2.52 us
  local copies, waits for them, and re-layouts: 31.6 us -> 43.7 us
  other arithmetic: 35.7 us -> 45.2 us
    psum x1 -> x0, waiting for transfers between devices: 189 us -> none  [on_device(): lax.psum((d_heads_weight, d_mixing_weight), 'dp')]
    ppermute x0 -> x60, starting transfers between devices: none -> 64.8 us  [the longest x56 57.7 us: step(): lax.ppermute(held, 'dp', perm)]
    ppermute x0 -> x60, waiting for transfers between devices: none -> 60.8 us  [the longest x56 60.8 us: step(): lax.ppermute(held, 'dp', perm)]
    ppermute x13 -> x22, waiting for transfers between devices: 64 us -> 21.9 us  [swap(): lax.ppermute(values, 'tensor', [(at, at ^ bit) for at in range(size)])]
    all_gather x3 -> x0, blocking collectives: 41.7 us -> none  [the longest x1 31.1 us: on_device(): all_mods = lax.all_gather(own_mods, 'dp', axis=0, tiled=True)]
    psum x1 -> x0, blocking collectives: 39.5 us -> none  [on_device(): lax.psum((d_heads_bias, d_mixing_bias, d_up_bias, d_down_bias), 'dp')]
    pallas_call x3 -> x19, Pallas kernels: 6.2 us -> 24.3 us  [call(): pl.pallas_call(kernel, out_shape=out_shape, in_specs=[IN_SMEM] * scalars...]
    pallas_call x0 -> x4, Pallas kernels: none -> 9.68 us  [place_rows(): pl.pallas_call(functools.partial(place_kernel, count), out_shape=jax.Shap...]
  transfers between devices with their start and end apart: 15 -> 82, of which waited for: 6 -> 27; matrix products, arithmetic and copies ran while one was open for 11% -> 22% of each run, Pallas kernels for 0% -> 8%
where the time goes in v2:
time: 312 us; the launch traced here: 310 us
  waiting for transfers between devices  82.7 us (27%)
  starting transfers between devices  78.6 us (25%)
  other arithmetic  45.2 us (14%)
  local copies, waits for them, and re-layouts  43.7 us (14%)
  Pallas kernels  33.9 us (11%)
  matrix products  22.9 us (7%)
    ppermute x56, waiting for transfers between devices, step(): lax.ppermute(held, 'dp', perm)  60.8 us
    ppermute x56, starting transfers between devices, step(): lax.ppermute(held, 'dp', perm)  57.7 us
    unnamed x318, local copies, waits for them, and re-layouts  29.1 us
    pallas_call x19, Pallas kernels, call(): pl.pallas_call(kernel, out_shape=out_shape, in_specs=[IN_SMEM] * scalars...  24.3 us
    ppermute x22, waiting for transfers between devices, swap(): lax.ppermute(values, 'tensor', [(at, at ^ bit) for at in range(size)])  21.9 us
    ppermute x22, starting transfers between devices, swap(): lax.ppermute(values, 'tensor', [(at, at ^ bit) for at in range(size)])  13.7 us
    pallas_call x4, Pallas kernels, place_rows(): pl.pallas_call(functools.partial(place_kernel, count), out_shape=jax.Shap...  9.68 us
  transfers between devices with their start and end apart: 82, of which 27 were waited for; matrix products, arithmetic and copies ran while one was open for 22% of the time, Pallas kernels for 8%

profile of v2, /device:TPU:0, one launch (start us, length us, event | category | flops | bytes accessed | tf_op | source)
XLA Modules:
  0.0 309.6 jit_solution(9977468287444058325)
XLA Ops:
  3.4 2.4 collective-permute-start
  20.0 4.0 %collective-permute-done.4 = f32[2,1152]{1,0:T(2,128)S(1)} collective-permute-done((f32[2,1152]{1,0:T(2,128)}, f32[2,1152]{1,0:T(2,128)S(1)}, u32[]{:S(2)}, u32[]{:S(2)}) %collective-permute-start.4) | collective-permute-done | bytes 9248 | tf_op jit(solution)/shard_map/ppermute | solution.py:34
  26.6 2.2 fusion.25
  38.9 9.7 %collective-permute-done.6 = f32[512,192]{1,0:T(8,128)S(1)} collective-permute-done((f32[512,192]{1,0:T(8,128)S(1)}, f32[512,192]{1,0:T(8,128)S(1)}, u32[]{:S(2)}, u32[]{:S(2)}) %collective-permute-start.6) | collective-permute-done | bytes 393248 | tf_op jit(solution)/shard_map/ppermute | solution.py:34
  53.7 2.1 shard_map.264
  72.8 2.3 shard_map.265
  77.3 2.1 dynamic-slice_add_fusion.2
  79.4 4.8 %collective-permute-done.13.refs_0_ = f32[96,768]{1,0:T(8,128)S(1)} collective-permute-done((f32[96,768]{1,0:T(8,128)S(1)}, f32[96,768]{1,0:T(8,128)S(1)}, u32[]{:S(2)}, u32[]{:S(2)}) %collective-permute-start.13) | collective-permute-done | bytes 294944 | tf_op jit(solution)/shard_map/ppermute | solution.py:178
  88.0 2.3 add.428
  95.2 2.0 subtract_multiply_fusion
  97.2 5.3 %collective-permute-done.18.refs_0_ = f32[96,768]{1,0:T(8,128)S(1)} collective-permute-done((f32[96,768]{1,0:T(8,128)S(1)}, f32[96,768]{1,0:T(8,128)S(1)}, u32[]{:S(2)}, u32[]{:S(2)}) %collective-permute-start.18) | collective-permute-done | bytes 294944 | tf_op jit(solution)/shard_map/ppermute | solution.py:178
  107.3 2.3 collective-permute-done.15
  131.8 5.6 %collective-permute-done.22.refs_0_ = f32[96,768]{1,0:T(8,128)S(1)} collective-permute-done((f32[96,768]{1,0:T(8,128)S(1)}, f32[96,768]{1,0:T(8,128)S(1)}, u32[]{:S(2)}, u32[]{:S(2)}) %collective-permute-start.22) | collective-permute-done | bytes 294944 | tf_op jit(solution)/shard_map/ppermute | solution.py:178
  137.4 2.4 collective-permute-done.23.refs_1_
  143.4 2.3 collective-permute-done.24
  167.8 7.3 %collective-permute-done.30.refs_0_ = f32[48,768]{1,0:T(8,128)S(1)} collective-permute-done((f32[48,768]{1,0:T(8,128)S(1)}, f32[48,768]{1,0:T(8,128)S(1)}, u32[]{:S(2)}, u32[]{:S(2)}) %collective-permute-start.30) | collective-permute-done | bytes 147488 | tf_op jit(solution)/shard_map/ppermute | solution.py:178
  180.3 2.4 add.448
  186.8 3.4 %collective-permute-done.33.refs_0_ = f32[48,768]{1,0:T(8,128)} collective-permute-done((f32[48,768]{1,0:T(8,128)}, f32[48,768]{1,0:T(8,128)}, u32[]{:S(2)}, u32[]{:S(2)}) %collective-permute-start.33) | collective-permute-done | bytes 147488 | tf_op jit(solution)/shard_map/ppermute | solution.py:178
  218.0 3.0 fusion.12
  227.7 4.5 %collective-permute-done.45.refs_0_ = f32[48,768]{1,0:T(8,128)S(1)} collective-permute-done((f32[48,768]{1,0:T(8,128)S(1)}, f32[48,768]{1,0:T(8,128)S(1)}, u32[]{:S(2)}, u32[]{:S(2)}) %collective-permute-start.45) | collective-permute-done | bytes 147488 | tf_op jit(solution)/shard_map/ppermute | solution.py:178
  232.2 2.5 collective-permute-start.38
  244.1 2.6 shard_map.275
  258.7 4.7 %collective-permute-done.51.refs_3_ = f32[48,768]{1,0:T(8,128)} collective-permute-done((f32[48,768]{1,0:T(8,128)S(1)}, f32[48,768]{1,0:T(8,128)}, u32[]{:S(2)}, u32[]{:S(2)}) %collective-permute-start.51) | collective-permute-done | bytes 147488 | tf_op jit(solution)/shard_map/ppermute | solution.py:178
  271.1 5.0 %collective-permute-done.59.refs_4_ = f32[56,768]{1,0:T(8,128)} collective-permute-done((f32[56,768]{1,0:T(8,128)}, f32[56,768]{1,0:T(8,128)}, u32[]{:S(2)}, u32[]{:S(2)}) %collective-permute-start.59) | collective-permute-done | bytes 172064 | tf_op jit(solution)/shard_map/ppermute | solution.py:178
  281.1 2.5 collective-permute-done.60.refs_5_
  284.3 2.1 fusion.44
  287.8 3.2 %collective-permute-done.61.refs_6_ = f32[56,768]{1,0:T(8,128)S(1)} collective-permute-done((f32[56,768]{1,0:T(8,128)S(1)}, f32[56,768]{1,0:T(8,128)S(1)}, u32[]{:S(2)}, u32[]{:S(2)}) %collective-permute-start.61) | collective-permute-done | bytes 172064 | tf_op jit(solution)/shard_map/ppermute | solution.py:178
  292.0 2.1 fusion.43
  294.0 2.7 shard_map.281
  298.9 3.0 shard_map.282
  305.4 2.0 shard_map.284
  307.4 2.0 shard_map.285
  (581 shorter events, 200.2 us)
Async XLA Ops:
  8.4 20.6 %collective-permute-start.7 = (f32[192,768]{1,0:T(8,128)}, f32[192,768]{1,0:T(8,128)S(1)}, u32[]{:S(2)}, u32[]{:S(2)}) collective-permute-start(f32[192,768]{1,0:T(8,128)} %convert_element_type.117), channel_id=1, source_target_pairs={{0,2},{1,3},{2,0},{3,1},{4,6},{5,7},{6,4},{7,5},{8,10},{9,11},{10,... | collective-permute-start | bytes 1769480 | tf_op jit(solution)/shard_map/ppermute | solution.py:34
  30.1 19.7 %collective-permute-start.8 = (f32[384,768]{1,0:T(8,128)S(1)}, f32[384,768]{1,0:T(8,128)}, u32[]{:S(2)}, u32[]{:S(2)}) collective-permute-start(f32[384,768]{1,0:T(8,128)S(1)} %pad_maximum_fusion.4.own_ref), channel_id=1, source_target_pairs={{0,1},{1,0},{2,3},{3,2},{4,5},{5,4},{6,7},{7,6},{8,9},{9,8},{10,11... | collective-permute-start | bytes 3538952 | tf_op jit(solution)/shard_map/ppermute | solution.py:34
  34.2 14.4 %collective-permute-start.6 = (f32[512,192]{1,0:T(8,128)S(1)}, f32[512,192]{1,0:T(8,128)S(1)}, u32[]{:S(2)}, u32[]{:S(2)}) collective-permute-start(f32[512,192]{1,0:T(8,128)S(1)} %convert_element_type.116), channel_id=1, source_target_pairs={{0,2},{1,3},{2,0},{3,1},{4,6},{5,7},{6,4},{7,5},{8,10},{9,11},{10,... | collective-permute-start | bytes 1179656 | tf_op jit(solution)/shard_map/ppermute | solution.py:34
  67.9 20.1 %collective-permute-start.12 = (f32[256,768]{1,0:T(8,128)}, f32[256,768]{1,0:T(8,128)}, u32[]{:S(2)}, u32[]{:S(2)}) collective-permute-start(f32[256,768]{1,0:T(8,128)} %dynamic-slice_add_fusion.1), channel_id=1, source_target_pairs={{0,2},{1,3},{2,0},{3,1},{4,6},{5,7},{6,4},{7,5},{8,10},{9,11},{10,... | collective-permute-start | bytes 2359304 | tf_op jit(solution)/shard_map/ppermute | solution.py:34
  90.3 19.3 %collective-permute-start.15 = (f32[256,768]{1,0:T(8,128)}, f32[256,768]{1,0:T(8,128)}, u32[]{:S(2)}, u32[]{:S(2)}) collective-permute-start(f32[256,768]{1,0:T(8,128)} %dynamic-slice_add_fusion.2), channel_id=1, source_target_pairs={{0,2},{1,3},{2,0},{3,1},{4,6},{5,7},{6,4},{7,5},{8,10},{9,11},{10,... | collective-permute-start | bytes 2359304 | tf_op jit(solution)/shard_map/ppermute | solution.py:34
  91.7 19.5 %collective-permute-start.17 = (f32[256,768]{1,0:T(8,128)}, f32[256,768]{1,0:T(8,128)}, u32[]{:S(2)}, u32[]{:S(2)}) collective-permute-start(f32[256,768]{1,0:T(8,128)} %add.428), channel_id=1, source_target_pairs={{0,1},{1,0},{2,3},{3,2},{4,5},{5,4},{6,7},{7,6},{8,9},{9,8},{10,11... | collective-permute-start | bytes 2359304 | tf_op jit(solution)/shard_map/ppermute | solution.py:34
  105.3 17.5 %collective-permute-start.20 = (f32[96,768]{1,0:T(8,128)}, f32[96,768]{1,0:T(8,128)S(1)}, u32[]{:S(2)}, u32[]{:S(2)}) collective-permute-start(f32[96,768]{1,0:T(8,128)} %get-tuple-element.105), channel_id=1, source_target_pairs={{0,8},{8,16},{16,24},{24,28},{28,20},{20,12},{12,4},{4,0},{1,9},{9... | collective-permute-start | bytes 884744 | tf_op jit(solution)/shard_map/ppermute | solution.py:178
  106.9 16.7 %collective-permute-start.21 = (f32[96,768]{1,0:T(8,128)}, f32[96,768]{1,0:T(8,128)}, u32[]{:S(2)}, u32[]{:S(2)}) collective-permute-start(f32[96,768]{1,0:T(8,128)} %get-tuple-element.107), channel_id=1, source_target_pairs={{0,4},{8,0},{16,8},{24,16},{28,24},{20,28},{12,20},{4,12},{1,5},{9... | collective-permute-start | bytes 884744 | tf_op jit(solution)/shard_map/ppermute | solution.py:178
  146.7 33.6 %collective-permute-start.25 = (f32[256,768]{1,0:T(8,128)}, f32[256,768]{1,0:T(8,128)}, u32[]{:S(2)}, u32[]{:S(2)}) collective-permute-start(f32[256,768]{1,0:T(8,128)} %dynamic-slice_add_fusion), channel_id=1, source_target_pairs={{0,2},{1,3},{2,0},{3,1},{4,6},{5,7},{6,4},{7,5},{8,10},{9,11},{10,... | collective-permute-start | bytes 2359304 | tf_op jit(solution)/shard_map/ppermute | solution.py:34
  148.1 13.6 %collective-permute-start.26 = (f32[96,768]{1,0:T(8,128)}, f32[96,768]{1,0:T(8,128)}, u32[]{:S(2)}, u32[]{:S(2)}) collective-permute-start(f32[96,768]{1,0:T(8,128)} %get-tuple-element.115), channel_id=1, source_target_pairs={{0,8},{8,16},{16,24},{24,28},{28,20},{20,12},{12,4},{4,0},{1,9},{9... | collective-permute-start | bytes 884744 | tf_op jit(solution)/shard_map/ppermute | solution.py:178
  149.6 12.1 %collective-permute-start.27 = (f32[96,768]{1,0:T(8,128)}, f32[96,768]{1,0:T(8,128)}, u32[]{:S(2)}, u32[]{:S(2)}) collective-permute-start(f32[96,768]{1,0:T(8,128)} %get-tuple-element.118), channel_id=1, source_target_pairs={{0,4},{8,0},{16,8},{24,16},{28,24},{20,28},{12,20},{4,12},{1,5},{9... | collective-permute-start | bytes 884744 | tf_op jit(solution)/shard_map/ppermute | solution.py:178
  163.7 14.5 %collective-permute-start.28 = (f32[96,768]{1,0:T(8,128)S(1)}, f32[96,768]{1,0:T(8,128)S(1)}, u32[]{:S(2)}, u32[]{:S(2)}) collective-permute-start(f32[96,768]{1,0:T(8,128)S(1)} %get-tuple-element.126), channel_id=1, source_target_pairs={{0,8},{8,16},{16,24},{24,28},{28,20},{20,12},{12,4},{4,0},{1,9},{9... | collective-permute-start | bytes 884744 | tf_op jit(solution)/shard_map/ppermute | solution.py:178
  165.3 12.9 %collective-permute-start.29 = (f32[96,768]{1,0:T(8,128)S(1)}, f32[96,768]{1,0:T(8,128)S(1)}, u32[]{:S(2)}, u32[]{:S(2)}) collective-permute-start(f32[96,768]{1,0:T(8,128)S(1)} %get-tuple-element.127), channel_id=1, source_target_pairs={{0,4},{8,0},{16,8},{24,16},{28,24},{20,28},{12,20},{4,12},{1,5},{9... | collective-permute-start | bytes 884744 | tf_op jit(solution)/shard_map/ppermute | solution.py:178
  165.8 11.2 %collective-permute-start.31 = (f32[56,768]{1,0:T(8,128)S(1)}, f32[56,768]{1,0:T(8,128)S(1)}, u32[]{:S(2)}, u32[]{:S(2)}) collective-permute-start(f32[56,768]{1,0:T(8,128)S(1)} %get-tuple-element.128), channel_id=1, source_target_pairs={{0,4},{8,0},{16,8},{24,16},{28,24},{20,28},{12,20},{4,12},{1,5},{9... | collective-permute-start | bytes 516104 | tf_op jit(solution)/shard_map/ppermute | solution.py:178
  182.7 12.6 %collective-permute-start.32 = (f32[256,768]{1,0:T(8,128)}, f32[256,768]{1,0:T(8,128)}, u32[]{:S(2)}, u32[]{:S(2)}) collective-permute-start(f32[256,768]{1,0:T(8,128)} %add.448), channel_id=1, source_target_pairs={{0,1},{1,0},{2,3},{3,2},{4,5},{5,4},{6,7},{7,6},{8,9},{9,8},{10,11... | collective-permute-start | bytes 2359304 | tf_op jit(solution)/shard_map/ppermute | solution.py:34
  184.8 21.4 %collective-permute-start.63 = (f32[96,768]{1,0:T(8,128)}, f32[96,768]{1,0:T(8,128)}, u32[]{:S(2)}, u32[]{:S(2)}) collective-permute-start(f32[96,768]{1,0:T(8,128)} %copy-done.73), channel_id=1, source_target_pairs={{0,8},{8,16},{16,24},{24,28},{28,20},{20,12},{12,4},{4,0},{1,9},{9... | collective-permute-start | bytes 884744 | tf_op jit(solution)/shard_map/ppermute | solution.py:178
  186.3 19.8 %collective-permute-start.64 = (f32[96,768]{1,0:T(8,128)}, f32[96,768]{1,0:T(8,128)}, u32[]{:S(2)}, u32[]{:S(2)}) collective-permute-start(f32[96,768]{1,0:T(8,128)} %copy-done.72), channel_id=1, source_target_pairs={{0,4},{8,0},{16,8},{24,16},{28,24},{20,28},{12,20},{4,12},{1,5},{9... | collective-permute-start | bytes 884744 | tf_op jit(solution)/shard_map/ppermute | solution.py:178
  207.6 13.4 %collective-permute-start.65 = (f32[96,768]{1,0:T(8,128)S(1)}, f32[96,768]{1,0:T(8,128)S(1)}, u32[]{:S(2)}, u32[]{:S(2)}) collective-permute-start(f32[96,768]{1,0:T(8,128)S(1)} %get-tuple-element.161.refs_0_), channel_id=1, source_target_pairs={{0,8},{8,16},{16,24},{24,28},{28,20},{20,12},{12,4},{4,0},{1,9},{9... | collective-permute-start | bytes 884744 | tf_op jit(solution)/shard_map/ppermute | solution.py:178
  209.1 13.8 %collective-permute-start.72 = (f32[96,768]{1,0:T(8,128)S(1)}, f32[96,768]{1,0:T(8,128)S(1)}, u32[]{:S(2)}, u32[]{:S(2)}) collective-permute-start(f32[96,768]{1,0:T(8,128)S(1)} %get-tuple-element.162.refs_0_), channel_id=1, source_target_pairs={{0,4},{8,0},{16,8},{24,16},{28,24},{20,28},{12,20},{4,12},{1,5},{9... | collective-permute-start | bytes 884744 | tf_op jit(solution)/shard_map/ppermute | solution.py:178
  221.0 14.4 %collective-permute-start.37 = (f32[4,1152]{1,0:T(4,128)}, f32[4,1152]{1,0:T(4,128)S(1)}, u32[]{:S(2)}, u32[]{:S(2)}) collective-permute-start(f32[4,1152]{1,0:T(4,128)} %get-tuple-element.210), channel_id=1, source_target_pairs={{0,16},{4,20},{8,24},{12,28},{16,0},{20,4},{24,8},{28,12},{1,17},{... | collective-permute-start | bytes 55304 | tf_op jit(solution)/shard_map/ppermute | solution.py:63
  222.9 14.5 %collective-permute-start.66 = (f32[96,768]{1,0:T(8,128)S(1)}, f32[96,768]{1,0:T(8,128)S(1)}, u32[]{:S(2)}, u32[]{:S(2)}) collective-permute-start(f32[96,768]{1,0:T(8,128)S(1)} %collective-permute-done.65.refs_1_), channel_id=1, source_target_pairs={{0,8},{8,16},{16,24},{24,28},{28,20},{20,12},{12,4},{4,0},{1,9},{9... | collective-permute-start | bytes 884744 | tf_op jit(solution)/shard_map/ppermute | solution.py:178
  223.8 13.8 %collective-permute-start.73 = (f32[96,768]{1,0:T(8,128)S(1)}, f32[96,768]{1,0:T(8,128)S(1)}, u32[]{:S(2)}, u32[]{:S(2)}) collective-permute-start(f32[96,768]{1,0:T(8,128)S(1)} %collective-permute-done.72.refs_1_), channel_id=1, source_target_pairs={{0,4},{8,0},{16,8},{24,16},{28,24},{20,28},{12,20},{4,12},{1,5},{9... | collective-permute-start | bytes 884744 | tf_op jit(solution)/shard_map/ppermute | solution.py:178
  232.2 11.9 %collective-permute-start.38 = (f32[4,1152]{1,0:T(4,128)}, f32[4,1152]{1,0:T(4,128)S(1)}, u32[]{:S(2)}, u32[]{:S(2)}) collective-permute-start(f32[4,1152]{1,0:T(4,128)} %get-tuple-element.210), channel_id=1, source_target_pairs={{0,24},{4,28},{8,0},{12,4},{16,8},{20,12},{24,16},{28,20},{1,25},{... | collective-permute-start | bytes 55304 | tf_op jit(solution)/shard_map/ppermute | solution.py:63
  237.4 14.6 %collective-permute-start.67 = (f32[96,768]{1,0:T(8,128)S(1)}, f32[96,768]{1,0:T(8,128)S(1)}, u32[]{:S(2)}, u32[]{:S(2)}) collective-permute-start(f32[96,768]{1,0:T(8,128)S(1)} %collective-permute-done.66.refs_2_), channel_id=1, source_target_pairs={{0,8},{8,16},{16,24},{24,28},{28,20},{20,12},{12,4},{4,0},{1,9},{9... | collective-permute-start | bytes 884744 | tf_op jit(solution)/shard_map/ppermute | solution.py:178
  237.6 15.1 %collective-permute-start.74 = (f32[96,768]{1,0:T(8,128)S(1)}, f32[96,768]{1,0:T(8,128)S(1)}, u32[]{:S(2)}, u32[]{:S(2)}) collective-permute-start(f32[96,768]{1,0:T(8,128)S(1)} %collective-permute-done.73.refs_2_), channel_id=1, source_target_pairs={{0,4},{8,0},{16,8},{24,16},{28,24},{20,28},{12,20},{4,12},{1,5},{9... | collective-permute-start | bytes 884744 | tf_op jit(solution)/shard_map/ppermute | solution.py:178
  252.0 12.0 %collective-permute-start.68 = (f32[96,768]{1,0:T(8,128)S(1)}, f32[96,768]{1,0:T(8,128)S(1)}, u32[]{:S(2)}, u32[]{:S(2)}) collective-permute-start(f32[96,768]{1,0:T(8,128)S(1)} %collective-permute-done.67.refs_3_), channel_id=1, source_target_pairs={{0,8},{8,16},{16,24},{24,28},{28,20},{20,12},{12,4},{4,0},{1,9},{9... | collective-permute-start | bytes 884744 | tf_op jit(solution)/shard_map/ppermute | solution.py:178
  252.6 12.8 %collective-permute-start.75 = (f32[96,768]{1,0:T(8,128)S(1)}, f32[96,768]{1,0:T(8,128)S(1)}, u32[]{:S(2)}, u32[]{:S(2)}) collective-permute-start(f32[96,768]{1,0:T(8,128)S(1)} %collective-permute-done.74.refs_3_), channel_id=1, source_target_pairs={{0,4},{8,0},{16,8},{24,16},{28,24},{20,28},{12,20},{4,12},{1,5},{9... | collective-permute-start | bytes 884744 | tf_op jit(solution)/shard_map/ppermute | solution.py:178
  258.7 18.2 %collective-permute-start.79 = (f32[16,192]{1,0:T(8,128)S(1)}, f32[16,192]{1,0:T(8,128)}, u32[]{:S(2)}, u32[]{:S(2)}) collective-permute-start(f32[16,192]{1,0:T(8,128)S(1)} %get-tuple-element.203), channel_id=1, source_target_pairs={{0,1},{1,0},{2,3},{3,2},{4,5},{5,4},{6,7},{7,6},{8,9},{9,8},{10,11... | collective-permute-start | bytes 36872 | tf_op jit(solution)/shard_map/ppermute | solution.py:34
  264.0 15.0 %collective-permute-start.69 = (f32[96,768]{1,0:T(8,128)S(1)}, f32[96,768]{1,0:T(8,128)S(1)}, u32[]{:S(2)}, u32[]{:S(2)}) collective-permute-start(f32[96,768]{1,0:T(8,128)S(1)} %collective-permute-done.68.refs_4_), channel_id=1, source_target_pairs={{0,8},{8,16},{16,24},{24,28},{28,20},{20,12},{12,4},{4,0},{1,9},{9... | collective-permute-start | bytes 884744 | tf_op jit(solution)/shard_map/ppermute | solution.py:178
  265.4 14.7 %collective-permute-start.76 = (f32[96,768]{1,0:T(8,128)S(1)}, f32[96,768]{1,0:T(8,128)S(1)}, u32[]{:S(2)}, u32[]{:S(2)}) collective-permute-start(f32[96,768]{1,0:T(8,128)S(1)} %collective-permute-done.75.refs_4_), channel_id=1, source_target_pairs={{0,4},{8,0},{16,8},{24,16},{28,24},{20,28},{12,20},{4,12},{1,5},{9... | collective-permute-start | bytes 884744 | tf_op jit(solution)/shard_map/ppermute | solution.py:178
  279.1 17.7 %collective-permute-start.70 = (f32[96,768]{1,0:T(8,128)S(1)}, f32[96,768]{1,0:T(8,128)S(1)}, u32[]{:S(2)}, u32[]{:S(2)}) collective-permute-start(f32[96,768]{1,0:T(8,128)S(1)} %collective-permute-done.69.refs_5_), channel_id=1, source_target_pairs={{0,8},{8,16},{16,24},{24,28},{28,20},{20,12},{12,4},{4,0},{1,9},{9... | collective-permute-start | bytes 884744 | tf_op jit(solution)/shard_map/ppermute | solution.py:178
  280.1 17.7 %collective-permute-start.77 = (f32[96,768]{1,0:T(8,128)S(1)}, f32[96,768]{1,0:T(8,128)S(1)}, u32[]{:S(2)}, u32[]{:S(2)}) collective-permute-start(f32[96,768]{1,0:T(8,128)S(1)} %collective-permute-done.76.refs_5_), channel_id=1, source_target_pairs={{0,4},{8,0},{16,8},{24,16},{28,24},{20,28},{12,20},{4,12},{1,5},{9... | collective-permute-start | bytes 884744 | tf_op jit(solution)/shard_map/ppermute | solution.py:178
  (206 other events, 1450.4 us)

commit v3 on v2

v3 whole, which is shorter than its diff:
```python
import functools
import math

import jax
import jax.numpy as jnp
from jax import lax
from jax.experimental import pallas as pl
from jax.experimental.pallas import tpu as pltpu
from jax.sharding import PartitionSpec as P

SEQ = 256
HEAD_DIM = 64
F32 = jnp.float32
BF16 = jnp.bfloat16


def swap(values, size, bit):
    return lax.ppermute(values, "tensor", [(at, at ^ bit) for at in range(size)])


def ring_place(size):
    order = list(range(0, size, 2)) + list(range(size - 1, 0, -2))
    index = lax.axis_index("dp")
    place = jnp.where(index % 2 == 0, index // 2, size - 1 - index // 2)
    return order, place


def gather_latents(own, size):
    if size % 2 or size > 16:
        return lax.all_gather(own, "dp", axis=0, tiled=True)
    rows = own.shape[0]
    index = lax.axis_index("dp")
    other = lax.ppermute(own, "dp", [(at, at ^ 1) for at in range(size)])
    odd = index % 2 == 1
    pair = jnp.concatenate([jnp.where(odd, other, own), jnp.where(odd, own, other)], axis=0)
    out = jnp.zeros((size * rows, own.shape[1]), own.dtype)
    out = lax.dynamic_update_slice_in_dim(out, pair, (index // 2) * 2 * rows, 0)
    for step in range(2, size, 2):
        got = lax.ppermute(pair, "dp", [(at, (at + step) % size) for at in range(size)])
        out = lax.dynamic_update_slice_in_dim(out, got, (((index - step) % size) // 2) * 2 * rows, 0)
    return out


def scatter_features(part, size):
    index = lax.axis_index("tensor")
    columns = part.shape[1] // size
    block = lambda at: lax.dynamic_slice_in_dim(part, at * columns, columns, 1)
    total = block(index)
    for bit in range(1, size):
        total = total + swap(block(index ^ bit), size, bit)
    return total


VMEM_LIMIT = 20 * 1024 * 1024
SMALL_LIMIT = 8 * 1024 * 1024
GELU_SCALE = (2.0 / math.pi) ** 0.5
IN_VMEM = pl.BlockSpec(memory_space=pltpu.VMEM)
IN_SMEM = pl.BlockSpec(memory_space=pltpu.SMEM)


QUICK = pl.CostEstimate(flops=1, transcendentals=0, bytes_accessed=1)


def call(kernel, out_shape, operands, scalars=1, scratch=(), limit=VMEM_LIMIT):
    single = not isinstance(out_shape, tuple)
    return pl.pallas_call(
        kernel,
        out_shape=out_shape,
        in_specs=[IN_SMEM] * scalars + [IN_VMEM] * (len(operands) - scalars),
        out_specs=IN_VMEM if single else [IN_VMEM] * len(out_shape),
        scratch_shapes=list(scratch),
        compiler_params=pltpu.CompilerParams(vmem_limit_bytes=limit),
        cost_estimate=QUICK,
    )(*operands)


def natural(blocks):
    index = lax.axis_index("tensor")
    low, high = index % 2 == 1, index >= 2
    return [
        jnp.where(
            high,
            jnp.where(low, blocks[at ^ 3], blocks[at ^ 2]),
            jnp.where(low, blocks[at ^ 1], blocks[at]),
        )
        for at in range(4)
    ]


def join_columns(own, size):
    blocks = [own] + [swap(own, size, bit) for bit in range(1, size)]
    return jnp.concatenate(natural(blocks), axis=1)


def place_kernel(steps, first, targets, outs, spots_ref, *refs):
    count = len(targets)
    pieces, out_refs, sems = refs[: steps * count], refs[steps * count : steps * count + outs], refs[-1]
    copies = []
    filled = [0] * outs
    for entry, runs in enumerate(targets):
        height = pieces[entry].shape[0]
        at = 0
        for share, out in runs:
            rows = height * share[0] // share[1]
            for step in range(steps):
                start = pl.multiple_of(spots_ref[first + step, entry] * rows + filled[out], 8)
                copies.append(
                    pltpu.make_async_copy(
                        pieces[step * count + entry].at[pl.ds(at, rows), :],
                        out_refs[out].at[pl.ds(start, rows), :],
                        sems.at[len(copies)],
                    )
                )
            at += rows
            filled[out] += rows * steps
    for copy in copies:
        copy.start()
    for copy in copies:
        copy.wait()


def place_rows(pieces, table, first, targets, shapes):
    steps = len(pieces)
    copies = steps * sum(len(runs) for runs in targets)
    return pl.pallas_call(
        functools.partial(place_kernel, steps, first, targets, len(shapes)),
        out_shape=[jax.ShapeDtypeStruct(shape, F32) for shape in shapes],
        in_specs=[IN_SMEM] + [IN_VMEM] * (steps * len(targets)),
        out_specs=[pl.BlockSpec(memory_space=pl.ANY)] * len(shapes),
        scratch_shapes=[pltpu.SemaphoreType.DMA((copies,))],
        compiler_params=pltpu.CompilerParams(vmem_limit_bytes=SMALL_LIMIT),
        cost_estimate=QUICK,
    )(table, *(piece for step in pieces for piece in step))


def add_kernel(step, spots_ref, *refs):
    count = len(refs) // 3
    for at in range(count):
        moved_ref, part_ref, out_ref = refs[at], refs[count + at], refs[2 * count + at]
        rows = moved_ref.shape[0]
        start = pl.multiple_of(spots_ref[step, at] * rows, 8)
        out_ref[...] = moved_ref[...] + part_ref[pl.ds(start, rows), :]


def add_pieces(moving, parts, table, step):
    return call(
        functools.partial(add_kernel, step),
        tuple(jax.ShapeDtypeStruct(held.shape, F32) for held in moving),
        (table, *moving, *parts),
        limit=SMALL_LIMIT,
    )


def ring_table(ways, size):
    order, place = ring_place(size)
    steps = jnp.arange(2 * size - 1, dtype=jnp.int32)[:, None]
    return (place - jnp.asarray(ways, jnp.int32)[None, :] * steps) % size


class Ring:
    def __init__(self, parts, firsts, ways, size, table):
        order, place = ring_place(size)
        self.perms = [[(order[at], order[(at + way) % size]) for at in range(size)] for way in ways]
        self.table = table
        self.parts, self.size, self.count = parts, size, 0
        self.moving = list(firsts)
        self.pieces = []

    def step(self, gate=None):
        if self.count == 2 * self.size - 2:
            return self.moving[0]
        self.count += 1
        self.moving = [lax.ppermute(held, "dp", perm) for held, perm in zip(self.moving, self.perms)]
        if gate is not None:
            self.moving = after(self.moving, gate)
        if self.count < self.size:
            self.moving = add_pieces(self.moving, self.parts, self.table, self.count)
        if self.count >= self.size - 1:
            self.pieces.append(self.moving)
        return self.moving[0]

    def finish(self, targets, shapes):
        while self.count < 2 * self.size - 2:
            self.step()
        return place_rows(self.pieces, self.table, self.size - 1, targets, shapes)


class Plain:
    def __init__(self, parts):
        self.parts = parts

    def step(self, gate=None):
        return self.parts[0]

    def finish(self, targets, shapes):
        outs = [[] for shape in shapes]
        for part, runs in zip(lax.psum(self.parts, "dp"), targets):
            at = 0
            for share, out in runs:
                rows = part.shape[0] * share[0] // share[1]
                outs[out].append(part[at : at + rows])
                at += rows
        return [jnp.concatenate(rows, axis=0) for rows in outs]


def whole_blocks(heights, size):
    return size <= 16 and size % 2 == 0 and all(height % (8 * size) == 0 for height in heights)


def start_sum(parts, firsts, ways, size, table, rings):
    return Ring(parts, firsts, ways, size, table) if rings else Plain(parts)


def column_sums(values):
    return jnp.sum(values.astype(F32), axis=0, keepdims=True)


def over_tokens(left, right):
    return lax.dot_general(left, right, (((0,), (0,)), ((), ())), preferred_element_type=F32)


def copy_block(spots_ref, at, part_ref, first_ref):
    rows = first_ref.shape[0]
    first_ref[...] = part_ref[pl.ds(pl.multiple_of(spots_ref[0, at] * rows, 8), rows), :]


def mlp_grads_kernel(
    spots_ref,
    flags_ref,
    mlp_in_ref,
    d_pre_ref,
    activated_ref,
    d_mlp_ref,
    down_weight_ref,
    up_ref,
    down_ref,
    bias_ref,
    up_first_ref,
    down_first_ref,
    mine_ref,
    theirs_ref,
    part_ref,
):
    up_ref[...] = over_tokens(mlp_in_ref[...], d_pre_ref[...])
    down_ref[...] = over_tokens(activated_ref[...], d_mlp_ref[...])
    bias_ref[0:1, :] = column_sums(d_pre_ref[...])
    bias_ref[1:2, :] = column_sums(d_mlp_ref[...])
    copy_block(spots_ref, 0, up_ref, up_first_ref)
    copy_block(spots_ref, 1, down_ref, down_first_ref)
    part_ref[...] = jnp.dot(activated_ref[...], down_weight_ref[...], preferred_element_type=F32)
    split_rows(flags_ref[0], part_ref, mine_ref, theirs_ref)


def attention_grads_kernel(
    blocks,
    spots_ref,
    heads_in_ref,
    d_queries_ref,
    d_keys_ref,
    d_values_ref,
    attended_ref,
    d_attn_ref,
    bias_ref,
    upper_ref,
    lower_ref,
    upper_first_ref,
    lower_first_ref,
):
    feats = d_queries_ref.shape[1]
    width = heads_in_ref.shape[1]
    heads_in = heads_in_ref[...]
    upper_ref[0:feats, :] = over_tokens(d_queries_ref[...], heads_in)
    upper_ref[feats : 2 * feats, :] = over_tokens(d_keys_ref[...], heads_in)
    values_part = over_tokens(d_values_ref[...], heads_in)
    mixing_part = over_tokens(attended_ref[...].astype(BF16), d_attn_ref[...])
    run = feats // blocks
    extra = lower_ref.shape[0] // blocks - 2 * run
    for at in range(blocks):
        base = at * (2 * run + extra)
        lower_ref[base : base + run, :] = values_part[at * run : (at + 1) * run]
        lower_ref[base + run : base + 2 * run, :] = mixing_part[at * run : (at + 1) * run]
        lower_ref[base + 2 * run : base + 2 * run + extra, :] = jnp.zeros((extra, width), F32)
    base = 2 * run
    lower_ref[base : base + 2, :] = bias_ref[...]
    lower_ref[base + 2 : base + 3, :] = column_sums(d_attn_ref[...])
    lower_ref[base + 3 : base + 4, 0:feats] = column_sums(d_queries_ref[...])
    lower_ref[base + 4 : base + 5, 0:feats] = column_sums(d_values_ref[...])
    copy_block(spots_ref, 0, upper_ref, upper_first_ref)
    copy_block(spots_ref, 1, lower_ref, lower_first_ref)


def of_rows(values):
    centered = values - jnp.mean(values, axis=-1, keepdims=True)
    inverse = lax.rsqrt(jnp.mean(centered * centered, axis=-1, keepdims=True) + 1e-06)
    return centered * inverse, inverse


def against_rows(left, right):
    return lax.dot_general(left, right, (((1,), (1,)), ((), ())), preferred_element_type=F32)


def times(left, right):
    return jnp.dot(left, right, preferred_element_type=F32)


def latent_rows(ref):
    return [slice(at * SEQ, (at + 1) * SEQ) for at in range(ref.shape[0] // SEQ)]


def head_columns(columns):
    return [slice(at * HEAD_DIM, (at + 1) * HEAD_DIM) for at in range(columns // HEAD_DIM)]


def softmax_rows(queries, key_rows):
    scores = against_rows(queries, key_rows) * HEAD_DIM ** (-0.5)
    exp_terms = jnp.exp(scores - jnp.max(scores, axis=-1, keepdims=True))
    return exp_terms / jnp.sum(exp_terms, axis=-1, keepdims=True)


def attend_kernel(
    table_ref, flags_ref, mixing_bias_ref, up_bias_ref, down_bias_ref, hidden_ref, scale_ref, shift_ref, weight_ref, bias_ref, heads_in_ref, queries_ref, keys_ref, values_ref, attended_ref
):
    feats = queries_ref.shape[1]
    bias = bias_ref[...].astype(F32)
    for at, rows in enumerate(latent_rows(hidden_ref)):
        normed, inverse = of_rows(hidden_ref[rows, :].astype(F32))
        heads_in = (normed * (1.0 + scale_ref[at : at + 1, :]) + shift_ref[at : at + 1, :]).astype(BF16)
        heads_in_ref[rows, :] = heads_in
        queries = (against_rows(heads_in, weight_ref[0:feats, :]) + bias[0:1]).astype(BF16)
        keys = against_rows(heads_in, weight_ref[feats : 2 * feats, :]).astype(BF16)
        values = (against_rows(heads_in, weight_ref[2 * feats : 3 * feats, :]) + bias[1:2]).astype(BF16)
        queries_ref[rows, :] = queries
        keys_ref[rows, :] = keys
        values_ref[rows, :] = values
        mixed = []
        for cols in head_columns(feats):
            weights = softmax_rows(queries[:, cols], keys[:, cols])
            mixed.append(times(weights.astype(BF16), values[:, cols]))
        attended_ref[rows, :] = jnp.concatenate(mixed, axis=1).astype(BF16).astype(F32)


def in_order(flags_ref, blocks):
    low, high = flags_ref[0] == 1, flags_ref[1] == 1
    return [
        jnp.where(
            high,
            jnp.where(low, blocks[at ^ 3], blocks[at ^ 2]),
            jnp.where(low, blocks[at ^ 1], blocks[at]),
        )
        for at in range(4)
    ]


def widen_kernel(values_ref, behind_ref, out_ref):
    out_ref[...] = values_ref[...].astype(F32)


def cotangent_kernel(cotangent_ref, gate_ref, down_ref, d_mlp_ref, d_act_ref):
    for at, rows in enumerate(latent_rows(cotangent_ref)):
        d_mlp = (cotangent_ref[rows, :].astype(F32) * gate_ref[at : at + 1, :]).astype(BF16)
        d_mlp_ref[rows, :] = d_mlp
        d_act_ref[rows, :] = against_rows(d_mlp, down_ref[...])


def mlp_kernel(
    odd_ref,
    own_ref,
    beside_ref,
    across_ref,
    corner_ref,
    mixing_own_ref,
    mixing_beside_ref,
    mixing_across_ref,
    mixing_corner_ref,
    mixing_bias_ref,
    hidden_ref,
    gate_ref,
    scale_ref,
    shift_ref,
    up_ref,
    up_bias_ref,
    d_act_ref,
    attn_out_ref,
    mlp_in_ref,
    activated_ref,
    d_pre_ref,
    mine_ref,
    theirs_ref,
    part_ref,
):
    odd = odd_ref[0]
    blocks = (own_ref, beside_ref, across_ref, corner_ref)
    mixing = in_order(
        odd_ref,
        [ref[...].astype(BF16) for ref in (mixing_own_ref, mixing_beside_ref, mixing_across_ref, mixing_corner_ref)],
    )
    for at, rows in enumerate(latent_rows(hidden_ref)):
        attn_out = mixing_bias_ref[...].astype(F32)
        for block, piece in enumerate(in_order(odd_ref, [ref[rows, :] for ref in blocks])):
            attn_out = attn_out + times(piece.astype(BF16), mixing[block])
        attn_out_ref[rows, :] = attn_out
        middle = hidden_ref[rows, :].astype(F32) + gate_ref[at : at + 1, :] * attn_out
        normed, inverse = of_rows(middle)
        mlp_in = (normed * (1.0 + scale_ref[at : at + 1, :]) + shift_ref[at : at + 1, :]).astype(BF16)
        mlp_in_ref[rows, :] = mlp_in
        pre_act = times(mlp_in, up_ref[...]) + up_bias_ref[...].astype(F32)
        square = pre_act * pre_act
        bend = jnp.tanh(GELU_SCALE * pre_act * (1.0 + 0.044715 * square))
        activated_ref[rows, :] = (0.5 * pre_act * (1.0 + bend)).astype(BF16)
        slope = 0.5 * (1.0 + bend) + 0.5 * pre_act * (1.0 - bend * bend) * (
            GELU_SCALE * (1.0 + 3.0 * 0.044715 * square)
        )
        d_pre = (d_act_ref[rows, :] * slope).astype(BF16)
        d_pre_ref[rows, :] = d_pre
        part_ref[rows, :] = against_rows(d_pre, up_ref[...])
    split_rows(odd, part_ref, mine_ref, theirs_ref)


def split_rows(odd, part_ref, mine_ref, theirs_ref):
    half = mine_ref.shape[0]
    mine_ref[...] = part_ref[pl.ds(pl.multiple_of(odd * half, 8), half), :]
    theirs_ref[...] = part_ref[pl.ds(pl.multiple_of((1 - odd) * half, 8), half), :]


def join_halves(odd, full_ref, other_ref, joined_ref):
    half = full_ref.shape[0]
    joined_ref[pl.ds(pl.multiple_of(odd * half, 8), half), :] = full_ref[...]
    joined_ref[pl.ds(pl.multiple_of((1 - odd) * half, 8), half), :] = other_ref[...]


def norm_grad(upstream, normed, inverse):
    mean_grad = jnp.mean(upstream, axis=-1, keepdims=True)
    mean_proj = jnp.mean(upstream * normed, axis=-1, keepdims=True)
    return inverse * (upstream - mean_grad - normed * mean_proj)


def middle_back_kernel(
    odd_ref,
    full_ref,
    other_ref,
    attn_out_ref,
    hidden_ref,
    cotangent_ref,
    gate_ref,
    scale_ref,
    d_middle_ref,
    d_attn_ref,
    d_shift_ref,
    d_scale_ref,
    d_gate_ref,
    joined_ref,
):
    join_halves(odd_ref[0], full_ref, other_ref, joined_ref)
    for at, rows in enumerate(latent_rows(hidden_ref)):
        gate = gate_ref[at : at + 1, :]
        attn_out = attn_out_ref[rows, :]
        normed, inverse = of_rows(hidden_ref[rows, :].astype(F32) + gate * attn_out)
        d_mlp_in = joined_ref[rows, :]
        d_shift_ref[at : at + 1, :] = jnp.sum(d_mlp_in, axis=0, keepdims=True)
        d_scale_ref[at : at + 1, :] = jnp.sum(d_mlp_in * normed, axis=0, keepdims=True)
        d_middle = cotangent_ref[rows, :].astype(F32) + norm_grad(
            d_mlp_in * (1.0 + scale_ref[at : at + 1, :]), normed, inverse
        )
        d_middle_ref[rows, :] = d_middle
        d_gate_ref[at : at + 1, :] = jnp.sum(d_middle * attn_out, axis=0, keepdims=True)
        d_attn_ref[rows, :] = (d_middle * gate).astype(BF16)


def attention_back_kernel(
    odd_ref,
    d_attn_ref,
    mixing_ref,
    queries_ref,
    keys_ref,
    values_ref,
    weight_ref,
    d_queries_ref,
    d_keys_ref,
    d_values_ref,
    mine_ref,
    theirs_ref,
    part_ref,
):
    feats = queries_ref.shape[1]
    scale = HEAD_DIM ** (-0.5)
    for rows in latent_rows(d_attn_ref):
        d_attended = against_rows(d_attn_ref[rows, :], mixing_ref[...]).astype(BF16)
        queries, keys, values = queries_ref[rows, :], keys_ref[rows, :], values_ref[rows, :]
        d_queries, d_keys, d_values = [], [], []
        for cols in head_columns(feats):
            weights = softmax_rows(queries[:, cols], keys[:, cols])
            d_weights = against_rows(d_attended[:, cols], values[:, cols])
            row_dots = jnp.sum(weights * d_weights, axis=-1, keepdims=True)
            d_scores = (weights * (d_weights - row_dots)).astype(BF16)
            d_queries.append(times(d_scores, keys[:, cols]) * scale)
            d_keys.append(over_tokens(d_scores, queries[:, cols]) * scale)
            d_values.append(over_tokens(weights.astype(BF16), d_attended[:, cols]))
        total = None
        for at, (ref, columns) in enumerate(
            ((d_queries_ref, d_queries), (d_keys_ref, d_keys), (d_values_ref, d_values))
        ):
            joined = jnp.concatenate(columns, axis=1).astype(BF16)
            ref[rows, :] = joined
            term = times(joined, weight_ref[at * feats : (at + 1) * feats, :])
            total = term if total is None else total + term
        part_ref[rows, :] = total
    split_rows(odd_ref[0], part_ref, mine_ref, theirs_ref)


def input_back_kernel(
    odd_ref, full_ref, other_ref, hidden_ref, d_middle_ref, scale_ref, input_grad_ref, d_shift_ref, d_scale_ref, joined_ref
):
    join_halves(odd_ref[0], full_ref, other_ref, joined_ref)
    for at, rows in enumerate(latent_rows(hidden_ref)):
        normed, inverse = of_rows(hidden_ref[rows, :].astype(F32))
        d_heads_in = joined_ref[rows, :]
        d_shift_ref[at : at + 1, :] = jnp.sum(d_heads_in, axis=0, keepdims=True)
        d_scale_ref[at : at + 1, :] = jnp.sum(d_heads_in * normed, axis=0, keepdims=True)
        input_grad_ref[rows, :] = d_middle_ref[rows, :] + norm_grad(
            d_heads_in * (1.0 + scale_ref[at : at + 1, :]), normed, inverse
        )


def block_out_kernel(
    odd_ref,
    full_ref,
    other_ref,
    bias_ref,
    attn_out_ref,
    hidden_ref,
    cotangent_ref,
    gate_one_ref,
    gate_two_ref,
    block_out_ref,
    d_gate_ref,
    joined_ref,
):
    join_halves(odd_ref[0], full_ref, other_ref, joined_ref)
    for at, rows in enumerate(latent_rows(hidden_ref)):
        mlp_out = joined_ref[rows, :] + bias_ref[...].astype(F32)
        middle = hidden_ref[rows, :].astype(F32) + gate_one_ref[at : at + 1, :] * attn_out_ref[rows, :]
        block_out_ref[rows, :] = (middle + gate_two_ref[at : at + 1, :] * mlp_out).astype(BF16)
        d_gate_ref[at : at + 1, :] = jnp.sum(
            cotangent_ref[rows, :].astype(F32) * mlp_out, axis=0, keepdims=True
        )


def sum_kernel(left_ref, right_ref, out_ref):
    out_ref[...] = left_ref[...] + right_ref[...]


def modulation_grad_kernel(mods_ref, silu_ref, weight_ref, weight_grad_ref, bias_grad_ref, silu_grad_ref):
    mods = mods_ref[...].astype(BF16)
    weight_grad_ref[...] = lax.dot_general(
        silu_ref[...], mods, (((0,), (0,)), ((), ())), preferred_element_type=F32
    )
    bias_grad_ref[...] = jnp.sum(mods.astype(F32), axis=0, keepdims=True)
    silu_grad_ref[...] = lax.dot_general(
        mods, weight_ref[...], (((1,), (1,)), ((), ())), preferred_element_type=F32
    )


def after(values, gate):
    flat, tree = jax.tree.flatten(values)
    return jax.tree.unflatten(tree, lax.optimization_barrier((*flat, gate))[:-1])


def on_device(
    tensor_size,
    dp_size,
    hidden_in,
    out_cotangent,
    class_label,
    time_step,
    modulation_weight,
    modulation_bias,
    heads_weight,
    heads_bias,
    mixing_weight,
    mixing_bias,
    up_weight,
    up_bias,
    down_weight,
    down_bias,
    class_table,
    time_table,
):
    model_width = hidden_in.shape[1]
    own_latents = hidden_in.shape[0] // SEQ
    tok_rows = own_latents * SEQ
    lat_first = lax.axis_index("dp") * own_latents

    class_pick = jax.nn.one_hot(class_label, class_table.shape[0], dtype=BF16)
    time_pick = jax.nn.one_hot(time_step, time_table.shape[0], dtype=BF16)
    cond_part = jnp.dot(class_pick, class_table, preferred_element_type=F32) + jnp.dot(
        time_pick, time_table, preferred_element_type=F32
    )
    condition = join_columns(cond_part, tensor_size)
    silu_all = jax.nn.silu(condition).astype(BF16)
    silu_own = lax.dynamic_slice_in_dim(silu_all, lat_first, own_latents)
    mod_part = jnp.dot(silu_own, modulation_weight, preferred_element_type=F32) + modulation_bias.astype(F32)
    modulation = join_columns(mod_part, tensor_size)
    shift_one, scale_one, gate_one, shift_two, scale_two, gate_two = (
        modulation[:, number * model_width : (number + 1) * model_width] for number in range(6)
    )

    own_feats = heads_weight.shape[2]
    half = tok_rows // 2
    index = lax.axis_index("tensor")
    ways = (1, -1)
    table = ring_table(ways, dp_size)
    rings = whole_blocks((model_width, own_feats, up_weight.shape[1]), dp_size)
    flags = jnp.stack([index % 2, index // 2]).astype(jnp.int32)
    tokens = lambda dtype: jax.ShapeDtypeStruct((tok_rows, model_width), dtype)
    features = lambda dtype: jax.ShapeDtypeStruct((tok_rows, own_feats), dtype)
    halves = jax.ShapeDtypeStruct((half, model_width), F32)
    per_latent = jax.ShapeDtypeStruct((own_latents, model_width), F32)
    add = lambda left, right: call(sum_kernel, halves, (left, right), scalars=0, limit=SMALL_LIMIT)

    mixing_own = call(
        widen_kernel,
        jax.ShapeDtypeStruct(mixing_weight.shape, F32),
        (mixing_weight, gate_two),
        scalars=0,
        limit=SMALL_LIMIT,
    )
    bias_rows = [bias.reshape(1, bias.shape[0]) for bias in (mixing_bias, up_bias, down_bias)]
    heads_rows = heads_weight.transpose(1, 2, 0).reshape(3 * own_feats, model_width)
    heads_in, queries, key_rows, value_rows, attended = call(
        attend_kernel,
        (tokens(BF16), features(BF16), features(BF16), features(BF16), features(F32)),
        (table, flags, *bias_rows, hidden_in, scale_one, shift_one, heads_rows, heads_bias),
        scalars=2,
    )
    mixing_far = swap(mixing_own, tensor_size, 2)
    attended_across = swap(attended, tensor_size, 2)
    attended_beside = swap(attended, tensor_size, 1)
    d_mlp, d_act = call(
        cotangent_kernel,
        (tokens(BF16), jax.ShapeDtypeStruct((tok_rows, down_weight.shape[0]), F32)),
        (after(out_cotangent, attended), gate_two, down_weight),
        scalars=0,
    )
    attended_across = after(attended_across, d_act)
    mixing_across = after(mixing_far, attended_across)
    mixing_blocks = (
        mixing_own,
        swap(mixing_own, tensor_size, 1),
        mixing_across,
        swap(mixing_across, tensor_size, 1),
    )
    attn_out, mlp_in, activated, d_pre, mine, theirs = call(
        mlp_kernel,
        (
            tokens(F32),
            tokens(BF16),
            jax.ShapeDtypeStruct((tok_rows, up_weight.shape[1]), BF16),
            jax.ShapeDtypeStruct((tok_rows, up_weight.shape[1]), BF16),
            halves,
            halves,
        ),
        (
            flags,
            attended,
            attended_beside,
            attended_across,
            swap(attended_across, tensor_size, 1),
            *mixing_blocks,
            bias_rows[0],
            hidden_in,
            gate_one,
            scale_two,
            shift_two,
            up_weight,
            bias_rows[1],
            d_act,
        ),
        scratch=[pltpu.VMEM((tok_rows, model_width), F32)],
    )
    chip_two = add(mine, swap(theirs, tensor_size, 1))

    activated, d_pre = after((activated, d_pre), chip_two)
    up_part, down_part, mlp_bias, up_first, down_first, mine, theirs = call(
        mlp_grads_kernel,
        (
            jax.ShapeDtypeStruct((model_width, d_pre.shape[1]), F32),
            jax.ShapeDtypeStruct((activated.shape[1], model_width), F32),
            jax.ShapeDtypeStruct((2, model_width), F32),
            jax.ShapeDtypeStruct((model_width // dp_size, d_pre.shape[1]), F32),
            jax.ShapeDtypeStruct((activated.shape[1] // dp_size, model_width), F32),
            halves,
            halves,
        ),
        (table, flags, mlp_in, d_pre, activated, d_mlp, down_weight),
        scalars=2,
        scratch=[pltpu.VMEM((tok_rows, model_width), F32)],
    )
    mlp_ring = start_sum((up_part, down_part), (up_first, down_first), ways, dp_size, table, rings)
    chip_out = add(mine, swap(theirs, tensor_size, 1))
    mlp_ring.step()
    across_two = after(after(swap(chip_two, tensor_size, 2), chip_out), mlp_ring.step())
    full_two = add(chip_two, across_two)
    chip_out = after(chip_out, full_two)
    out_across = swap(chip_out, tensor_size, 2)
    d_middle, d_attn, d_shift_two, d_scale_two, d_gate_one = call(
        middle_back_kernel,
        (tokens(F32), tokens(BF16), per_latent, per_latent, per_latent),
        (
            flags,
            full_two,
            swap(full_two, tensor_size, 1),
            attn_out,
            hidden_in,
            out_cotangent,
            gate_one,
            scale_two,
        ),
        scratch=[pltpu.VMEM((tok_rows, model_width), F32)],
    )
    d_attn = after(d_attn, mlp_ring.step(d_attn))
    d_queries, d_keys, d_values, mine, theirs = call(
        attention_back_kernel,
        (features(BF16), features(BF16), features(BF16), halves, halves),
        (flags, d_attn, mixing_weight, queries, key_rows, value_rows, heads_rows),
        scratch=[pltpu.VMEM((tok_rows, model_width), F32)],
    )
    beside_one = after(swap(theirs, tensor_size, 1), mlp_ring.step(theirs))
    full_out = add(chip_out, out_across)
    chip_one = after(add(mine, beside_one), full_out)
    out_other = swap(full_out, tensor_size, 1)

    d_queries, d_keys, d_values = after((d_queries, d_keys, d_values), chip_one)
    blocks = dp_size if rings else 1
    upper_rows, lower_rows = 2 * own_feats, 2 * own_feats + 8 * dp_size
    upper_part, lower_part, upper_first, lower_first = call(
        functools.partial(attention_grads_kernel, blocks),
        (
            jax.ShapeDtypeStruct((upper_rows, model_width), F32),
            jax.ShapeDtypeStruct((lower_rows, model_width), F32),
            jax.ShapeDtypeStruct((upper_rows // dp_size, model_width), F32),
            jax.ShapeDtypeStruct((lower_rows // dp_size, model_width), F32),
        ),
        (table, heads_in, d_queries, d_keys, d_values, attended, d_attn, mlp_bias),
    )
    heads_ring = start_sum((upper_part, lower_part), (upper_first, lower_first), ways, dp_size, table, rings)
    block_out, d_gate_two = call(
        block_out_kernel,
        (jax.ShapeDtypeStruct((tok_rows, model_width), BF16), per_latent),
        (
            flags,
            full_out,
            after(out_other, upper_first),
            bias_rows[2],
            attn_out,
            hidden_in,
            out_cotangent,
            gate_one,
            gate_two,
        ),
        scratch=[pltpu.VMEM((tok_rows, model_width), F32)],
    )
    gate = mlp_ring.step(heads_ring.step(d_gate_two))
    across_one = after(swap(chip_one, tensor_size, 2), gate)
    full_one = add(chip_one, across_one)
    input_grad, d_shift_one, d_scale_one = call(
        input_back_kernel,
        (jax.ShapeDtypeStruct((tok_rows, model_width), F32), per_latent, per_latent),
        (
            flags,
            full_one,
            after(swap(full_one, tensor_size, 1), heads_ring.step(full_one)),
            hidden_in,
            d_middle,
            scale_one,
        ),
        scratch=[pltpu.VMEM((tok_rows, model_width), F32)],
    )
    d_modulation = jnp.concatenate(
        [d_shift_one, d_scale_one, d_gate_one, d_shift_two, d_scale_two, d_gate_two], axis=1
    )
    own_cols = modulation_weight.shape[1]
    own_mods = lax.dynamic_slice_in_dim(d_modulation, lax.axis_index("tensor") * own_cols, own_cols, 1)
    mlp_ring.step(own_mods)
    heads_ring.step(own_mods)
    whole = (1, 1)
    up_weight_sum, down_weight_sum = mlp_ring.finish(
        (((whole, 0),), ((whole, 1),)), (up_part.shape, down_part.shape)
    )
    run = (own_feats, lower_rows)
    heads_sum, mixing_weight_sum, bias_sum = heads_ring.finish(
        (((whole, 0),), ((run, 0), (run, 1), ((8 * dp_size, lower_rows), 2))),
        ((3 * own_feats, model_width), (own_feats, model_width), (8 * dp_size, model_width)),
    )
    heads_weight_sum = heads_sum.reshape(3, own_feats, model_width).transpose(2, 0, 1)
    up_bias_sum, down_bias_sum, mixing_bias_sum = (bias_sum[row] for row in range(3))
    heads_bias_sum = bias_sum[3:5, :own_feats]
    all_mods = gather_latents(own_mods, dp_size)
    mod_weight_sum, mod_bias_row, d_silu_part = call(
        modulation_grad_kernel,
        (
            jax.ShapeDtypeStruct((model_width, own_cols), F32),
            jax.ShapeDtypeStruct((1, own_cols), F32),
            jax.ShapeDtypeStruct((all_mods.shape[0], model_width), F32),
        ),
        (all_mods, silu_all, modulation_weight),
        scalars=0,
    )
    mod_bias_sum = mod_bias_row.reshape(own_cols)
    d_silu_own = scatter_features(d_silu_part, tensor_size)
    sigmoid_part = jax.nn.sigmoid(cond_part)
    d_condition = d_silu_own * sigmoid_part * (1.0 + cond_part * (1.0 - sigmoid_part))
    exact = dict(preferred_element_type=F32, precision=lax.Precision.HIGHEST)
    class_sum = jnp.einsum("lk,lf->kf", class_pick.astype(F32), d_condition, **exact)
    time_sum = jnp.einsum("lk,lf->kf", time_pick.astype(F32), d_condition, **exact)
    return (
        block_out,
        input_grad,
        mod_weight_sum,
        mod_bias_sum,
        heads_weight_sum,
        heads_bias_sum,
        mixing_weight_sum,
        mixing_bias_sum,
        up_weight_sum,
        up_bias_sum,
        down_weight_sum,
        down_bias_sum,
        class_sum,
        time_sum,
    )


def solution(mesh):
    in_specs = (
        P("dp", None),
        P("dp", None),
        P(),
        P(),
        P(None, "tensor"),
        P("tensor"),
        P(None, None, "tensor"),
        P(None, "tensor"),
        P("tensor", None),
        P(),
        P(None, "tensor"),
        P("tensor"),
        P("tensor", None),
        P(),
        P(None, "tensor"),
        P(None, "tensor"),
    )
    out_specs = (
        P("dp", None),
        P("dp", None),
        P(None, "tensor"),
        P("tensor"),
        P(None, None, "tensor"),
        P(None, "tensor"),
        P("tensor", None),
        P(),
        P(None, "tensor"),
        P("tensor"),
        P("tensor", None),
        P(),
        P(None, "tensor"),
        P(None, "tensor"),
    )

    def run(*args):
        return on_device(mesh.shape["tensor"], mesh.shape["dp"], *args)

    return jax.shard_map(run, mesh=mesh, in_specs=in_specs, out_specs=out_specs, check_vma=False)
```

time: 312 us -> 269 us (0.86)
  other arithmetic: 45.2 us -> 2.99 us
  waiting for transfers between devices: 82.7 us -> 117 us
  local copies, waits for them, and re-layouts: 43.7 us -> 13.9 us
  Pallas kernels: 33.9 us -> 51 us
  matrix products: 22.9 us -> 6.85 us
  starting transfers between devices: 78.6 us -> 75.1 us
    pallas_call x19 -> x31, Pallas kernels: 24.3 us -> 45 us  [call(): pl.pallas_call(kernel, out_shape=out_shape, in_specs=[IN_SMEM] * scalars...]
    ppermute x22 -> x24, waiting for transfers between devices: 21.9 us -> 39.2 us  [swap(): lax.ppermute(values, 'tensor', [(at, at ^ bit) for at in range(size)])]
    unnamed x318 -> x127, local copies, waits for them, and re-layouts: 29.1 us -> 12 us
    dot_general x12 -> x0, matrix products: 12.6 us -> none  [the longest x1 2.24 us: on_device(): jnp.einsum('bsd,dce->bsce', heads_in, heads_weight, preferred_element_typ...]
    add x8 -> x0, other arithmetic: 12.6 us -> none  [the longest x3 4.03 us: chip_rows(): return mine + swap(theirs, size, 1)]
    ppermute x56, waiting for transfers between devices: 60.8 us -> 72.9 us  [step(): lax.ppermute(held, 'dp', perm)]
    convert_element_type x10 -> x0, other arithmetic: 10.8 us -> none  [the longest x1 2.98 us: on_device(): (middle + gate_two * mlp_out).reshape(tok_rows, model_width).astype(BF16)]
    reduce_sum x7 -> x0, other arithmetic: 5.61 us -> none  [the longest x1 1.5 us: norm_back(): mean_grad = jnp.mean(upstream, axis=-1, keepdims=True)]
  transfers between devices with their start and end apart: 82 -> 84, of which waited for: 27 -> 39; matrix products, arithmetic and copies ran while one was open for 22% -> 3% of each run, Pallas kernels for 8% -> 14%
where the time goes in v3:
time: 269 us
  waiting for transfers between devices  117 us (43%)
  starting transfers between devices  75.1 us (28%)
  Pallas kernels  51 us (19%)
  local copies, waits for them, and re-layouts  13.9 us (5%)
  matrix products  6.85 us (3%)
  other arithmetic  2.99 us (1%)
    ppermute x56, waiting for transfers between devices, step(): lax.ppermute(held, 'dp', perm)  72.9 us
    ppermute x56, starting transfers between devices, step(): lax.ppermute(held, 'dp', perm)  56.9 us
    pallas_call x31, Pallas kernels, call(): pl.pallas_call(kernel, out_shape=out_shape, in_specs=[IN_SMEM] * scalars...  45 us
    ppermute x24, waiting for transfers between devices, swap(): lax.ppermute(values, 'tensor', [(at, at ^ bit) for at in range(size)])  39.2 us
    ppermute x24, starting transfers between devices, swap(): lax.ppermute(values, 'tensor', [(at, at ^ bit) for at in range(size)])  12.6 us
    unnamed x127, local copies, waits for them, and re-layouts  12 us
    pallas_call x2, Pallas kernels, place_rows(): pl.pallas_call(functools.partial(place_kernel, steps, first, targets, len...  6.09 us
  transfers between devices with their start and end apart: 84, of which 39 were waited for; matrix products, arithmetic and copies ran while one was open for 3% of the time, Pallas kernels for 14%

profile of v3, /device:TPU:0, one launch (start us, length us, event | category | flops | bytes accessed | tf_op | source)
XLA Modules:
  0.0 268.9 jit_solution(10537550785669533930)
XLA Ops:
  4.4 2.6 collective-permute-start.1
  17.7 3.6 %shard_map.272 = (bf16[512,768]{1,0:T(8,128)(2,1)S(1)}, bf16[512,192]{1,0:T(8,128)(2,1)S(1)}, bf16[512,192]{1,0:T(8,128)(2,1)S(1)}, bf16[512,192]{1,0:T(8,128)(2,1)S(1)}, f32[512,192]{1,0:T(8,128)S(1)}) custom-call(s32[15,2]{1,0:T(8,128)S(1)} %add_select_fusion.table_ref.spots_ref, s32[2]{0:T(128)S(1)} %pad_add_fusion.flags_ref.odd_ref, ...), custom_call_target="tpu_custom_call" | custom-call | flops 1 | bytes 1 | tf_op jit(solution)/shard_map/pallas_call | solution.py:66
  22.9 19.9 %collective-permute-done.7.across_ref = f32[512,192]{1,0:T(8,128)S(1)} collective-permute-done((f32[512,192]{1,0:T(8,128)S(1)}, f32[512,192]{1,0:T(8,128)S(1)}, u32[]{:S(2)}, u32[]{:S(2)}) %collective-permute-start.7) | collective-permute-done | bytes 393248 | tf_op jit(solution)/shard_map/ppermute | solution.py:18
  43.3 2.2 collective-permute-done.6.beside_ref
  46.3 5.1 %shard_map.275 = (f32[512,768]{1,0:T(8,128)S(1)}, bf16[512,768]{1,0:T(8,128)(2,1)S(1)}, bf16[512,768]{1,0:T(8,128)(2,1)S(1)}, bf16[512,768]{1,0:T(8,128)(2,1)S(1...) custom-call(s32[2]{0:T(128)S(1)} %pad_add_fusion.flags_ref.odd_ref, ...), custom_call_target="tpu_custom_call" | custom-call | flops 1 | bytes 1 | tf_op jit(solution)/shard_map/pallas_call | solution.py:66
  53.9 3.0 %shard_map.277 = (f32[768,768]{1,0:T(8,128)S(1)}, f32[768,768]{1,0:T(8,128)S(1)}, f32[2,768]{1,0:T(2,128)S(1)}, f32[96,768]{1,0:T(8,128)S(1)}, f32[96,768]{1,0:T...) custom-call(s32[15,2]{1,0:T(8,128)S(1)} %add_select_fusion.table_ref.spots_ref, ...), custom_call_target="tpu_custom_call" | custom-call | flops 1 | bytes 1 | tf_op jit(solution)/shard_map/pallas_call | solution.py:66
  60.5 7.0 %collective-permute-done.15.refs_0_ = f32[96,768]{1,0:T(8,128)S(1)} collective-permute-done((f32[96,768]{1,0:T(8,128)S(1)}, f32[96,768]{1,0:T(8,128)S(1)}, u32[]{:S(2)}, u32[]{:S(2)}) %collective-permute-start.15) | collective-permute-done | bytes 294944 | tf_op jit(solution)/shard_map/ppermute | solution.py:173
  71.6 5.8 %collective-permute-done.17.refs_0_ = f32[96,768]{1,0:T(8,128)S(1)} collective-permute-done((f32[96,768]{1,0:T(8,128)S(1)}, f32[96,768]{1,0:T(8,128)S(1)}, u32[]{:S(2)}, u32[]{:S(2)}) %collective-permute-start.17) | collective-permute-done | bytes 294944 | tf_op jit(solution)/shard_map/ppermute | solution.py:173
  85.8 3.3 %collective-permute-done.23.refs_1_ = f32[96,768]{1,0:T(8,128)S(1)} collective-permute-done((f32[96,768]{1,0:T(8,128)S(1)}, f32[96,768]{1,0:T(8,128)S(1)}, u32[]{:S(2)}, u32[]{:S(2)}) %collective-permute-start.23) | collective-permute-done | bytes 294944 | tf_op jit(solution)/shard_map/ppermute | solution.py:173
  90.5 5.2 %shard_map.285 = (bf16[512,192]{1,0:T(8,128)(2,1)S(1)}, bf16[512,192]{1,0:T(8,128)(2,1)S(1)}, bf16[512,192]{1,0:T(8,128)(2,1)S(1)}, f32[256,768]{1,0:T(8,128)S(1)}, f32[256,768]{1,0:T(8,128)S(1)}) custom-call(s32[2]{0:T(128)S(1)} %pad_add_fusion.flags_ref.odd_ref, bf16[512,768]{1,0:T(8,128)(2,1)S(1)} %get-tuple-element.152.d_attn_ref, ...), custom_call_target="tpu_custom_call" | custom-call | flops 1 | bytes 1 | tf_op jit(solution)/shard_map/pallas_call | solution.py:66
  97.9 3.3 %collective-permute-done.19.right_ref = f32[256,768]{1,0:T(8,128)S(1)} collective-permute-done((f32[256,768]{1,0:T(8,128)S(1)}, f32[256,768]{1,0:T(8,128)S(1)}, u32[]{:S(2)}, u32[]{:S(2)}) %collective-permute-start.19) | collective-permute-done | bytes 786464 | tf_op jit(solution)/shard_map/ppermute | solution.py:18
  101.4 3.9 %collective-permute-done.26.refs_1_ = f32[96,768]{1,0:T(8,128)S(1)} collective-permute-done((f32[96,768]{1,0:T(8,128)S(1)}, f32[96,768]{1,0:T(8,128)S(1)}, u32[]{:S(2)}, u32[]{:S(2)}) %collective-permute-start.26) | collective-permute-done | bytes 294944 | tf_op jit(solution)/shard_map/ppermute | solution.py:173
  113.0 2.3 shard_map.289
  115.4 4.3 %collective-permute-done.30.refs_0_ = f32[48,768]{1,0:T(8,128)S(1)} collective-permute-done((f32[48,768]{1,0:T(8,128)S(1)}, f32[48,768]{1,0:T(8,128)S(1)}, u32[]{:S(2)}, u32[]{:S(2)}) %collective-permute-start.30) | collective-permute-done | bytes 147488 | tf_op jit(solution)/shard_map/ppermute | solution.py:173
  121.9 3.3 %collective-permute-done.27.right_ref = f32[256,768]{1,0:T(8,128)S(1)} collective-permute-done((f32[256,768]{1,0:T(8,128)S(1)}, f32[256,768]{1,0:T(8,128)S(1)}, u32[]{:S(2)}, u32[]{:S(2)}) %collective-permute-start.27) | collective-permute-done | bytes 786464 | tf_op jit(solution)/shard_map/ppermute | solution.py:18
  130.3 4.5 %collective-permute-done.33.refs_0_ = f32[48,768]{1,0:T(8,128)} collective-permute-done((f32[48,768]{1,0:T(8,128)}, f32[48,768]{1,0:T(8,128)}, u32[]{:S(2)}, u32[]{:S(2)}) %collective-permute-start.33) | collective-permute-done | bytes 147488 | tf_op jit(solution)/shard_map/ppermute | solution.py:173
  138.6 4.0 %shard_map.294 = (f32[512,768]{1,0:T(8,128)}, f32[2,768]{1,0:T(2,128)S(1)}, f32[2,768]{1,0:T(2,128)S(1)}) custom-call(s32[2]{0:T(128)S(1)} %copy-done.41, f32[256,768]{1,0:T(8,128)} %shard_map.292.full_ref, f32[256,768]{1,0:T(8,128)} %collective-permute-done.32.other_ref, bf16[512,768]{1,0:T(8,128)(2,1)S(1)} %copy-done.10, f32[512,768]{1,0:T(8,128)S(1)} %copy-done.17, ...), custom_call_target="tpu_custom_call" | custom-call | flops 1 | bytes 1 | tf_op jit(solution)/shard_map/pallas_call | solution.py:66
  148.2 5.0 %collective-permute-done.65.refs_0_ = f32[96,768]{1,0:T(8,128)S(1)} collective-permute-done((f32[96,768]{1,0:T(8,128)S(1)}, f32[96,768]{1,0:T(8,128)S(1)}, u32[]{:S(2)}, u32[]{:S(2)}) %collective-permute-start.65) | collective-permute-done | bytes 294944 | tf_op jit(solution)/shard_map/ppermute | solution.py:173
  160.0 5.0 %collective-permute-done.41.refs_0_ = f32[48,768]{1,0:T(8,128)S(1)} collective-permute-done((f32[48,768]{1,0:T(8,128)S(1)}, f32[48,768]{1,0:T(8,128)S(1)}, u32[]{:S(2)}, u32[]{:S(2)}) %collective-permute-start.41) | collective-permute-done | bytes 147488 | tf_op jit(solution)/shard_map/ppermute | solution.py:173
  178.3 4.2 %collective-permute-done.45.refs_0_ = f32[48,768]{1,0:T(8,128)} collective-permute-done((f32[48,768]{1,0:T(8,128)}, f32[48,768]{1,0:T(8,128)}, u32[]{:S(2)}, u32[]{:S(2)}) %collective-permute-start.45) | collective-permute-done | bytes 147488 | tf_op jit(solution)/shard_map/ppermute | solution.py:173
  183.5 2.3 collective-permute-start.47
  189.0 2.8 %collective-permute-done.48.refs_1_ = f32[56,768]{1,0:T(8,128)S(1)} collective-permute-done((f32[56,768]{1,0:T(8,128)S(1)}, f32[56,768]{1,0:T(8,128)S(1)}, u32[]{:S(2)}, u32[]{:S(2)}) %collective-permute-start.48) | collective-permute-done | bytes 172064 | tf_op jit(solution)/shard_map/ppermute | solution.py:173
  196.1 2.8 %collective-permute-start.37 = (f32[4,1152]{1,0:T(4,128)S(1)}, f32[4,1152]{1,0:T(4,128)S(1)}, u32[]{:S(2)}, u32[]{:S(2)}) collective-permute-start(f32[4,1152]{1,0:T(4,128)S(1)} %get-tuple-element.240), channel_id=1, source_target_pairs={{0,16},{4,20},{8,24},{12,28},{16,0},{20,4},{24,8},{28,12},{1,17},{... | collective-permute-start | bytes 55304 | tf_op jit(solution)/shard_map/ppermute | solution.py:39
  198.9 5.3 %collective-permute-done.36 = f32[4,1152]{1,0:T(4,128)S(1)} collective-permute-done((f32[4,1152]{1,0:T(4,128)S(1)}, f32[4,1152]{1,0:T(4,128)S(1)}, u32[]{:S(2)}, u32[]{:S(2)}) %collective-permute-start.36) | collective-permute-done | bytes 18464 | tf_op jit(solution)/shard_map/ppermute | solution.py:39
  213.5 5.5 %collective-permute-done.51.refs_4_ = f32[48,768]{1,0:T(8,128)S(1)} collective-permute-done((f32[48,768]{1,0:T(8,128)S(1)}, f32[48,768]{1,0:T(8,128)S(1)}, u32[]{:S(2)}, u32[]{:S(2)}) %collective-permute-start.51) | collective-permute-done | bytes 147488 | tf_op jit(solution)/shard_map/ppermute | solution.py:173
  225.3 2.6 shard_map.295
  230.6 2.7 %collective-permute-done.83 = f32[16,192]{1,0:T(8,128)S(1)} collective-permute-done((f32[16,192]{1,0:T(8,128)S(1)}, f32[16,192]{1,0:T(8,128)S(1)}, u32[]{:S(2)}, u32[]{:S(2)}) %collective-permute-start.83) | collective-permute-done | bytes 12320 | tf_op jit(solution)/shard_map/ppermute | solution.py:18
  241.1 2.3 collective-permute-done.58.refs_11_
  246.0 3.8 %collective-permute-done.59.refs_12_ = f32[48,768]{1,0:T(8,128)S(1)} collective-permute-done((f32[48,768]{1,0:T(8,128)S(1)}, f32[48,768]{1,0:T(8,128)S(1)}, u32[]{:S(2)}, u32[]{:S(2)}) %collective-permute-start.59) | collective-permute-done | bytes 147488 | tf_op jit(solution)/shard_map/ppermute | solution.py:173
  256.7 2.8 %collective-permute-done.62.refs_15_ = f32[56,768]{1,0:T(8,128)S(1)} collective-permute-done((f32[56,768]{1,0:T(8,128)S(1)}, f32[56,768]{1,0:T(8,128)S(1)}, u32[]{:S(2)}, u32[]{:S(2)}) %collective-permute-start.62) | collective-permute-done | bytes 172064 | tf_op jit(solution)/shard_map/ppermute | solution.py:173
  261.4 2.6 shard_map.301
  265.2 3.5 %shard_map.304 = (f32[768,768]{1,0:T(8,128)}, f32[768,768]{1,0:T(8,128)}) custom-call(s32[15,2]{1,0:T(8,128)S(1)} %add_select_fusion.table_ref.spots_ref, f32[96,768]{1,0:T(8,128)S(1)} %copy-done.21, f32[96,768]{1,0:T(8,128)S(1)} %copy-done.23, f32[96,768]{1,0:T(8,128)S(1)} %collective-permute-done.67.refs_2_, ...), custom_call_target="tpu_custom_call" | custom-call | flops 1 | bytes 1 | tf_op jit(solution)/shard_map/pallas_call | solution.py:125
  (325 shorter events, 130.7 us)
Async XLA Ops:
  16.2 26.6 %collective-permute-start.10 = (f32[192,768]{1,0:T(8,128)S(1)}, f32[192,768]{1,0:T(8,128)S(1)}, u32[]{:S(2)}, u32[]{:S(2)}) collective-permute-start(f32[192,768]{1,0:T(8,128)S(1)} %shard_map.274.mixing_own_ref), channel_id=1, source_target_pairs={{0,2},{1,3},{2,0},{3,1},{4,6},{5,7},{6,4},{7,5},{8,10},{9,11},{10,... | collective-permute-start | bytes 1769480 | tf_op jit(solution)/shard_map/ppermute | solution.py:18
  21.3 21.5 %collective-permute-start.7 = (f32[512,192]{1,0:T(8,128)S(1)}, f32[512,192]{1,0:T(8,128)S(1)}, u32[]{:S(2)}, u32[]{:S(2)}) collective-permute-start(f32[512,192]{1,0:T(8,128)S(1)} %get-tuple-element.120.own_ref.attended_ref), channel_id=1, source_target_pairs={{0,2},{1,3},{2,0},{3,1},{4,6},{5,7},{6,4},{7,5},{8,10},{9,11},{10,... | collective-permute-start | bytes 1179656 | tf_op jit(solution)/shard_map/ppermute | solution.py:18
  22.0 23.5 %collective-permute-start.9 = (f32[192,768]{1,0:T(8,128)S(1)}, f32[192,768]{1,0:T(8,128)S(1)}, u32[]{:S(2)}, u32[]{:S(2)}) collective-permute-start(f32[192,768]{1,0:T(8,128)S(1)} %shard_map.274.mixing_own_ref), channel_id=1, source_target_pairs={{0,1},{1,0},{2,3},{3,2},{4,5},{5,4},{6,7},{7,6},{8,9},{9,8},{10,11... | collective-permute-start | bytes 1769480 | tf_op jit(solution)/shard_map/ppermute | solution.py:18
  56.9 22.6 %collective-permute-start.13 = (f32[256,768]{1,0:T(8,128)S(1)}, f32[256,768]{1,0:T(8,128)S(1)}, u32[]{:S(2)}, u32[]{:S(2)}) collective-permute-start(f32[256,768]{1,0:T(8,128)S(1)} %get-tuple-element.134), channel_id=1, source_target_pairs={{0,1},{1,0},{2,3},{3,2},{4,5},{5,4},{6,7},{7,6},{8,9},{9,8},{10,11... | collective-permute-start | bytes 2359304 | tf_op jit(solution)/shard_map/ppermute | solution.py:18
  57.1 22.5 %collective-permute-start.14 = (f32[256,768]{1,0:T(8,128)S(1)}, f32[256,768]{1,0:T(8,128)S(1)}, u32[]{:S(2)}, u32[]{:S(2)}) collective-permute-start(f32[256,768]{1,0:T(8,128)S(1)} %shard_map.276.left_ref), channel_id=1, source_target_pairs={{0,2},{1,3},{2,0},{3,1},{4,6},{5,7},{6,4},{7,5},{8,10},{9,11},{10,... | collective-permute-start | bytes 2359304 | tf_op jit(solution)/shard_map/ppermute | solution.py:18
  81.8 19.3 %collective-permute-start.19 = (f32[256,768]{1,0:T(8,128)S(1)}, f32[256,768]{1,0:T(8,128)S(1)}, u32[]{:S(2)}, u32[]{:S(2)}) collective-permute-start(f32[256,768]{1,0:T(8,128)S(1)} %shard_map.278.left_ref), channel_id=1, source_target_pairs={{0,2},{1,3},{2,0},{3,1},{4,6},{5,7},{6,4},{7,5},{8,10},{9,11},{10,... | collective-permute-start | bytes 2359304 | tf_op jit(solution)/shard_map/ppermute | solution.py:18
  95.7 10.5 %collective-permute-start.24 = (f32[256,768]{1,0:T(8,128)S(1)}, f32[256,768]{1,0:T(8,128)S(1)}, u32[]{:S(2)}, u32[]{:S(2)}) collective-permute-start(f32[256,768]{1,0:T(8,128)S(1)} %get-tuple-element.160), channel_id=1, source_target_pairs={{0,1},{1,0},{2,3},{3,2},{4,5},{5,4},{6,7},{7,6},{8,9},{9,8},{10,11... | collective-permute-start | bytes 2359304 | tf_op jit(solution)/shard_map/ppermute | solution.py:18
  101.3 11.3 %collective-permute-start.20 = (f32[256,768]{1,0:T(8,128)S(1)}, f32[256,768]{1,0:T(8,128)S(1)}, u32[]{:S(2)}, u32[]{:S(2)}) collective-permute-start(f32[256,768]{1,0:T(8,128)S(1)} %shard_map.282.full_ref), channel_id=1, source_target_pairs={{0,1},{1,0},{2,3},{3,2},{4,5},{5,4},{6,7},{7,6},{8,9},{9,8},{10,11... | collective-permute-start | bytes 2359304 | tf_op jit(solution)/shard_map/ppermute | solution.py:18
  106.3 18.9 %collective-permute-start.27 = (f32[256,768]{1,0:T(8,128)S(1)}, f32[256,768]{1,0:T(8,128)S(1)}, u32[]{:S(2)}, u32[]{:S(2)}) collective-permute-start(f32[256,768]{1,0:T(8,128)S(1)} %shard_map.287.left_ref), channel_id=1, source_target_pairs={{0,2},{1,3},{2,0},{3,1},{4,6},{5,7},{6,4},{7,5},{8,10},{9,11},{10,... | collective-permute-start | bytes 2359304 | tf_op jit(solution)/shard_map/ppermute | solution.py:18
  107.3 13.9 %collective-permute-start.29 = (f32[96,768]{1,0:T(8,128)S(1)}, f32[96,768]{1,0:T(8,128)S(1)}, u32[]{:S(2)}, u32[]{:S(2)}) collective-permute-start(f32[96,768]{1,0:T(8,128)S(1)} %get-tuple-element.174), channel_id=1, source_target_pairs={{0,4},{8,0},{16,8},{24,16},{28,24},{20,28},{12,20},{4,12},{1,5},{9... | collective-permute-start | bytes 884744 | tf_op jit(solution)/shard_map/ppermute | solution.py:173
  108.8 12.3 %collective-permute-start.28 = (f32[96,768]{1,0:T(8,128)S(1)}, f32[96,768]{1,0:T(8,128)S(1)}, u32[]{:S(2)}, u32[]{:S(2)}) collective-permute-start(f32[96,768]{1,0:T(8,128)S(1)} %get-tuple-element.164), channel_id=1, source_target_pairs={{0,8},{8,16},{16,24},{24,28},{28,20},{20,12},{12,4},{4,0},{1,9},{9... | collective-permute-start | bytes 884744 | tf_op jit(solution)/shard_map/ppermute | solution.py:173
  126.2 11.1 %collective-permute-start.32 = (f32[256,768]{1,0:T(8,128)}, f32[256,768]{1,0:T(8,128)}, u32[]{:S(2)}, u32[]{:S(2)}) collective-permute-start(f32[256,768]{1,0:T(8,128)} %shard_map.292.full_ref), channel_id=1, source_target_pairs={{0,1},{1,0},{2,3},{3,2},{4,5},{5,4},{6,7},{7,6},{8,9},{9,8},{10,11... | collective-permute-start | bytes 2359304 | tf_op jit(solution)/shard_map/ppermute | solution.py:18
  128.3 15.0 %collective-permute-start.63 = (f32[96,768]{1,0:T(8,128)}, f32[96,768]{1,0:T(8,128)S(1)}, u32[]{:S(2)}, u32[]{:S(2)}) collective-permute-start(f32[96,768]{1,0:T(8,128)} %copy-done.51), channel_id=1, source_target_pairs={{0,8},{8,16},{16,24},{24,28},{28,20},{20,12},{12,4},{4,0},{1,9},{9... | collective-permute-start | bytes 884744 | tf_op jit(solution)/shard_map/ppermute | solution.py:173
  129.9 13.5 %collective-permute-start.64 = (f32[96,768]{1,0:T(8,128)}, f32[96,768]{1,0:T(8,128)S(1)}, u32[]{:S(2)}, u32[]{:S(2)}) collective-permute-start(f32[96,768]{1,0:T(8,128)} %copy-done.52), channel_id=1, source_target_pairs={{0,4},{8,0},{16,8},{24,16},{28,24},{20,28},{12,20},{4,12},{1,5},{9... | collective-permute-start | bytes 884744 | tf_op jit(solution)/shard_map/ppermute | solution.py:173
  146.2 11.1 %collective-permute-start.40 = (f32[56,768]{1,0:T(8,128)S(1)}, f32[56,768]{1,0:T(8,128)S(1)}, u32[]{:S(2)}, u32[]{:S(2)}) collective-permute-start(f32[56,768]{1,0:T(8,128)S(1)} %get-tuple-element.200), channel_id=1, source_target_pairs={{0,4},{8,0},{16,8},{24,16},{28,24},{20,28},{12,20},{4,12},{1,5},{9... | collective-permute-start | bytes 516104 | tf_op jit(solution)/shard_map/ppermute | solution.py:173
  155.2 14.5 %collective-permute-start.67 = (f32[96,768]{1,0:T(8,128)S(1)}, f32[96,768]{1,0:T(8,128)S(1)}, u32[]{:S(2)}, u32[]{:S(2)}) collective-permute-start(f32[96,768]{1,0:T(8,128)S(1)} %get-tuple-element.221.refs_0_), channel_id=1, source_target_pairs={{0,8},{8,16},{16,24},{24,28},{28,20},{20,12},{12,4},{4,0},{1,9},{9... | collective-permute-start | bytes 884744 | tf_op jit(solution)/shard_map/ppermute | solution.py:173
  156.8 14.4 %collective-permute-start.68 = (f32[96,768]{1,0:T(8,128)S(1)}, f32[96,768]{1,0:T(8,128)S(1)}, u32[]{:S(2)}, u32[]{:S(2)}) collective-permute-start(f32[96,768]{1,0:T(8,128)S(1)} %get-tuple-element.222.refs_1_), channel_id=1, source_target_pairs={{0,4},{8,0},{16,8},{24,16},{28,24},{20,28},{12,20},{4,12},{1,5},{9... | collective-permute-start | bytes 884744 | tf_op jit(solution)/shard_map/ppermute | solution.py:173
  169.7 16.2 %collective-permute-start.69 = (f32[96,768]{1,0:T(8,128)S(1)}, f32[96,768]{1,0:T(8,128)S(1)}, u32[]{:S(2)}, u32[]{:S(2)}) collective-permute-start(f32[96,768]{1,0:T(8,128)S(1)} %collective-permute-done.67.refs_2_), channel_id=1, source_target_pairs={{0,8},{8,16},{16,24},{24,28},{28,20},{20,12},{12,4},{4,0},{1,9},{9... | collective-permute-start | bytes 884744 | tf_op jit(solution)/shard_map/ppermute | solution.py:173
  171.2 16.7 %collective-permute-start.70 = (f32[96,768]{1,0:T(8,128)S(1)}, f32[96,768]{1,0:T(8,128)}, u32[]{:S(2)}, u32[]{:S(2)}) collective-permute-start(f32[96,768]{1,0:T(8,128)S(1)} %collective-permute-done.68.refs_3_), channel_id=1, source_target_pairs={{0,4},{8,0},{16,8},{24,16},{28,24},{20,28},{12,20},{4,12},{1,5},{9... | collective-permute-start | bytes 884744 | tf_op jit(solution)/shard_map/ppermute | solution.py:173
  185.9 20.3 %collective-permute-start.71 = (f32[96,768]{1,0:T(8,128)S(1)}, f32[96,768]{1,0:T(8,128)}, u32[]{:S(2)}, u32[]{:S(2)}) collective-permute-start(f32[96,768]{1,0:T(8,128)S(1)} %collective-permute-done.69.refs_4_), channel_id=1, source_target_pairs={{0,8},{8,16},{16,24},{24,28},{28,20},{20,12},{12,4},{4,0},{1,9},{9... | collective-permute-start | bytes 884744 | tf_op jit(solution)/shard_map/ppermute | solution.py:173
  187.9 18.4 %collective-permute-start.72 = (f32[96,768]{1,0:T(8,128)}, f32[96,768]{1,0:T(8,128)}, u32[]{:S(2)}, u32[]{:S(2)}) collective-permute-start(f32[96,768]{1,0:T(8,128)} %collective-permute-done.70.refs_5_), channel_id=1, source_target_pairs={{0,4},{8,0},{16,8},{24,16},{28,24},{20,28},{12,20},{4,12},{1,5},{9... | collective-permute-start | bytes 884744 | tf_op jit(solution)/shard_map/ppermute | solution.py:173
  196.1 12.2 %collective-permute-start.37 = (f32[4,1152]{1,0:T(4,128)S(1)}, f32[4,1152]{1,0:T(4,128)S(1)}, u32[]{:S(2)}, u32[]{:S(2)}) collective-permute-start(f32[4,1152]{1,0:T(4,128)S(1)} %get-tuple-element.240), channel_id=1, source_target_pairs={{0,16},{4,20},{8,24},{12,28},{16,0},{20,4},{24,8},{28,12},{1,17},{... | collective-permute-start | bytes 55304 | tf_op jit(solution)/shard_map/ppermute | solution.py:39
  206.2 14.8 %collective-permute-start.73 = (f32[96,768]{1,0:T(8,128)}, f32[96,768]{1,0:T(8,128)S(1)}, u32[]{:S(2)}, u32[]{:S(2)}) collective-permute-start(f32[96,768]{1,0:T(8,128)} %collective-permute-done.71.refs_6_), channel_id=1, source_target_pairs={{0,8},{8,16},{16,24},{24,28},{28,20},{20,12},{12,4},{4,0},{1,9},{9... | collective-permute-start | bytes 884744 | tf_op jit(solution)/shard_map/ppermute | solution.py:173
  206.2 15.1 %collective-permute-start.74 = (f32[96,768]{1,0:T(8,128)}, f32[96,768]{1,0:T(8,128)S(1)}, u32[]{:S(2)}, u32[]{:S(2)}) collective-permute-start(f32[96,768]{1,0:T(8,128)} %collective-permute-done.72.refs_7_), channel_id=1, source_target_pairs={{0,4},{8,0},{16,8},{24,16},{28,24},{20,28},{12,20},{4,12},{1,5},{9... | collective-permute-start | bytes 884744 | tf_op jit(solution)/shard_map/ppermute | solution.py:173
  208.3 14.8 %collective-permute-start.38 = (f32[4,1152]{1,0:T(4,128)S(1)}, f32[4,1152]{1,0:T(4,128)S(1)}, u32[]{:S(2)}, u32[]{:S(2)}) collective-permute-start(f32[4,1152]{1,0:T(4,128)S(1)} %get-tuple-element.240), channel_id=1, source_target_pairs={{0,24},{4,28},{8,0},{12,4},{16,8},{20,12},{24,16},{28,20},{1,25},{... | collective-permute-start | bytes 55304 | tf_op jit(solution)/shard_map/ppermute | solution.py:39
  219.3 16.7 %collective-permute-start.56 = (f32[56,768]{1,0:T(8,128)S(1)}, f32[56,768]{1,0:T(8,128)S(1)}, u32[]{:S(2)}, u32[]{:S(2)}) collective-permute-start(f32[56,768]{1,0:T(8,128)S(1)} %collective-permute-done.54.refs_7_), channel_id=1, source_target_pairs={{0,4},{8,0},{16,8},{24,16},{28,24},{20,28},{12,20},{4,12},{1,5},{9... | collective-permute-start | bytes 516104 | tf_op jit(solution)/shard_map/ppermute | solution.py:173
  221.1 17.0 %collective-permute-start.75 = (f32[96,768]{1,0:T(8,128)S(1)}, f32[96,768]{1,0:T(8,128)S(1)}, u32[]{:S(2)}, u32[]{:S(2)}) collective-permute-start(f32[96,768]{1,0:T(8,128)S(1)} %collective-permute-done.73.refs_8_), channel_id=1, source_target_pairs={{0,8},{8,16},{16,24},{24,28},{28,20},{20,12},{12,4},{4,0},{1,9},{9... | collective-permute-start | bytes 884744 | tf_op jit(solution)/shard_map/ppermute | solution.py:173
  221.4 17.5 %collective-permute-start.76 = (f32[96,768]{1,0:T(8,128)S(1)}, f32[96,768]{1,0:T(8,128)S(1)}, u32[]{:S(2)}, u32[]{:S(2)}) collective-permute-start(f32[96,768]{1,0:T(8,128)S(1)} %collective-permute-done.74.refs_9_), channel_id=1, source_target_pairs={{0,4},{8,0},{16,8},{24,16},{28,24},{20,28},{12,20},{4,12},{1,5},{9... | collective-permute-start | bytes 884744 | tf_op jit(solution)/shard_map/ppermute | solution.py:173
  238.0 15.2 %collective-permute-start.77 = (f32[96,768]{1,0:T(8,128)S(1)}, f32[96,768]{1,0:T(8,128)S(1)}, u32[]{:S(2)}, u32[]{:S(2)}) collective-permute-start(f32[96,768]{1,0:T(8,128)S(1)} %collective-permute-done.75.refs_10_), channel_id=1, source_target_pairs={{0,8},{8,16},{16,24},{24,28},{28,20},{20,12},{12,4},{4,0},{1,9},{9... | collective-permute-start | bytes 884744 | tf_op jit(solution)/shard_map/ppermute | solution.py:173
  238.9 15.4 %collective-permute-start.78 = (f32[96,768]{1,0:T(8,128)S(1)}, f32[96,768]{1,0:T(8,128)S(1)}, u32[]{:S(2)}, u32[]{:S(2)}) collective-permute-start(f32[96,768]{1,0:T(8,128)S(1)} %collective-permute-done.76.refs_11_), channel_id=1, source_target_pairs={{0,4},{8,0},{16,8},{24,16},{28,24},{20,28},{12,20},{4,12},{1,5},{9... | collective-permute-start | bytes 884744 | tf_op jit(solution)/shard_map/ppermute | solution.py:173
  253.3 11.9 %collective-permute-start.79 = (f32[96,768]{1,0:T(8,128)S(1)}, f32[96,768]{1,0:T(8,128)S(1)}, u32[]{:S(2)}, u32[]{:S(2)}) collective-permute-start(f32[96,768]{1,0:T(8,128)S(1)} %collective-permute-done.77.refs_12_), channel_id=1, source_target_pairs={{0,8},{8,16},{16,24},{24,28},{28,20},{20,12},{12,4},{4,0},{1,9},{9... | collective-permute-start | bytes 884744 | tf_op jit(solution)/shard_map/ppermute | solution.py:173
  254.2 11.0 %collective-permute-start.80 = (f32[96,768]{1,0:T(8,128)S(1)}, f32[96,768]{1,0:T(8,128)S(1)}, u32[]{:S(2)}, u32[]{:S(2)}) collective-permute-start(f32[96,768]{1,0:T(8,128)S(1)} %collective-permute-done.78.refs_13_), channel_id=1, source_target_pairs={{0,4},{8,0},{16,8},{24,16},{28,24},{20,28},{12,20},{4,12},{1,5},{9... | collective-permute-start | bytes 884744 | tf_op jit(solution)/shard_map/ppermute | solution.py:173
  (113 other events, 1194.0 us)

commit v4 on v3

--- a/solution.py
+++ b/solution.py
@@ -92,9 +92,11 @@
     return jnp.concatenate(natural(blocks), axis=1)
 
 
-def place_kernel(steps, first, targets, outs, spots_ref, *refs):
+def place_kernel(steps, size, first, targets, outs, kept, spots_ref, *refs):
     count = len(targets)
-    pieces, out_refs, sems = refs[: steps * count], refs[steps * count : steps * count + outs], refs[-1]
+    pieces = refs[: steps * count]
+    out_refs = refs[steps * count + kept : steps * count + kept + outs]
+    token_ref, sems = refs[-2], refs[-1]
     copies = []
     filled = [0] * outs
     for entry, runs in enumerate(targets):
@@ -112,25 +114,30 @@
                     )
                 )
             at += rows
-            filled[out] += rows * steps
+            filled[out] += rows * size
     for copy in copies:
         copy.start()
+    token_ref[...] = jnp.zeros(token_ref.shape, F32)
     for copy in copies:
         copy.wait()
 
 
-def place_rows(pieces, table, first, targets, shapes):
+def place_rows(pieces, size, table, first, targets, shapes, filled=()):
     steps = len(pieces)
     copies = steps * sum(len(runs) for runs in targets)
-    return pl.pallas_call(
-        functools.partial(place_kernel, steps, first, targets, len(shapes)),
-        out_shape=[jax.ShapeDtypeStruct(shape, F32) for shape in shapes],
-        in_specs=[IN_SMEM] + [IN_VMEM] * (steps * len(targets)),
-        out_specs=[pl.BlockSpec(memory_space=pl.ANY)] * len(shapes),
+    operands = [piece for step in pieces for piece in step]
+    anywhere = pl.BlockSpec(memory_space=pl.ANY)
+    *outs, token = pl.pallas_call(
+        functools.partial(place_kernel, steps, size, first, targets, len(shapes), len(filled)),
+        out_shape=[jax.ShapeDtypeStruct(shape, F32) for shape in (*shapes, (8, 128))],
+        in_specs=[IN_SMEM] + [IN_VMEM] * len(operands) + [anywhere] * len(filled),
+        out_specs=[anywhere] * len(shapes) + [IN_VMEM],
         scratch_shapes=[pltpu.SemaphoreType.DMA((copies,))],
+        input_output_aliases={1 + len(operands) + at: at for at in range(len(filled))},
         compiler_params=pltpu.CompilerParams(vmem_limit_bytes=SMALL_LIMIT),
         cost_estimate=QUICK,
-    )(table, *(piece for step in pieces for piece in step))
+    )(table, *operands, *filled)
+    return outs, token
 
 
 def add_kernel(step, spots_ref, *refs):
@@ -179,10 +186,19 @@
             self.pieces.append(self.moving)
         return self.moving[0]
 
-    def finish(self, targets, shapes):
-        while self.count < 2 * self.size - 2:
+    def finish(self, targets, shapes, gate=None):
+        steps = 2 * self.size - 2
+        while self.count < steps - 2:
             self.step()
-        return place_rows(self.pieces, self.table, self.size - 1, targets, shapes)
+        early = len(self.pieces)
+        outs, token = place_rows(self.pieces, self.size, self.table, self.size - 1, targets, shapes)
+        self.step(token)
+        if gate is not None:
+            self.moving = after(self.moving, gate)
+        self.step()
+        return place_rows(
+            self.pieces[early:], self.size, self.table, self.size - 1 + early, targets, shapes, outs
+        )
 
 
 class Plain:
@@ -192,7 +208,7 @@
     def step(self, gate=None):
         return self.parts[0]
 
-    def finish(self, targets, shapes):
+    def finish(self, targets, shapes, gate=None):
         outs = [[] for shape in shapes]
         for part, runs in zip(lax.psum(self.parts, "dp"), targets):
             at = 0
@@ -200,7 +216,7 @@
                 rows = part.shape[0] * share[0] // share[1]
                 outs[out].append(part[at : at + rows])
                 at += rows
-        return [jnp.concatenate(rows, axis=0) for rows in outs]
+        return [jnp.concatenate(rows, axis=0) for rows in outs], None
 
 
 def whole_blocks(heights, size):
@@ -260,31 +276,27 @@
     d_values_ref,
     attended_ref,
     d_attn_ref,
-    bias_ref,
     upper_ref,
     lower_ref,
     upper_first_ref,
     lower_first_ref,
+    bias_ref,
 ):
     feats = d_queries_ref.shape[1]
-    width = heads_in_ref.shape[1]
     heads_in = heads_in_ref[...]
     upper_ref[0:feats, :] = over_tokens(d_queries_ref[...], heads_in)
     upper_ref[feats : 2 * feats, :] = over_tokens(d_keys_ref[...], heads_in)
     values_part = over_tokens(d_values_ref[...], heads_in)
     mixing_part = over_tokens(attended_ref[...].astype(BF16), d_attn_ref[...])
     run = feats // blocks
-    extra = lower_ref.shape[0] // blocks - 2 * run
     for at in range(blocks):
-        base = at * (2 * run + extra)
+        base = at * 2 * run
         lower_ref[base : base + run, :] = values_part[at * run : (at + 1) * run]
         lower_ref[base + run : base + 2 * run, :] = mixing_part[at * run : (at + 1) * run]
-        lower_ref[base + 2 * run : base + 2 * run + extra, :] = jnp.zeros((extra, width), F32)
-    base = 2 * run
-    lower_ref[base : base + 2, :] = bias_ref[...]
-    lower_ref[base + 2 : base + 3, :] = column_sums(d_attn_ref[...])
-    lower_ref[base + 3 : base + 4, 0:feats] = column_sums(d_queries_ref[...])
-    lower_ref[base + 4 : base + 5, 0:feats] = column_sums(d_values_ref[...])
+    bias_ref[...] = jnp.zeros(bias_ref.shape, F32)
+    bias_ref[0:1, :] = column_sums(d_attn_ref[...])
+    bias_ref[1:2, 0:feats] = column_sums(d_queries_ref[...])
+    bias_ref[2:3, 0:feats] = column_sums(d_values_ref[...])
     copy_block(spots_ref, 0, upper_ref, upper_first_ref)
     copy_block(spots_ref, 1, lower_ref, lower_first_ref)
 
@@ -351,8 +363,8 @@
     ]
 
 
-def widen_kernel(values_ref, behind_ref, out_ref):
-    out_ref[...] = values_ref[...].astype(F32)
+def widen_kernel(first, values_ref, behind_ref, out_ref):
+    out_ref[...] = values_ref[first : first + out_ref.shape[0], :].astype(F32)
 
 
 def cotangent_kernel(cotangent_ref, gate_ref, down_ref, d_mlp_ref, d_act_ref):
@@ -368,10 +380,14 @@
     beside_ref,
     across_ref,
     corner_ref,
-    mixing_own_ref,
-    mixing_beside_ref,
-    mixing_across_ref,
-    mixing_corner_ref,
+    mixing_0_ref,
+    mixing_1_ref,
+    mixing_2_ref,
+    mixing_3_ref,
+    mixing_4_ref,
+    mixing_5_ref,
+    mixing_6_ref,
+    mixing_7_ref,
     mixing_bias_ref,
     hidden_ref,
     gate_ref,
@@ -392,7 +408,15 @@
     blocks = (own_ref, beside_ref, across_ref, corner_ref)
     mixing = in_order(
         odd_ref,
-        [ref[...].astype(BF16) for ref in (mixing_own_ref, mixing_beside_ref, mixing_across_ref, mixing_corner_ref)],
+        [
+            jnp.concatenate([top[...].astype(BF16), low[...].astype(BF16)], axis=0)
+            for top, low in (
+                (mixing_0_ref, mixing_1_ref),
+                (mixing_2_ref, mixing_3_ref),
+                (mixing_4_ref, mixing_5_ref),
+                (mixing_6_ref, mixing_7_ref),
+            )
+        ],
     )
     for at, rows in enumerate(latent_rows(hidden_ref)):
         attn_out = mixing_bias_ref[...].astype(F32)
@@ -549,8 +573,32 @@
     out_ref[...] = left_ref[...] + right_ref[...]
 
 
-def modulation_grad_kernel(mods_ref, silu_ref, weight_ref, weight_grad_ref, bias_grad_ref, silu_grad_ref):
-    mods = mods_ref[...].astype(BF16)
+def pack_kernel(
+    flags_ref, shift_one, scale_one, gate_one, shift_two, scale_two, gate_two, mlp_bias_ref, heads_bias_ref, out_ref, all_ref
+):
+    latents, width = shift_one.shape
+    columns = out_ref.shape[1]
+    for at, ref in enumerate((shift_one, scale_one, gate_one, shift_two, scale_two, gate_two)):
+        all_ref[:, at * width : (at + 1) * width] = ref[...]
+    start = pl.multiple_of((flags_ref[0] + 2 * flags_ref[1]) * columns, 128)
+    out_ref[...] = jnp.zeros(out_ref.shape, F32)
+    out_ref[0:latents, :] = all_ref[:, pl.ds(start, columns)]
+    out_ref[latents : latents + 2, 0:width] = mlp_bias_ref[...]
+    out_ref[latents + 2 : latents + 5, 0:width] = heads_bias_ref[...]
+
+
+def modulation_grad_kernel(
+    latents, carried_ref, silu_ref, weight_ref, weight_grad_ref, bias_grad_ref, silu_grad_ref, bias_sum_ref
+):
+    groups = silu_ref.shape[0] // latents
+    height = carried_ref.shape[0] // groups
+    mods = jnp.concatenate(
+        [carried_ref[at * height : at * height + latents, :] for at in range(groups)], axis=0
+    ).astype(BF16)
+    total = carried_ref[latents : latents + 5, :]
+    for at in range(1, groups):
+        total = total + carried_ref[at * height + latents : at * height + latents + 5, :]
+    bias_sum_ref[...] = total
     weight_grad_ref[...] = lax.dot_general(
         silu_ref[...], mods, (((0,), (0,)), ((), ())), preferred_element_type=F32
     )
@@ -617,13 +665,17 @@
     per_latent = jax.ShapeDtypeStruct((own_latents, model_width), F32)
     add = lambda left, right: call(sum_kernel, halves, (left, right), scalars=0, limit=SMALL_LIMIT)
 
-    mixing_own = call(
-        widen_kernel,
-        jax.ShapeDtypeStruct(mixing_weight.shape, F32),
-        (mixing_weight, gate_two),
-        scalars=0,
-        limit=SMALL_LIMIT,
-    )
+    mixing_half = own_feats // 2
+    mixing_own = [
+        call(
+            functools.partial(widen_kernel, first),
+            jax.ShapeDtypeStruct((mixing_half, model_width), F32),
+            (mixing_weight, behind),
+            scalars=0,
+            limit=SMALL_LIMIT,
+        )
+        for first, behind in ((0, cond_part), (mixing_half, gate_two))
+    ]
     bias_rows = [bias.reshape(1, bias.shape[0]) for bias in (mixing_bias, up_bias, down_bias)]
     heads_rows = heads_weight.transpose(1, 2, 0).reshape(3 * own_feats, model_width)
     heads_in, queries, key_rows, value_rows, attended = call(
@@ -632,7 +684,7 @@
         (table, flags, *bias_rows, hidden_in, scale_one, shift_one, heads_rows, heads_bias),
         scalars=2,
     )
-    mixing_far = swap(mixing_own, tensor_size, 2)
+    mixing_far = [swap(rows, tensor_size, 2) for rows in mixing_own]
     attended_across = swap(attended, tensor_size, 2)
     attended_beside = swap(attended, tensor_size, 1)
     d_mlp, d_act = call(
@@ -644,10 +696,10 @@
     attended_across = after(attended_across, d_act)
     mixing_across = after(mixing_far, attended_across)
     mixing_blocks = (
-        mixing_own,
-        swap(mixing_own, tensor_size, 1),
-        mixing_across,
-        swap(mixing_across, tensor_size, 1),
+        *mixing_own,
+        *(swap(rows, tensor_size, 1) for rows in mixing_own),
+        *mixing_across,
+        *(swap(rows, tensor_size, 1) for rows in mixing_across),
     )
     attn_out, mlp_in, activated, d_pre, mine, theirs = call(
         mlp_kernel,
@@ -731,16 +783,17 @@
 
     d_queries, d_keys, d_values = after((d_queries, d_keys, d_values), chip_one)
     blocks = dp_size if rings else 1
-    upper_rows, lower_rows = 2 * own_feats, 2 * own_feats + 8 * dp_size
-    upper_part, lower_part, upper_first, lower_first = call(
+    upper_rows, lower_rows = 2 * own_feats, 2 * own_feats
+    upper_part, lower_part, upper_first, lower_first, heads_bias_part = call(
         functools.partial(attention_grads_kernel, blocks),
         (
             jax.ShapeDtypeStruct((upper_rows, model_width), F32),
             jax.ShapeDtypeStruct((lower_rows, model_width), F32),
             jax.ShapeDtypeStruct((upper_rows // dp_size, model_width), F32),
             jax.ShapeDtypeStruct((lower_rows // dp_size, model_width), F32),
+            jax.ShapeDtypeStruct((3, model_width), F32),
         ),
-        (table, heads_in, d_queries, d_keys, d_values, attended, d_attn, mlp_bias),
+        (table, heads_in, d_queries, d_keys, d_values, attended, d_attn),
     )
     heads_ring = start_sum((upper_part, lower_part), (upper_first, lower_first), ways, dp_size, table, rings)
     block_out, d_gate_two = call(
@@ -768,44 +821,59 @@
         (
             flags,
             full_one,
-            after(swap(full_one, tensor_size, 1), heads_ring.step(full_one)),
+            swap(full_one, tensor_size, 1),
             hidden_in,
             d_middle,
             scale_one,
         ),
         scratch=[pltpu.VMEM((tok_rows, model_width), F32)],
     )
-    d_modulation = jnp.concatenate(
-        [d_shift_one, d_scale_one, d_gate_one, d_shift_two, d_scale_two, d_gate_two], axis=1
-    )
     own_cols = modulation_weight.shape[1]
-    own_mods = lax.dynamic_slice_in_dim(d_modulation, lax.axis_index("tensor") * own_cols, own_cols, 1)
+    carried = -(-(own_latents + 5) // 8) * 8
+    own_mods = call(
+        pack_kernel,
+        jax.ShapeDtypeStruct((carried, own_cols), F32),
+        (
+            flags,
+            d_shift_one,
+            d_scale_one,
+            d_gate_one,
+            d_shift_two,
+            d_scale_two,
+            d_gate_two,
+            mlp_bias,
+            heads_bias_part,
+        ),
+        scratch=[pltpu.VMEM((own_latents, 6 * model_width), F32)],
+        limit=SMALL_LIMIT,
+    )
     mlp_ring.step(own_mods)
     heads_ring.step(own_mods)
     whole = (1, 1)
-    up_weight_sum, down_weight_sum = mlp_ring.finish(
-        (((whole, 0),), ((whole, 1),)), (up_part.shape, down_part.shape)
-    )
-    run = (own_feats, lower_rows)
-    heads_sum, mixing_weight_sum, bias_sum = heads_ring.finish(
-        (((whole, 0),), ((run, 0), (run, 1), ((8 * dp_size, lower_rows), 2))),
-        ((3 * own_feats, model_width), (own_feats, model_width), (8 * dp_size, model_width)),
+    run = (1, 2)
+    (heads_sum, mixing_weight_sum), placed = heads_ring.finish(
+        (((whole, 0),), ((run, 0), (run, 1))),
+        ((3 * own_feats, model_width), (own_feats, model_width)),
+    )
+    (up_weight_sum, down_weight_sum), placed = mlp_ring.finish(
+        (((whole, 0),), ((whole, 1),)), (up_part.shape, down_part.shape), placed
     )
     heads_weight_sum = heads_sum.reshape(3, own_feats, model_width).transpose(2, 0, 1)
-    up_bias_sum, down_bias_sum, mixing_bias_sum = (bias_sum[row] for row in range(3))
-    heads_bias_sum = bias_sum[3:5, :own_feats]
     all_mods = gather_latents(own_mods, dp_size)
-    mod_weight_sum, mod_bias_row, d_silu_part = call(
-        modulation_grad_kernel,
+    mod_weight_sum, mod_bias_row, d_silu_part, bias_sum = call(
+        functools.partial(modulation_grad_kernel, own_latents),
         (
             jax.ShapeDtypeStruct((model_width, own_cols), F32),
             jax.ShapeDtypeStruct((1, own_cols), F32),
-            jax.ShapeDtypeStruct((all_mods.shape[0], model_width), F32),
+            jax.ShapeDtypeStruct((silu_all.shape[0], model_width), F32),
+            jax.ShapeDtypeStruct((5, own_cols), F32),
         ),
         (all_mods, silu_all, modulation_weight),
         scalars=0,
     )
     mod_bias_sum = mod_bias_row.reshape(own_cols)
+    up_bias_sum, down_bias_sum, mixing_bias_sum = (bias_sum[row, :model_width] for row in range(3))
+    heads_bias_sum = bias_sum[3:5, :own_feats]
     d_silu_own = scatter_features(d_silu_part, tensor_size)
     sigmoid_part = jax.nn.sigmoid(cond_part)
     d_condition = d_silu_own * sigmoid_part * (1.0 + cond_part * (1.0 - sigmoid_part))

time: 269 us -> 255 us (0.948)
  waiting for transfers between devices: 117 us -> 103 us
  local copies, waits for them, and re-layouts: 13.9 us -> 7.3 us
  starting transfers between devices: 75.1 us -> 79.2 us
  Pallas kernels: 51 us -> 53.8 us
    ppermute x56, waiting for transfers between devices: 72.9 us -> 63.8 us  [step(): lax.ppermute(held, 'dp', perm)]
    unnamed x127 -> x48, local copies, waits for them, and re-layouts: 12 us -> 5.07 us
    pallas_call x2 -> x4, Pallas kernels: 6.09 us -> 11.3 us  [place_rows(): pl.pallas_call(functools.partial(place_kernel, steps, size, first, target...]
    ppermute x24 -> x27, waiting for transfers between devices: 39.2 us -> 35.6 us  [swap(): lax.ppermute(values, 'tensor', [(at, at ^ bit) for at in range(size)])]
    ppermute x24 -> x27, starting transfers between devices: 12.6 us -> 15.6 us  [swap(): lax.ppermute(values, 'tensor', [(at, at ^ bit) for at in range(size)])]
    pallas_call x31 -> x33, Pallas kernels: 45 us -> 42.5 us  [call(): pl.pallas_call(kernel, out_shape=out_shape, in_specs=[IN_SMEM] * scalars...]
  transfers between devices with their start and end apart: 84 -> 87, of which waited for: 39 -> 37; matrix products, arithmetic and copies ran while one was open for 3% -> 4% of each run, Pallas kernels for 14% -> 17%
where the time goes in v4:
time: 255 us; the launch traced here: 254 us
  waiting for transfers between devices  103 us (40%)
  starting transfers between devices  79.2 us (31%)
  Pallas kernels  53.8 us (21%)
  local copies, waits for them, and re-layouts  7.3 us (3%)
  matrix products  5.93 us (2%)
  other arithmetic  3.66 us (1%)
    ppermute x56, waiting for transfers between devices, step(): lax.ppermute(held, 'dp', perm)  63.8 us
    ppermute x56, starting transfers between devices, step(): lax.ppermute(held, 'dp', perm)  57.5 us
    pallas_call x33, Pallas kernels, call(): pl.pallas_call(kernel, out_shape=out_shape, in_specs=[IN_SMEM] * scalars...  42.5 us
    ppermute x27, waiting for transfers between devices, swap(): lax.ppermute(values, 'tensor', [(at, at ^ bit) for at in range(size)])  35.6 us
    ppermute x27, starting transfers between devices, swap(): lax.ppermute(values, 'tensor', [(at, at ^ bit) for at in range(size)])  15.6 us
    pallas_call x4, Pallas kernels, place_rows(): pl.pallas_call(functools.partial(place_kernel, steps, size, first, target...  11.3 us
    ppermute x3, starting transfers between devices, gather_latents(): lax.ppermute(pair, 'dp', [(at, (at + step) % size) for at in range(size)])  5.61 us
  transfers between devices with their start and end apart: 87, of which 37 were waited for; matrix products, arithmetic and copies ran while one was open for 4% of the time, Pallas kernels for 17%

profile of v4, /device:TPU:0, one launch (start us, length us, event | category | flops | bytes accessed | tf_op | source)
XLA Modules:
  0.0 254.4 jit_solution(11256887637566051989)
XLA Ops:
  4.2 2.6 %collective-permute-start.1 = (f32[16,192]{1,0:T(8,128)S(1)}, f32[16,192]{1,0:T(8,128)S(1)}, u32[]{:S(2)}, u32[]{:S(2)}) collective-permute-start(f32[16,192]{1,0:T(8,128)S(1)} %convolution_add_fusion.1.behind_ref), channel_id=1, source_target_pairs={{0,2},{1,3},{2,0},{3,1},{4,6},{5,7},{6,4},{7,5},{8,10},{9,11},{10,... | collective-permute-start | bytes 36872 | tf_op jit(solution)/shard_map/ppermute | solution.py:18
  13.6 3.9 %collective-permute-done.4 = f32[2,1152]{1,0:T(2,128)S(1)} collective-permute-done((f32[2,1152]{1,0:T(2,128)S(1)}, f32[2,1152]{1,0:T(2,128)S(1)}, u32[]{:S(2)}, u32[]{:S(2)}) %collective-permute-start.4) | collective-permute-done | bytes 9248 | tf_op jit(solution)/shard_map/ppermute | solution.py:18
  17.6 3.7 %shard_map.272 = (bf16[512,768]{1,0:T(8,128)(2,1)S(1)}, bf16[512,192]{1,0:T(8,128)(2,1)S(1)}, bf16[512,192]{1,0:T(8,128)(2,1)S(1)}, bf16[512,192]{1,0:T(8,128)(2,1)S(1)}, f32[512,192]{1,0:T(8,128)S(1)}) custom-call(s32[15,2]{1,0:T(8,128)S(1)} %add_select_fusion.table_ref.spots_ref, s32[2]{0:T(128)S(1)} %pad_add_fusion.flags_ref.odd_ref, ...), custom_call_target="tpu_custom_call" | custom-call | flops 1 | bytes 1 | tf_op jit(solution)/shard_map/pallas_call | solution.py:66
  24.8 11.3 %collective-permute-done.7.across_ref = f32[512,192]{1,0:T(8,128)S(1)} collective-permute-done((f32[512,192]{1,0:T(8,128)S(1)}, f32[512,192]{1,0:T(8,128)S(1)}, u32[]{:S(2)}, u32[]{:S(2)}) %collective-permute-start.7) | collective-permute-done | bytes 393248 | tf_op jit(solution)/shard_map/ppermute | solution.py:18
  36.6 5.0 %collective-permute-done.12.mixing_5_ref = f32[96,768]{1,0:T(8,128)S(1)} collective-permute-done((f32[96,768]{1,0:T(8,128)S(1)}, f32[96,768]{1,0:T(8,128)S(1)}, u32[]{:S(2)}, u32[]{:S(2)}) %collective-permute-start.12) | collective-permute-done | bytes 294944 | tf_op jit(solution)/shard_map/ppermute | solution.py:18
  43.6 5.2 %shard_map.276 = (f32[512,768]{1,0:T(8,128)S(1)}, bf16[512,768]{1,0:T(8,128)(2,1)S(1)}, bf16[512,768]{1,0:T(8,128)(2,1)S(1)}, bf16[512,768]{1,0:T(8,128)(2,1)S(1...) custom-call(s32[2]{0:T(128)S(1)} %pad_add_fusion.flags_ref.odd_ref, ...), custom_call_target="tpu_custom_call" | custom-call | flops 1 | bytes 1 | tf_op jit(solution)/shard_map/pallas_call | solution.py:66
  48.9 2.2 collective-permute-done.15.right_ref
  51.2 2.9 %shard_map.278 = (f32[768,768]{1,0:T(8,128)S(1)}, f32[768,768]{1,0:T(8,128)S(1)}, f32[2,768]{1,0:T(2,128)S(1)}, f32[96,768]{1,0:T(8,128)S(1)}, f32[96,768]{1,0:T...) custom-call(s32[15,2]{1,0:T(8,128)S(1)} %add_select_fusion.table_ref.spots_ref, ...), custom_call_target="tpu_custom_call" | custom-call | flops 1 | bytes 1 | tf_op jit(solution)/shard_map/pallas_call | solution.py:66
  58.1 7.0 %collective-permute-done.18.refs_0_ = f32[96,768]{1,0:T(8,128)S(1)} collective-permute-done((f32[96,768]{1,0:T(8,128)S(1)}, f32[96,768]{1,0:T(8,128)S(1)}, u32[]{:S(2)}, u32[]{:S(2)}) %collective-permute-start.18) | collective-permute-done | bytes 294944 | tf_op jit(solution)/shard_map/ppermute | solution.py:180
  69.2 5.8 %collective-permute-done.20.refs_0_ = f32[96,768]{1,0:T(8,128)S(1)} collective-permute-done((f32[96,768]{1,0:T(8,128)S(1)}, f32[96,768]{1,0:T(8,128)S(1)}, u32[]{:S(2)}, u32[]{:S(2)}) %collective-permute-start.20) | collective-permute-done | bytes 294944 | tf_op jit(solution)/shard_map/ppermute | solution.py:180
  80.0 2.1 shard_map.284
  82.1 4.7 %collective-permute-done.26.refs_1_ = f32[96,768]{1,0:T(8,128)S(1)} collective-permute-done((f32[96,768]{1,0:T(8,128)S(1)}, f32[96,768]{1,0:T(8,128)S(1)}, u32[]{:S(2)}, u32[]{:S(2)}) %collective-permute-start.26) | collective-permute-done | bytes 294944 | tf_op jit(solution)/shard_map/ppermute | solution.py:180
  87.7 5.2 %shard_map.286 = (bf16[512,192]{1,0:T(8,128)(2,1)S(1)}, bf16[512,192]{1,0:T(8,128)(2,1)S(1)}, bf16[512,192]{1,0:T(8,128)(2,1)S(1)}, f32[256,768]{1,0:T(8,128)S(1)}, f32[256,768]{1,0:T(8,128)S(1)}) custom-call(s32[2]{0:T(128)S(1)} %pad_add_fusion.flags_ref.odd_ref, bf16[512,768]{1,0:T(8,128)(2,1)S(1)} %get-tuple-element.162.d_attn_ref, ...), custom_call_target="tpu_custom_call" | custom-call | flops 1 | bytes 1 | tf_op jit(solution)/shard_map/pallas_call | solution.py:66
  95.1 3.7 %collective-permute-done.22.right_ref = f32[256,768]{1,0:T(8,128)S(1)} collective-permute-done((f32[256,768]{1,0:T(8,128)S(1)}, f32[256,768]{1,0:T(8,128)S(1)}, u32[]{:S(2)}, u32[]{:S(2)}) %collective-permute-start.22) | collective-permute-done | bytes 786464 | tf_op jit(solution)/shard_map/ppermute | solution.py:18
  98.9 3.5 %collective-permute-done.29.refs_1_ = f32[96,768]{1,0:T(8,128)S(1)} collective-permute-done((f32[96,768]{1,0:T(8,128)S(1)}, f32[96,768]{1,0:T(8,128)S(1)}, u32[]{:S(2)}, u32[]{:S(2)}) %collective-permute-start.29) | collective-permute-done | bytes 294944 | tf_op jit(solution)/shard_map/ppermute | solution.py:180
  110.1 2.3 shard_map.290
  112.5 3.1 %collective-permute-done.34.refs_1_ = f32[48,768]{1,0:T(8,128)S(1)} collective-permute-done((f32[48,768]{1,0:T(8,128)S(1)}, f32[48,768]{1,0:T(8,128)S(1)}, u32[]{:S(2)}, u32[]{:S(2)}) %collective-permute-start.34) | collective-permute-done | bytes 147488 | tf_op jit(solution)/shard_map/ppermute | solution.py:180
  118.3 4.1 %collective-permute-done.30.right_ref = f32[256,768]{1,0:T(8,128)S(1)} collective-permute-done((f32[256,768]{1,0:T(8,128)S(1)}, f32[256,768]{1,0:T(8,128)S(1)}, u32[]{:S(2)}, u32[]{:S(2)}) %collective-permute-start.30) | collective-permute-done | bytes 786464 | tf_op jit(solution)/shard_map/ppermute | solution.py:18
  126.7 3.0 %shard_map.294 = (f32[512,768]{1,0:T(8,128)}, f32[2,768]{1,0:T(2,128)S(1)}, f32[2,768]{1,0:T(2,128)S(1)}) custom-call(s32[2]{0:T(128)S(1)} %pad_add_fusion.flags_ref.odd_ref, f32[256,768]{1,0:T(8,128)S(1)} %shard_map.293.full_ref, f32[256,768]{1,0:T(8,128)S(1)} %collective-permute-done.35.other_ref, bf16[512,768]{1,0:T(8,128)(2,1)S(1)} %copy-done.2, ...), custom_call_target="tpu_custom_call" | custom-call | flops 1 | bytes 1 | tf_op jit(solution)/shard_map/pallas_call | solution.py:66
  130.2 2.2 collective-permute-done.67.refs_1_
  139.6 6.3 %collective-permute-done.42.refs_0_ = f32[48,768]{1,0:T(8,128)S(1)} collective-permute-done((f32[48,768]{1,0:T(8,128)S(1)}, f32[48,768]{1,0:T(8,128)S(1)}, u32[]{:S(2)}, u32[]{:S(2)}) %collective-permute-start.42) | collective-permute-done | bytes 147488 | tf_op jit(solution)/shard_map/ppermute | solution.py:180
  158.8 2.9 %collective-permute-done.46.refs_0_ = f32[48,768]{1,0:T(8,128)S(1)} collective-permute-done((f32[48,768]{1,0:T(8,128)}, f32[48,768]{1,0:T(8,128)S(1)}, u32[]{:S(2)}, u32[]{:S(2)}) %collective-permute-start.46) | collective-permute-done | bytes 147488 | tf_op jit(solution)/shard_map/ppermute | solution.py:180
  170.1 2.2 collective-permute-done.49.refs_1_
  186.6 3.7 %collective-permute-done.37 = f32[16,1152]{1,0:T(8,128)} collective-permute-done((f32[16,1152]{1,0:T(8,128)}, f32[16,1152]{1,0:T(8,128)}, u32[]{:S(2)}, u32[]{:S(2)}) %collective-permute-start.37) | collective-permute-done | bytes 73760 | tf_op jit(solution)/shard_map/ppermute | solution.py:39
  193.3 3.0 %collective-permute-start.39 = (f32[16,1152]{1,0:T(8,128)}, f32[16,1152]{1,0:T(8,128)S(1)}, u32[]{:S(2)}, u32[]{:S(2)}) collective-permute-start(f32[16,1152]{1,0:T(8,128)} %get-tuple-element.247), channel_id=1, source_target_pairs={{0,24},{4,28},{8,0},{12,4},{16,8},{20,12},{24,16},{28,20},{1,25},{... | collective-permute-start | bytes 221192 | tf_op jit(solution)/shard_map/ppermute | solution.py:39
  198.4 4.2 %collective-permute-done.53.refs_4_ = f32[48,768]{1,0:T(8,128)S(1)} collective-permute-done((f32[48,768]{1,0:T(8,128)S(1)}, f32[48,768]{1,0:T(8,128)S(1)}, u32[]{:S(2)}, u32[]{:S(2)}) %collective-permute-start.53) | collective-permute-done | bytes 147488 | tf_op jit(solution)/shard_map/ppermute | solution.py:180
  208.4 2.6 %shard_map.296 = (f32[768,1152]{1,0:T(8,128)}, f32[1,1152]{1,0:T(1,128)S(1)}, f32[16,768]{1,0:T(8,128)S(1)}, f32[5,1152]{1,0:T(8,128)S(1)}) custom-call(f32[64,1152]{1,0:T(8,128)S(1)} %constant_dynamic-update-slice_fusion.carried_ref, bf16[16,768]{1,0:T(8,128)(2,1)S(1)} %multiply_convert_fusion.silu_ref, bf16[768,1152]{1,0:T(8,128)(2,1)S(1)} %copy-done.4), custom_call_target="tpu_custom_call" | custom-call | flops 1 | bytes 1 | tf_op jit(solution)/shard_map/pallas_call | solution.py:66
  214.8 2.8 %collective-permute-done.86 = f32[16,192]{1,0:T(8,128)} collective-permute-done((f32[16,192]{1,0:T(8,128)S(1)}, f32[16,192]{1,0:T(8,128)}, u32[]{:S(2)}, u32[]{:S(2)}) %collective-permute-start.86) | collective-permute-done | bytes 12320 | tf_op jit(solution)/shard_map/ppermute | solution.py:18
  225.1 5.3 %collective-permute-done.56.refs_10_ = f32[48,768]{1,0:T(8,128)S(1)} collective-permute-done((f32[48,768]{1,0:T(8,128)S(1)}, f32[48,768]{1,0:T(8,128)S(1)}, u32[]{:S(2)}, u32[]{:S(2)}) %collective-permute-start.56) | collective-permute-done | bytes 147488 | tf_op jit(solution)/shard_map/ppermute | solution.py:180
  242.5 3.0 %shard_map.303 = (f32[576,768]{1,0:T(8,128)}, f32[192,768]{1,0:T(8,128)}, f32[8,128]{1,0:T(8,128)}) custom-call(s32[15,2]{1,0:T(8,128)S(1)} %add_select_fusion.table_ref.spots_ref, f32[48,768]{1,0:T(8,128)S(1)} %get-tuple-element.219.refs_0_, f32[48,768]{1,0:T(8,128)S(1)} %copy-done.14, f32[48,768]{1,0:T(8,128)S(1)} %collective-permute-done.52.refs_2_, ...), custom_call_target="tpu_custom_call" | custom-call | flops 1 | bytes 1 | tf_op jit(solution)/shard_map/pallas_call | solution.py:130
  248.0 3.8 %shard_map.307 = (f32[768,768]{1,0:T(8,128)}, f32[768,768]{1,0:T(8,128)}, f32[8,128]{1,0:T(8,128)}) custom-call(s32[15,2]{1,0:T(8,128)S(1)} %add_select_fusion.table_ref.spots_ref, f32[96,768]{1,0:T(8,128)S(1)} %get-tuple-element.233.refs_0_, f32[96,768]{1,0:T(8,128)S(1)} %get-tuple-element.234.refs_1_, f32[96,768]{1,0:T(8,128)S(1)} %copy-done.12, ...), custom_call_target="tpu_custom_call" | custom-call | flops 1 | bytes 1 | tf_op jit(solution)/shard_map/pallas_call | solution.py:130
  251.9 2.3 shard_map.308
  (254 shorter events, 127.6 us)
Async XLA Ops:
  7.9 28.2 %collective-permute-start.11 = (f32[96,768]{1,0:T(8,128)S(1)}, f32[96,768]{1,0:T(8,128)S(1)}, u32[]{:S(2)}, u32[]{:S(2)}) collective-permute-start(f32[96,768]{1,0:T(8,128)S(1)} %shard_map.274.mixing_0_ref), channel_id=1, source_target_pairs={{0,2},{1,3},{2,0},{3,1},{4,6},{5,7},{6,4},{7,5},{8,10},{9,11},{10,... | collective-permute-start | bytes 884744 | tf_op jit(solution)/shard_map/ppermute | solution.py:18
  21.2 14.8 %collective-permute-start.7 = (f32[512,192]{1,0:T(8,128)S(1)}, f32[512,192]{1,0:T(8,128)S(1)}, u32[]{:S(2)}, u32[]{:S(2)}) collective-permute-start(f32[512,192]{1,0:T(8,128)S(1)} %get-tuple-element.129.own_ref.attended_ref), channel_id=1, source_target_pairs={{0,2},{1,3},{2,0},{3,1},{4,6},{5,7},{6,4},{7,5},{8,10},{9,11},{10,... | collective-permute-start | bytes 1179656 | tf_op jit(solution)/shard_map/ppermute | solution.py:18
  23.1 18.5 %collective-permute-start.12 = (f32[96,768]{1,0:T(8,128)S(1)}, f32[96,768]{1,0:T(8,128)S(1)}, u32[]{:S(2)}, u32[]{:S(2)}) collective-permute-start(f32[96,768]{1,0:T(8,128)S(1)} %shard_map.275.mixing_1_ref), channel_id=1, source_target_pairs={{0,2},{1,3},{2,0},{3,1},{4,6},{5,7},{6,4},{7,5},{8,10},{9,11},{10,... | collective-permute-start | bytes 884744 | tf_op jit(solution)/shard_map/ppermute | solution.py:18
  23.4 18.1 %collective-permute-start.9 = (f32[96,768]{1,0:T(8,128)S(1)}, f32[96,768]{1,0:T(8,128)S(1)}, u32[]{:S(2)}, u32[]{:S(2)}) collective-permute-start(f32[96,768]{1,0:T(8,128)S(1)} %shard_map.274.mixing_0_ref), channel_id=1, source_target_pairs={{0,1},{1,0},{2,3},{3,2},{4,5},{5,4},{6,7},{7,6},{8,9},{9,8},{10,11... | collective-permute-start | bytes 884744 | tf_op jit(solution)/shard_map/ppermute | solution.py:18
  23.4 18.6 %collective-permute-start.6 = (f32[512,192]{1,0:T(8,128)S(1)}, f32[512,192]{1,0:T(8,128)S(1)}, u32[]{:S(2)}, u32[]{:S(2)}) collective-permute-start(f32[512,192]{1,0:T(8,128)S(1)} %get-tuple-element.129.own_ref.attended_ref), channel_id=1, source_target_pairs={{0,1},{1,0},{2,3},{3,2},{4,5},{5,4},{6,7},{7,6},{8,9},{9,8},{10,11... | collective-permute-start | bytes 1179656 | tf_op jit(solution)/shard_map/ppermute | solution.py:18
  54.1 22.9 %collective-permute-start.16 = (f32[256,768]{1,0:T(8,128)S(1)}, f32[256,768]{1,0:T(8,128)S(1)}, u32[]{:S(2)}, u32[]{:S(2)}) collective-permute-start(f32[256,768]{1,0:T(8,128)S(1)} %get-tuple-element.144), channel_id=1, source_target_pairs={{0,1},{1,0},{2,3},{3,2},{4,5},{5,4},{6,7},{7,6},{8,9},{9,8},{10,11... | collective-permute-start | bytes 2359304 | tf_op jit(solution)/shard_map/ppermute | solution.py:18
  54.3 22.8 %collective-permute-start.17 = (f32[256,768]{1,0:T(8,128)S(1)}, f32[256,768]{1,0:T(8,128)S(1)}, u32[]{:S(2)}, u32[]{:S(2)}) collective-permute-start(f32[256,768]{1,0:T(8,128)S(1)} %shard_map.277.left_ref), channel_id=1, source_target_pairs={{0,2},{1,3},{2,0},{3,1},{4,6},{5,7},{6,4},{7,5},{8,10},{9,11},{10,... | collective-permute-start | bytes 2359304 | tf_op jit(solution)/shard_map/ppermute | solution.py:18
  79.4 19.3 %collective-permute-start.22 = (f32[256,768]{1,0:T(8,128)S(1)}, f32[256,768]{1,0:T(8,128)S(1)}, u32[]{:S(2)}, u32[]{:S(2)}) collective-permute-start(f32[256,768]{1,0:T(8,128)S(1)} %shard_map.279.left_ref), channel_id=1, source_target_pairs={{0,2},{1,3},{2,0},{3,1},{4,6},{5,7},{6,4},{7,5},{8,10},{9,11},{10,... | collective-permute-start | bytes 2359304 | tf_op jit(solution)/shard_map/ppermute | solution.py:18
  98.8 10.8 %collective-permute-start.23 = (f32[256,768]{1,0:T(8,128)S(1)}, f32[256,768]{1,0:T(8,128)S(1)}, u32[]{:S(2)}, u32[]{:S(2)}) collective-permute-start(f32[256,768]{1,0:T(8,128)S(1)} %shard_map.283.full_ref), channel_id=1, source_target_pairs={{0,1},{1,0},{2,3},{3,2},{4,5},{5,4},{6,7},{7,6},{8,9},{9,8},{10,11... | collective-permute-start | bytes 2359304 | tf_op jit(solution)/shard_map/ppermute | solution.py:18
  103.5 18.9 %collective-permute-start.30 = (f32[256,768]{1,0:T(8,128)S(1)}, f32[256,768]{1,0:T(8,128)S(1)}, u32[]{:S(2)}, u32[]{:S(2)}) collective-permute-start(f32[256,768]{1,0:T(8,128)S(1)} %shard_map.288.left_ref), channel_id=1, source_target_pairs={{0,2},{1,3},{2,0},{3,1},{4,6},{5,7},{6,4},{7,5},{8,10},{9,11},{10,... | collective-permute-start | bytes 2359304 | tf_op jit(solution)/shard_map/ppermute | solution.py:18
  104.4 13.1 %collective-permute-start.32 = (f32[96,768]{1,0:T(8,128)S(1)}, f32[96,768]{1,0:T(8,128)S(1)}, u32[]{:S(2)}, u32[]{:S(2)}) collective-permute-start(f32[96,768]{1,0:T(8,128)S(1)} %get-tuple-element.183), channel_id=1, source_target_pairs={{0,4},{8,0},{16,8},{24,16},{28,24},{20,28},{12,20},{4,12},{1,5},{9... | collective-permute-start | bytes 884744 | tf_op jit(solution)/shard_map/ppermute | solution.py:180
  106.0 11.6 %collective-permute-start.31 = (f32[96,768]{1,0:T(8,128)S(1)}, f32[96,768]{1,0:T(8,128)S(1)}, u32[]{:S(2)}, u32[]{:S(2)}) collective-permute-start(f32[96,768]{1,0:T(8,128)S(1)} %get-tuple-element.174), channel_id=1, source_target_pairs={{0,8},{8,16},{16,24},{24,28},{28,20},{20,12},{12,4},{4,0},{1,9},{9... | collective-permute-start | bytes 884744 | tf_op jit(solution)/shard_map/ppermute | solution.py:180
  124.6 12.2 %collective-permute-start.41 = (f32[48,768]{1,0:T(8,128)S(1)}, f32[48,768]{1,0:T(8,128)S(1)}, u32[]{:S(2)}, u32[]{:S(2)}) collective-permute-start(f32[48,768]{1,0:T(8,128)S(1)} %get-tuple-element.206), channel_id=1, source_target_pairs={{0,4},{8,0},{16,8},{24,16},{28,24},{20,28},{12,20},{4,12},{1,5},{9... | collective-permute-start | bytes 442376 | tf_op jit(solution)/shard_map/ppermute | solution.py:180
  134.7 13.9 %collective-permute-start.68 = (f32[96,768]{1,0:T(8,128)S(1)}, f32[96,768]{1,0:T(8,128)S(1)}, u32[]{:S(2)}, u32[]{:S(2)}) collective-permute-start(f32[96,768]{1,0:T(8,128)S(1)} %get-tuple-element.231), channel_id=1, source_target_pairs={{0,8},{8,16},{16,24},{24,28},{28,20},{20,12},{12,4},{4,0},{1,9},{9... | collective-permute-start | bytes 884744 | tf_op jit(solution)/shard_map/ppermute | solution.py:180
  135.3 13.4 %collective-permute-start.69 = (f32[96,768]{1,0:T(8,128)S(1)}, f32[96,768]{1,0:T(8,128)S(1)}, u32[]{:S(2)}, u32[]{:S(2)}) collective-permute-start(f32[96,768]{1,0:T(8,128)S(1)} %get-tuple-element.232), channel_id=1, source_target_pairs={{0,4},{8,0},{16,8},{24,16},{28,24},{20,28},{12,20},{4,12},{1,5},{9... | collective-permute-start | bytes 884744 | tf_op jit(solution)/shard_map/ppermute | solution.py:180
  149.4 17.0 %collective-permute-start.70 = (f32[96,768]{1,0:T(8,128)S(1)}, f32[96,768]{1,0:T(8,128)S(1)}, u32[]{:S(2)}, u32[]{:S(2)}) collective-permute-start(f32[96,768]{1,0:T(8,128)S(1)} %get-tuple-element.233.refs_0_), channel_id=1, source_target_pairs={{0,8},{8,16},{16,24},{24,28},{28,20},{20,12},{12,4},{4,0},{1,9},{9... | collective-permute-start | bytes 884744 | tf_op jit(solution)/shard_map/ppermute | solution.py:180
  151.0 17.0 %collective-permute-start.76 = (f32[96,768]{1,0:T(8,128)S(1)}, f32[96,768]{1,0:T(8,128)}, u32[]{:S(2)}, u32[]{:S(2)}) collective-permute-start(f32[96,768]{1,0:T(8,128)S(1)} %get-tuple-element.234.refs_1_), channel_id=1, source_target_pairs={{0,4},{8,0},{16,8},{24,16},{28,24},{20,28},{12,20},{4,12},{1,5},{9... | collective-permute-start | bytes 884744 | tf_op jit(solution)/shard_map/ppermute | solution.py:180
  176.6 13.9 %collective-permute-start.72 = (f32[96,768]{1,0:T(8,128)}, f32[96,768]{1,0:T(8,128)}, u32[]{:S(2)}, u32[]{:S(2)}) collective-permute-start(f32[96,768]{1,0:T(8,128)} %collective-permute-done.71.refs_4_), channel_id=1, source_target_pairs={{0,8},{8,16},{16,24},{24,28},{28,20},{20,12},{12,4},{4,0},{1,9},{9... | collective-permute-start | bytes 884744 | tf_op jit(solution)/shard_map/ppermute | solution.py:180
  178.8 13.5 %collective-permute-start.78 = (f32[96,768]{1,0:T(8,128)}, f32[96,768]{1,0:T(8,128)}, u32[]{:S(2)}, u32[]{:S(2)}) collective-permute-start(f32[96,768]{1,0:T(8,128)} %collective-permute-done.77.refs_5_), channel_id=1, source_target_pairs={{0,4},{8,0},{16,8},{24,16},{28,24},{20,28},{12,20},{4,12},{1,5},{9... | collective-permute-start | bytes 884744 | tf_op jit(solution)/shard_map/ppermute | solution.py:180
  182.1 11.2 %collective-permute-start.38 = (f32[16,1152]{1,0:T(8,128)}, f32[16,1152]{1,0:T(8,128)S(1)}, u32[]{:S(2)}, u32[]{:S(2)}) collective-permute-start(f32[16,1152]{1,0:T(8,128)} %get-tuple-element.247), channel_id=1, source_target_pairs={{0,16},{4,20},{8,24},{12,28},{16,0},{20,4},{24,8},{28,12},{1,17},{... | collective-permute-start | bytes 221192 | tf_op jit(solution)/shard_map/ppermute | solution.py:39
  184.7 11.6 %collective-permute-start.52 = (f32[48,768]{1,0:T(8,128)S(1)}, f32[48,768]{1,0:T(8,128)S(1)}, u32[]{:S(2)}, u32[]{:S(2)}) collective-permute-start(f32[48,768]{1,0:T(8,128)S(1)} %get-tuple-element.219.refs_0_), channel_id=1, source_target_pairs={{0,8},{8,16},{16,24},{24,28},{28,20},{20,12},{12,4},{4,0},{1,9},{9... | collective-permute-start | bytes 442376 | tf_op jit(solution)/shard_map/ppermute | solution.py:180
  190.4 14.4 %collective-permute-start.73 = (f32[96,768]{1,0:T(8,128)}, f32[96,768]{1,0:T(8,128)S(1)}, u32[]{:S(2)}, u32[]{:S(2)}) collective-permute-start(f32[96,768]{1,0:T(8,128)} %collective-permute-done.72.refs_6_), channel_id=1, source_target_pairs={{0,8},{8,16},{16,24},{24,28},{28,20},{20,12},{12,4},{4,0},{1,9},{9... | collective-permute-start | bytes 884744 | tf_op jit(solution)/shard_map/ppermute | solution.py:180
  192.3 13.7 %collective-permute-start.79 = (f32[96,768]{1,0:T(8,128)}, f32[96,768]{1,0:T(8,128)S(1)}, u32[]{:S(2)}, u32[]{:S(2)}) collective-permute-start(f32[96,768]{1,0:T(8,128)} %collective-permute-done.78.refs_7_), channel_id=1, source_target_pairs={{0,4},{8,0},{16,8},{24,16},{28,24},{20,28},{12,20},{4,12},{1,5},{9... | collective-permute-start | bytes 884744 | tf_op jit(solution)/shard_map/ppermute | solution.py:180
  193.3 13.5 %collective-permute-start.39 = (f32[16,1152]{1,0:T(8,128)}, f32[16,1152]{1,0:T(8,128)S(1)}, u32[]{:S(2)}, u32[]{:S(2)}) collective-permute-start(f32[16,1152]{1,0:T(8,128)} %get-tuple-element.247), channel_id=1, source_target_pairs={{0,24},{4,28},{8,0},{12,4},{16,8},{20,12},{24,16},{28,20},{1,25},{... | collective-permute-start | bytes 221192 | tf_op jit(solution)/shard_map/ppermute | solution.py:39
  204.9 13.5 %collective-permute-start.74 = (f32[96,768]{1,0:T(8,128)S(1)}, f32[96,768]{1,0:T(8,128)S(1)}, u32[]{:S(2)}, u32[]{:S(2)}) collective-permute-start(f32[96,768]{1,0:T(8,128)S(1)} %collective-permute-done.73.refs_8_), channel_id=1, source_target_pairs={{0,8},{8,16},{16,24},{24,28},{28,20},{20,12},{12,4},{4,0},{1,9},{9... | collective-permute-start | bytes 884744 | tf_op jit(solution)/shard_map/ppermute | solution.py:180
  206.0 13.3 %collective-permute-start.80 = (f32[96,768]{1,0:T(8,128)S(1)}, f32[96,768]{1,0:T(8,128)S(1)}, u32[]{:S(2)}, u32[]{:S(2)}) collective-permute-start(f32[96,768]{1,0:T(8,128)S(1)} %collective-permute-done.79.refs_9_), channel_id=1, source_target_pairs={{0,4},{8,0},{16,8},{24,16},{28,24},{20,28},{12,20},{4,12},{1,5},{9... | collective-permute-start | bytes 884744 | tf_op jit(solution)/shard_map/ppermute | solution.py:180
  211.0 11.2 %collective-permute-start.55 = (f32[48,768]{1,0:T(8,128)}, f32[48,768]{1,0:T(8,128)S(1)}, u32[]{:S(2)}, u32[]{:S(2)}) collective-permute-start(f32[48,768]{1,0:T(8,128)} %collective-permute-done.54.refs_6_), channel_id=1, source_target_pairs={{0,8},{8,16},{16,24},{24,28},{28,20},{20,12},{12,4},{4,0},{1,9},{9... | collective-permute-start | bytes 442376 | tf_op jit(solution)/shard_map/ppermute | solution.py:180
  212.1 11.1 %collective-permute-start.61 = (f32[48,768]{1,0:T(8,128)}, f32[48,768]{1,0:T(8,128)}, u32[]{:S(2)}, u32[]{:S(2)}) collective-permute-start(f32[48,768]{1,0:T(8,128)} %collective-permute-done.60.refs_7_), channel_id=1, source_target_pairs={{0,4},{8,0},{16,8},{24,16},{28,24},{20,28},{12,20},{4,12},{1,5},{9... | collective-permute-start | bytes 442376 | tf_op jit(solution)/shard_map/ppermute | solution.py:180
  218.3 14.0 %collective-permute-start.75 = (f32[96,768]{1,0:T(8,128)S(1)}, f32[96,768]{1,0:T(8,128)S(1)}, u32[]{:S(2)}, u32[]{:S(2)}) collective-permute-start(f32[96,768]{1,0:T(8,128)S(1)} %collective-permute-done.74.refs_10_), channel_id=1, source_target_pairs={{0,8},{8,16},{16,24},{24,28},{28,20},{20,12},{12,4},{4,0},{1,9},{9... | collective-permute-start | bytes 884744 | tf_op jit(solution)/shard_map/ppermute | solution.py:180
  219.3 13.0 %collective-permute-start.81 = (f32[96,768]{1,0:T(8,128)S(1)}, f32[96,768]{1,0:T(8,128)S(1)}, u32[]{:S(2)}, u32[]{:S(2)}) collective-permute-start(f32[96,768]{1,0:T(8,128)S(1)} %collective-permute-done.80.refs_11_), channel_id=1, source_target_pairs={{0,4},{8,0},{16,8},{24,16},{28,24},{20,28},{12,20},{4,12},{1,5},{9... | collective-permute-start | bytes 884744 | tf_op jit(solution)/shard_map/ppermute | solution.py:180
  232.4 19.5 %collective-permute-start.82 = (f32[96,768]{1,0:T(8,128)S(1)}, f32[96,768]{1,0:T(8,128)S(1)}, u32[]{:S(2)}, u32[]{:S(2)}) collective-permute-start(f32[96,768]{1,0:T(8,128)S(1)} %collective-permute-done.75.refs_0_), channel_id=1, source_target_pairs={{0,8},{8,16},{16,24},{24,28},{28,20},{20,12},{12,4},{4,0},{1,9},{9... | collective-permute-start | bytes 884744 | tf_op jit(solution)/shard_map/ppermute | solution.py:180
  233.6 18.2 %collective-permute-start.83 = (f32[96,768]{1,0:T(8,128)S(1)}, f32[96,768]{1,0:T(8,128)S(1)}, u32[]{:S(2)}, u32[]{:S(2)}) collective-permute-start(f32[96,768]{1,0:T(8,128)S(1)} %collective-permute-done.81.refs_1_), channel_id=1, source_target_pairs={{0,4},{8,0},{16,8},{24,16},{28,24},{20,28},{12,20},{4,12},{1,5},{9... | collective-permute-start | bytes 884744 | tf_op jit(solution)/shard_map/ppermute | solution.py:180
  (79 other events, 676.1 us)

commit v5 on v4

--- a/solution.py
+++ b/solution.py
@@ -92,7 +92,8 @@
     return jnp.concatenate(natural(blocks), axis=1)
 
 
-def place_kernel(steps, size, first, targets, outs, kept, spots_ref, *refs):
+def place_kernel(steps, size, first, targets, outs, kept, waits, spots_ref, *refs):
+    refs = refs[waits:]
     count = len(targets)
     pieces = refs[: steps * count]
     out_refs = refs[steps * count + kept : steps * count + kept + outs]
@@ -122,21 +123,21 @@
         copy.wait()
 
 
-def place_rows(pieces, size, table, first, targets, shapes, filled=()):
+def place_rows(pieces, size, table, first, targets, shapes, filled=(), behind=()):
     steps = len(pieces)
     copies = steps * sum(len(runs) for runs in targets)
     operands = [piece for step in pieces for piece in step]
     anywhere = pl.BlockSpec(memory_space=pl.ANY)
     *outs, token = pl.pallas_call(
-        functools.partial(place_kernel, steps, size, first, targets, len(shapes), len(filled)),
+        functools.partial(place_kernel, steps, size, first, targets, len(shapes), len(filled), len(behind)),
         out_shape=[jax.ShapeDtypeStruct(shape, F32) for shape in (*shapes, (8, 128))],
-        in_specs=[IN_SMEM] + [IN_VMEM] * len(operands) + [anywhere] * len(filled),
+        in_specs=[IN_SMEM] + [IN_VMEM] * (len(behind) + len(operands)) + [anywhere] * len(filled),
         out_specs=[anywhere] * len(shapes) + [IN_VMEM],
         scratch_shapes=[pltpu.SemaphoreType.DMA((copies,))],
-        input_output_aliases={1 + len(operands) + at: at for at in range(len(filled))},
+        input_output_aliases={1 + len(behind) + len(operands) + at: at for at in range(len(filled))},
         compiler_params=pltpu.CompilerParams(vmem_limit_bytes=SMALL_LIMIT),
         cost_estimate=QUICK,
-    )(table, *operands, *filled)
+    )(table, *behind, *operands, *filled)
     return outs, token
 
 
@@ -188,14 +189,18 @@
 
     def finish(self, targets, shapes, gate=None):
         steps = 2 * self.size - 2
+        if gate is None:
+            while self.count < steps:
+                self.step()
+            return place_rows(self.pieces, self.size, self.table, self.size - 1, targets, shapes)
         while self.count < steps - 2:
             self.step()
         early = len(self.pieces)
-        outs, token = place_rows(self.pieces, self.size, self.table, self.size - 1, targets, shapes)
-        self.step(token)
-        if gate is not None:
-            self.moving = after(self.moving, gate)
-        self.step()
+        outs, token = place_rows(
+            self.pieces, self.size, self.table, self.size - 1, targets, shapes, (), (gate,)
+        )
+        while self.count < steps:
+            self.step()
         return place_rows(
             self.pieces[early:], self.size, self.table, self.size - 1 + early, targets, shapes, outs
         )

time: 255 us -> 259 us (1.016)
  local copies, waits for them, and re-layouts: 7.3 us -> 12.2 us
    unnamed x48 -> x72, local copies, waits for them, and re-layouts: 5.07 us -> 9.94 us
    pallas_call x4 -> x3, Pallas kernels: 11.3 us -> 8.76 us  [place_rows(): pl.pallas_call(functools.partial(place_kernel, steps, size, first, target...]
  transfers between devices with their start and end apart: 87 -> 87, of which waited for: 37 -> 39; matrix products, arithmetic and copies ran while one was open for 4% -> 3% of each run, Pallas kernels for 17% -> 16%
where the time goes in v5:
time: 259 us; the launch traced here: 258 us
  waiting for transfers between devices  105 us (41%)
  starting transfers between devices  78.9 us (30%)
  Pallas kernels  51.3 us (20%)
  local copies, waits for them, and re-layouts  12.2 us (5%)
  matrix products  5.93 us (2%)
  other arithmetic  2.93 us (1%)
    ppermute x56, waiting for transfers between devices, step(): lax.ppermute(held, 'dp', perm)  66.2 us
    ppermute x56, starting transfers between devices, step(): lax.ppermute(held, 'dp', perm)  57.3 us
    pallas_call x33, Pallas kernels, call(): pl.pallas_call(kernel, out_shape=out_shape, in_specs=[IN_SMEM] * scalars...  42.5 us
    ppermute x27, waiting for transfers between devices, swap(): lax.ppermute(values, 'tensor', [(at, at ^ bit) for at in range(size)])  35.5 us
    ppermute x27, starting transfers between devices, swap(): lax.ppermute(values, 'tensor', [(at, at ^ bit) for at in range(size)])  15.6 us
    unnamed x72, local copies, waits for them, and re-layouts  9.94 us
    pallas_call x3, Pallas kernels, place_rows(): pl.pallas_call(functools.partial(place_kernel, steps, size, first, target...  8.76 us
    ppermute x3, starting transfers between devices, gather_latents(): lax.ppermute(pair, 'dp', [(at, (at + step) % size) for at in range(size)])  5.61 us
  transfers between devices with their start and end apart: 87, of which 39 were waited for; matrix products, arithmetic and copies ran while one was open for 3% of the time, Pallas kernels for 16%

profile of v5, /device:TPU:0, one launch (start us, length us, event | category | flops | bytes accessed | tf_op | source)
XLA Modules:
  0.0 258.2 jit_solution(3724731126349760304)
XLA Ops:
  4.2 2.6 collective-permute-start.1
  13.6 3.9 %collective-permute-done.4 = f32[2,1152]{1,0:T(2,128)S(1)} collective-permute-done((f32[2,1152]{1,0:T(2,128)S(1)}, f32[2,1152]{1,0:T(2,128)S(1)}, u32[]{:S(2)}, u32[]{:S(2)}) %collective-permute-start.4) | collective-permute-done | bytes 9248 | tf_op jit(solution)/shard_map/ppermute | solution.py:18
  17.6 3.7 %shard_map.272 = (bf16[512,768]{1,0:T(8,128)(2,1)S(1)}, bf16[512,192]{1,0:T(8,128)(2,1)S(1)}, bf16[512,192]{1,0:T(8,128)(2,1)S(1)}, bf16[512,192]{1,0:T(8,128)(2,1)S(1)}, f32[512,192]{1,0:T(8,128)S(1)}) custom-call(s32[15,2]{1,0:T(8,128)S(1)} %add_select_fusion.table_ref.spots_ref, s32[2]{0:T(128)S(1)} %pad_add_fusion.flags_ref.odd_ref, ...), custom_call_target="tpu_custom_call" | custom-call | flops 1 | bytes 1 | tf_op jit(solution)/shard_map/pallas_call | solution.py:66
  24.8 11.3 %collective-permute-done.7.across_ref = f32[512,192]{1,0:T(8,128)S(1)} collective-permute-done((f32[512,192]{1,0:T(8,128)S(1)}, f32[512,192]{1,0:T(8,128)S(1)}, u32[]{:S(2)}, u32[]{:S(2)}) %collective-permute-start.7) | collective-permute-done | bytes 393248 | tf_op jit(solution)/shard_map/ppermute | solution.py:18
  36.6 5.0 %collective-permute-done.12.mixing_5_ref = f32[96,768]{1,0:T(8,128)S(1)} collective-permute-done((f32[96,768]{1,0:T(8,128)S(1)}, f32[96,768]{1,0:T(8,128)S(1)}, u32[]{:S(2)}, u32[]{:S(2)}) %collective-permute-start.12) | collective-permute-done | bytes 294944 | tf_op jit(solution)/shard_map/ppermute | solution.py:18
  43.6 5.2 %shard_map.276 = (f32[512,768]{1,0:T(8,128)S(1)}, bf16[512,768]{1,0:T(8,128)(2,1)S(1)}, bf16[512,768]{1,0:T(8,128)(2,1)S(1)}, bf16[512,768]{1,0:T(8,128)(2,1)S(1...) custom-call(s32[2]{0:T(128)S(1)} %pad_add_fusion.flags_ref.odd_ref, ...), custom_call_target="tpu_custom_call" | custom-call | flops 1 | bytes 1 | tf_op jit(solution)/shard_map/pallas_call | solution.py:66
  48.9 2.2 collective-permute-done.15.right_ref
  51.2 2.9 %shard_map.278 = (f32[768,768]{1,0:T(8,128)S(1)}, f32[768,768]{1,0:T(8,128)S(1)}, f32[2,768]{1,0:T(2,128)S(1)}, f32[96,768]{1,0:T(8,128)S(1)}, f32[96,768]{1,0:T...) custom-call(s32[15,2]{1,0:T(8,128)S(1)} %add_select_fusion.table_ref.spots_ref, ...), custom_call_target="tpu_custom_call" | custom-call | flops 1 | bytes 1 | tf_op jit(solution)/shard_map/pallas_call | solution.py:66
  58.1 7.0 %collective-permute-done.18.refs_0_ = f32[96,768]{1,0:T(8,128)S(1)} collective-permute-done((f32[96,768]{1,0:T(8,128)S(1)}, f32[96,768]{1,0:T(8,128)S(1)}, u32[]{:S(2)}, u32[]{:S(2)}) %collective-permute-start.18) | collective-permute-done | bytes 294944 | tf_op jit(solution)/shard_map/ppermute | solution.py:181
  69.2 5.8 %collective-permute-done.20.refs_0_ = f32[96,768]{1,0:T(8,128)S(1)} collective-permute-done((f32[96,768]{1,0:T(8,128)S(1)}, f32[96,768]{1,0:T(8,128)S(1)}, u32[]{:S(2)}, u32[]{:S(2)}) %collective-permute-start.20) | collective-permute-done | bytes 294944 | tf_op jit(solution)/shard_map/ppermute | solution.py:181
  82.1 4.7 %collective-permute-done.26.refs_1_ = f32[96,768]{1,0:T(8,128)S(1)} collective-permute-done((f32[96,768]{1,0:T(8,128)S(1)}, f32[96,768]{1,0:T(8,128)S(1)}, u32[]{:S(2)}, u32[]{:S(2)}) %collective-permute-start.26) | collective-permute-done | bytes 294944 | tf_op jit(solution)/shard_map/ppermute | solution.py:181
  87.7 5.2 %shard_map.286 = (bf16[512,192]{1,0:T(8,128)(2,1)S(1)}, bf16[512,192]{1,0:T(8,128)(2,1)S(1)}, bf16[512,192]{1,0:T(8,128)(2,1)S(1)}, f32[256,768]{1,0:T(8,128)S(1)}, f32[256,768]{1,0:T(8,128)S(1)}) custom-call(s32[2]{0:T(128)S(1)} %pad_add_fusion.flags_ref.odd_ref, bf16[512,768]{1,0:T(8,128)(2,1)S(1)} %get-tuple-element.155.d_attn_ref, ...), custom_call_target="tpu_custom_call" | custom-call | flops 1 | bytes 1 | tf_op jit(solution)/shard_map/pallas_call | solution.py:66
  95.1 3.7 %collective-permute-done.22.right_ref = f32[256,768]{1,0:T(8,128)S(1)} collective-permute-done((f32[256,768]{1,0:T(8,128)S(1)}, f32[256,768]{1,0:T(8,128)S(1)}, u32[]{:S(2)}, u32[]{:S(2)}) %collective-permute-start.22) | collective-permute-done | bytes 786464 | tf_op jit(solution)/shard_map/ppermute | solution.py:18
  98.9 3.5 %collective-permute-done.29.refs_1_ = f32[96,768]{1,0:T(8,128)S(1)} collective-permute-done((f32[96,768]{1,0:T(8,128)S(1)}, f32[96,768]{1,0:T(8,128)S(1)}, u32[]{:S(2)}, u32[]{:S(2)}) %collective-permute-start.29) | collective-permute-done | bytes 294944 | tf_op jit(solution)/shard_map/ppermute | solution.py:181
  110.1 2.3 shard_map.290
  112.5 3.1 %collective-permute-done.34.refs_1_ = f32[48,768]{1,0:T(8,128)S(1)} collective-permute-done((f32[48,768]{1,0:T(8,128)S(1)}, f32[48,768]{1,0:T(8,128)S(1)}, u32[]{:S(2)}, u32[]{:S(2)}) %collective-permute-start.34) | collective-permute-done | bytes 147488 | tf_op jit(solution)/shard_map/ppermute | solution.py:181
  118.3 4.1 %collective-permute-done.30.right_ref = f32[256,768]{1,0:T(8,128)S(1)} collective-permute-done((f32[256,768]{1,0:T(8,128)S(1)}, f32[256,768]{1,0:T(8,128)S(1)}, u32[]{:S(2)}, u32[]{:S(2)}) %collective-permute-start.30) | collective-permute-done | bytes 786464 | tf_op jit(solution)/shard_map/ppermute | solution.py:18
  126.7 3.0 %shard_map.294 = (f32[512,768]{1,0:T(8,128)}, f32[2,768]{1,0:T(2,128)S(1)}, f32[2,768]{1,0:T(2,128)S(1)}) custom-call(s32[2]{0:T(128)S(1)} %pad_add_fusion.flags_ref.odd_ref, f32[256,768]{1,0:T(8,128)S(1)} %shard_map.293.full_ref, f32[256,768]{1,0:T(8,128)S(1)} %collective-permute-done.35.other_ref, bf16[512,768]{1,0:T(8,128)(2,1)S(1)} %copy-done.2, ...), custom_call_target="tpu_custom_call" | custom-call | flops 1 | bytes 1 | tf_op jit(solution)/shard_map/pallas_call | solution.py:66
  130.2 2.2 collective-permute-done.67.refs_1_
  139.6 6.3 %collective-permute-done.42.refs_0_ = f32[48,768]{1,0:T(8,128)S(1)} collective-permute-done((f32[48,768]{1,0:T(8,128)S(1)}, f32[48,768]{1,0:T(8,128)S(1)}, u32[]{:S(2)}, u32[]{:S(2)}) %collective-permute-start.42) | collective-permute-done | bytes 147488 | tf_op jit(solution)/shard_map/ppermute | solution.py:181
  158.8 2.9 %collective-permute-done.46.refs_0_ = f32[48,768]{1,0:T(8,128)S(1)} collective-permute-done((f32[48,768]{1,0:T(8,128)}, f32[48,768]{1,0:T(8,128)S(1)}, u32[]{:S(2)}, u32[]{:S(2)}) %collective-permute-start.46) | collective-permute-done | bytes 147488 | tf_op jit(solution)/shard_map/ppermute | solution.py:181
  170.1 2.2 collective-permute-done.49.refs_1_
  186.6 3.7 %collective-permute-done.37 = f32[16,1152]{1,0:T(8,128)} collective-permute-done((f32[16,1152]{1,0:T(8,128)}, f32[16,1152]{1,0:T(8,128)}, u32[]{:S(2)}, u32[]{:S(2)}) %collective-permute-start.37) | collective-permute-done | bytes 73760 | tf_op jit(solution)/shard_map/ppermute | solution.py:39
  193.3 3.0 %collective-permute-start.39 = (f32[16,1152]{1,0:T(8,128)}, f32[16,1152]{1,0:T(8,128)S(1)}, u32[]{:S(2)}, u32[]{:S(2)}) collective-permute-start(f32[16,1152]{1,0:T(8,128)} %get-tuple-element.233), channel_id=1, source_target_pairs={{0,24},{4,28},{8,0},{12,4},{16,8},{20,12},{24,16},{28,20},{1,25},{... | collective-permute-start | bytes 221192 | tf_op jit(solution)/shard_map/ppermute | solution.py:39
  198.4 4.1 %collective-permute-done.54.refs_4_ = f32[48,768]{1,0:T(8,128)S(1)} collective-permute-done((f32[48,768]{1,0:T(8,128)S(1)}, f32[48,768]{1,0:T(8,128)S(1)}, u32[]{:S(2)}, u32[]{:S(2)}) %collective-permute-start.54) | collective-permute-done | bytes 147488 | tf_op jit(solution)/shard_map/ppermute | solution.py:181
  208.4 2.6 %shard_map.296 = (f32[768,1152]{1,0:T(8,128)}, f32[1,1152]{1,0:T(1,128)S(1)}, f32[16,768]{1,0:T(8,128)S(1)}, f32[5,1152]{1,0:T(8,128)S(1)}) custom-call(f32[64,1152]{1,0:T(8,128)S(1)} %constant_dynamic-update-slice_fusion.carried_ref, bf16[16,768]{1,0:T(8,128)(2,1)S(1)} %multiply_convert_fusion.silu_ref, bf16[768,1152]{1,0:T(8,128)(2,1)S(1)} %copy-done.4), custom_call_target="tpu_custom_call" | custom-call | flops 1 | bytes 1 | tf_op jit(solution)/shard_map/pallas_call | solution.py:66
  214.8 2.7 %collective-permute-done.86 = f32[16,192]{1,0:T(8,128)S(1)} collective-permute-done((f32[16,192]{1,0:T(8,128)S(1)}, f32[16,192]{1,0:T(8,128)S(1)}, u32[]{:S(2)}, u32[]{:S(2)}) %collective-permute-start.86) | collective-permute-done | bytes 12320 | tf_op jit(solution)/shard_map/ppermute | solution.py:18
  226.3 3.9 %collective-permute-done.60.refs_10_ = f32[48,768]{1,0:T(8,128)S(1)} collective-permute-done((f32[48,768]{1,0:T(8,128)S(1)}, f32[48,768]{1,0:T(8,128)S(1)}, u32[]{:S(2)}, u32[]{:S(2)}) %collective-permute-start.60) | collective-permute-done | bytes 147488 | tf_op jit(solution)/shard_map/ppermute | solution.py:181
  241.5 3.3 %collective-permute-done.64.refs_14_ = f32[48,768]{1,0:T(8,128)S(1)} collective-permute-done((f32[48,768]{1,0:T(8,128)S(1)}, f32[48,768]{1,0:T(8,128)S(1)}, u32[]{:S(2)}, u32[]{:S(2)}) %collective-permute-start.64) | collective-permute-done | bytes 147488 | tf_op jit(solution)/shard_map/ppermute | solution.py:181
  249.1 2.7 %shard_map.303 = (f32[576,768]{1,0:T(8,128)}, f32[192,768]{1,0:T(8,128)}, f32[8,128]{1,0:T(8,128)S(1)}) custom-call(s32[15,2]{1,0:T(8,128)S(1)} %add_select_fusion.table_ref.spots_ref, f32[48,768]{1,0:T(8,128)S(1)} %get-tuple-element.212.refs_0_, f32[48,768]{1,0:T(8,128)S(1)} %copy-done.18, f32[48,768]{1,0:T(8,128)S(1)} %copy-done.20, ...), custom_call_target="tpu_custom_call" | custom-call | flops 1 | bytes 1 | tf_op jit(solution)/shard_map/pallas_call | solution.py:131
  251.8 3.8 %shard_map.306 = (f32[768,768]{1,0:T(8,128)}, f32[768,768]{1,0:T(8,128)}, f32[8,128]{1,0:T(8,128)}) custom-call(s32[15,2]{1,0:T(8,128)S(1)} %add_select_fusion.table_ref.spots_ref, f32[8,128]{1,0:T(8,128)S(1)} %get-tuple-element.224.refs_0_, f32[96,768]{1,0:T(8,128)S(1)} %get-tuple-element.222.refs_1_, f32[96,768]{1,0:T(8,128)S(1)} %get-tuple-element.223.refs_2_, ...), custom_call_target="tpu_custom_call" | custom-call | flops 1 | bytes 1 | tf_op jit(solution)/shard_map/pallas_call | solution.py:131
  255.7 2.3 shard_map.307
  (277 shorter events, 132.1 us)
Async XLA Ops:
  7.9 28.2 %collective-permute-start.11 = (f32[96,768]{1,0:T(8,128)S(1)}, f32[96,768]{1,0:T(8,128)S(1)}, u32[]{:S(2)}, u32[]{:S(2)}) collective-permute-start(f32[96,768]{1,0:T(8,128)S(1)} %shard_map.274.mixing_0_ref), channel_id=1, source_target_pairs={{0,2},{1,3},{2,0},{3,1},{4,6},{5,7},{6,4},{7,5},{8,10},{9,11},{10,... | collective-permute-start | bytes 884744 | tf_op jit(solution)/shard_map/ppermute | solution.py:18
  21.2 14.8 %collective-permute-start.7 = (f32[512,192]{1,0:T(8,128)S(1)}, f32[512,192]{1,0:T(8,128)S(1)}, u32[]{:S(2)}, u32[]{:S(2)}) collective-permute-start(f32[512,192]{1,0:T(8,128)S(1)} %get-tuple-element.122.own_ref.attended_ref), channel_id=1, source_target_pairs={{0,2},{1,3},{2,0},{3,1},{4,6},{5,7},{6,4},{7,5},{8,10},{9,11},{10,... | collective-permute-start | bytes 1179656 | tf_op jit(solution)/shard_map/ppermute | solution.py:18
  23.1 18.5 %collective-permute-start.12 = (f32[96,768]{1,0:T(8,128)S(1)}, f32[96,768]{1,0:T(8,128)S(1)}, u32[]{:S(2)}, u32[]{:S(2)}) collective-permute-start(f32[96,768]{1,0:T(8,128)S(1)} %shard_map.275.mixing_1_ref), channel_id=1, source_target_pairs={{0,2},{1,3},{2,0},{3,1},{4,6},{5,7},{6,4},{7,5},{8,10},{9,11},{10,... | collective-permute-start | bytes 884744 | tf_op jit(solution)/shard_map/ppermute | solution.py:18
  23.4 18.1 %collective-permute-start.9 = (f32[96,768]{1,0:T(8,128)S(1)}, f32[96,768]{1,0:T(8,128)S(1)}, u32[]{:S(2)}, u32[]{:S(2)}) collective-permute-start(f32[96,768]{1,0:T(8,128)S(1)} %shard_map.274.mixing_0_ref), channel_id=1, source_target_pairs={{0,1},{1,0},{2,3},{3,2},{4,5},{5,4},{6,7},{7,6},{8,9},{9,8},{10,11... | collective-permute-start | bytes 884744 | tf_op jit(solution)/shard_map/ppermute | solution.py:18
  23.4 18.6 %collective-permute-start.6 = (f32[512,192]{1,0:T(8,128)S(1)}, f32[512,192]{1,0:T(8,128)S(1)}, u32[]{:S(2)}, u32[]{:S(2)}) collective-permute-start(f32[512,192]{1,0:T(8,128)S(1)} %get-tuple-element.122.own_ref.attended_ref), channel_id=1, source_target_pairs={{0,1},{1,0},{2,3},{3,2},{4,5},{5,4},{6,7},{7,6},{8,9},{9,8},{10,11... | collective-permute-start | bytes 1179656 | tf_op jit(solution)/shard_map/ppermute | solution.py:18
  54.1 22.9 %collective-permute-start.16 = (f32[256,768]{1,0:T(8,128)S(1)}, f32[256,768]{1,0:T(8,128)S(1)}, u32[]{:S(2)}, u32[]{:S(2)}) collective-permute-start(f32[256,768]{1,0:T(8,128)S(1)} %get-tuple-element.137), channel_id=1, source_target_pairs={{0,1},{1,0},{2,3},{3,2},{4,5},{5,4},{6,7},{7,6},{8,9},{9,8},{10,11... | collective-permute-start | bytes 2359304 | tf_op jit(solution)/shard_map/ppermute | solution.py:18
  54.3 22.8 %collective-permute-start.17 = (f32[256,768]{1,0:T(8,128)S(1)}, f32[256,768]{1,0:T(8,128)S(1)}, u32[]{:S(2)}, u32[]{:S(2)}) collective-permute-start(f32[256,768]{1,0:T(8,128)S(1)} %shard_map.277.left_ref), channel_id=1, source_target_pairs={{0,2},{1,3},{2,0},{3,1},{4,6},{5,7},{6,4},{7,5},{8,10},{9,11},{10,... | collective-permute-start | bytes 2359304 | tf_op jit(solution)/shard_map/ppermute | solution.py:18
  79.4 19.3 %collective-permute-start.22 = (f32[256,768]{1,0:T(8,128)S(1)}, f32[256,768]{1,0:T(8,128)S(1)}, u32[]{:S(2)}, u32[]{:S(2)}) collective-permute-start(f32[256,768]{1,0:T(8,128)S(1)} %shard_map.279.left_ref), channel_id=1, source_target_pairs={{0,2},{1,3},{2,0},{3,1},{4,6},{5,7},{6,4},{7,5},{8,10},{9,11},{10,... | collective-permute-start | bytes 2359304 | tf_op jit(solution)/shard_map/ppermute | solution.py:18
  98.8 10.8 %collective-permute-start.23 = (f32[256,768]{1,0:T(8,128)S(1)}, f32[256,768]{1,0:T(8,128)S(1)}, u32[]{:S(2)}, u32[]{:S(2)}) collective-permute-start(f32[256,768]{1,0:T(8,128)S(1)} %shard_map.283.full_ref), channel_id=1, source_target_pairs={{0,1},{1,0},{2,3},{3,2},{4,5},{5,4},{6,7},{7,6},{8,9},{9,8},{10,11... | collective-permute-start | bytes 2359304 | tf_op jit(solution)/shard_map/ppermute | solution.py:18
  103.5 18.9 %collective-permute-start.30 = (f32[256,768]{1,0:T(8,128)S(1)}, f32[256,768]{1,0:T(8,128)S(1)}, u32[]{:S(2)}, u32[]{:S(2)}) collective-permute-start(f32[256,768]{1,0:T(8,128)S(1)} %shard_map.288.left_ref), channel_id=1, source_target_pairs={{0,2},{1,3},{2,0},{3,1},{4,6},{5,7},{6,4},{7,5},{8,10},{9,11},{10,... | collective-permute-start | bytes 2359304 | tf_op jit(solution)/shard_map/ppermute | solution.py:18
  104.4 13.1 %collective-permute-start.32 = (f32[96,768]{1,0:T(8,128)S(1)}, f32[96,768]{1,0:T(8,128)S(1)}, u32[]{:S(2)}, u32[]{:S(2)}) collective-permute-start(f32[96,768]{1,0:T(8,128)S(1)} %get-tuple-element.176), channel_id=1, source_target_pairs={{0,4},{8,0},{16,8},{24,16},{28,24},{20,28},{12,20},{4,12},{1,5},{9... | collective-permute-start | bytes 884744 | tf_op jit(solution)/shard_map/ppermute | solution.py:181
  106.0 11.6 %collective-permute-start.31 = (f32[96,768]{1,0:T(8,128)S(1)}, f32[96,768]{1,0:T(8,128)S(1)}, u32[]{:S(2)}, u32[]{:S(2)}) collective-permute-start(f32[96,768]{1,0:T(8,128)S(1)} %get-tuple-element.167), channel_id=1, source_target_pairs={{0,8},{8,16},{16,24},{24,28},{28,20},{20,12},{12,4},{4,0},{1,9},{9... | collective-permute-start | bytes 884744 | tf_op jit(solution)/shard_map/ppermute | solution.py:181
  124.6 12.2 %collective-permute-start.41 = (f32[48,768]{1,0:T(8,128)S(1)}, f32[48,768]{1,0:T(8,128)S(1)}, u32[]{:S(2)}, u32[]{:S(2)}) collective-permute-start(f32[48,768]{1,0:T(8,128)S(1)} %get-tuple-element.199), channel_id=1, source_target_pairs={{0,4},{8,0},{16,8},{24,16},{28,24},{20,28},{12,20},{4,12},{1,5},{9... | collective-permute-start | bytes 442376 | tf_op jit(solution)/shard_map/ppermute | solution.py:181
  134.7 13.9 %collective-permute-start.68 = (f32[96,768]{1,0:T(8,128)S(1)}, f32[96,768]{1,0:T(8,128)S(1)}, u32[]{:S(2)}, u32[]{:S(2)}) collective-permute-start(f32[96,768]{1,0:T(8,128)S(1)} %get-tuple-element.220), channel_id=1, source_target_pairs={{0,8},{8,16},{16,24},{24,28},{28,20},{20,12},{12,4},{4,0},{1,9},{9... | collective-permute-start | bytes 884744 | tf_op jit(solution)/shard_map/ppermute | solution.py:181
  135.3 13.4 %collective-permute-start.69 = (f32[96,768]{1,0:T(8,128)S(1)}, f32[96,768]{1,0:T(8,128)S(1)}, u32[]{:S(2)}, u32[]{:S(2)}) collective-permute-start(f32[96,768]{1,0:T(8,128)S(1)} %get-tuple-element.221), channel_id=1, source_target_pairs={{0,4},{8,0},{16,8},{24,16},{28,24},{20,28},{12,20},{4,12},{1,5},{9... | collective-permute-start | bytes 884744 | tf_op jit(solution)/shard_map/ppermute | solution.py:181
  149.4 17.0 %collective-permute-start.70 = (f32[96,768]{1,0:T(8,128)S(1)}, f32[96,768]{1,0:T(8,128)S(1)}, u32[]{:S(2)}, u32[]{:S(2)}) collective-permute-start(f32[96,768]{1,0:T(8,128)S(1)} %get-tuple-element.222.refs_1_), channel_id=1, source_target_pairs={{0,8},{8,16},{16,24},{24,28},{28,20},{20,12},{12,4},{4,0},{1,9},{9... | collective-permute-start | bytes 884744 | tf_op jit(solution)/shard_map/ppermute | solution.py:181
  151.0 17.0 %collective-permute-start.76 = (f32[96,768]{1,0:T(8,128)S(1)}, f32[96,768]{1,0:T(8,128)}, u32[]{:S(2)}, u32[]{:S(2)}) collective-permute-start(f32[96,768]{1,0:T(8,128)S(1)} %get-tuple-element.223.refs_2_), channel_id=1, source_target_pairs={{0,4},{8,0},{16,8},{24,16},{28,24},{20,28},{12,20},{4,12},{1,5},{9... | collective-permute-start | bytes 884744 | tf_op jit(solution)/shard_map/ppermute | solution.py:181
  176.6 13.9 %collective-permute-start.72 = (f32[96,768]{1,0:T(8,128)}, f32[96,768]{1,0:T(8,128)}, u32[]{:S(2)}, u32[]{:S(2)}) collective-permute-start(f32[96,768]{1,0:T(8,128)} %collective-permute-done.71.refs_5_), channel_id=1, source_target_pairs={{0,8},{8,16},{16,24},{24,28},{28,20},{20,12},{12,4},{4,0},{1,9},{9... | collective-permute-start | bytes 884744 | tf_op jit(solution)/shard_map/ppermute | solution.py:181
  178.8 13.5 %collective-permute-start.78 = (f32[96,768]{1,0:T(8,128)}, f32[96,768]{1,0:T(8,128)}, u32[]{:S(2)}, u32[]{:S(2)}) collective-permute-start(f32[96,768]{1,0:T(8,128)} %collective-permute-done.77.refs_6_), channel_id=1, source_target_pairs={{0,4},{8,0},{16,8},{24,16},{28,24},{20,28},{12,20},{4,12},{1,5},{9... | collective-permute-start | bytes 884744 | tf_op jit(solution)/shard_map/ppermute | solution.py:181
  182.1 11.2 %collective-permute-start.38 = (f32[16,1152]{1,0:T(8,128)}, f32[16,1152]{1,0:T(8,128)S(1)}, u32[]{:S(2)}, u32[]{:S(2)}) collective-permute-start(f32[16,1152]{1,0:T(8,128)} %get-tuple-element.233), channel_id=1, source_target_pairs={{0,16},{4,20},{8,24},{12,28},{16,0},{20,4},{24,8},{28,12},{1,17},{... | collective-permute-start | bytes 221192 | tf_op jit(solution)/shard_map/ppermute | solution.py:39
  184.7 11.6 %collective-permute-start.52 = (f32[48,768]{1,0:T(8,128)S(1)}, f32[48,768]{1,0:T(8,128)S(1)}, u32[]{:S(2)}, u32[]{:S(2)}) collective-permute-start(f32[48,768]{1,0:T(8,128)S(1)} %get-tuple-element.212.refs_0_), channel_id=1, source_target_pairs={{0,8},{8,16},{16,24},{24,28},{28,20},{20,12},{12,4},{4,0},{1,9},{9... | collective-permute-start | bytes 442376 | tf_op jit(solution)/shard_map/ppermute | solution.py:181
  190.4 14.4 %collective-permute-start.73 = (f32[96,768]{1,0:T(8,128)}, f32[96,768]{1,0:T(8,128)S(1)}, u32[]{:S(2)}, u32[]{:S(2)}) collective-permute-start(f32[96,768]{1,0:T(8,128)} %collective-permute-done.72.refs_7_), channel_id=1, source_target_pairs={{0,8},{8,16},{16,24},{24,28},{28,20},{20,12},{12,4},{4,0},{1,9},{9... | collective-permute-start | bytes 884744 | tf_op jit(solution)/shard_map/ppermute | solution.py:181
  192.3 13.7 %collective-permute-start.79 = (f32[96,768]{1,0:T(8,128)}, f32[96,768]{1,0:T(8,128)S(1)}, u32[]{:S(2)}, u32[]{:S(2)}) collective-permute-start(f32[96,768]{1,0:T(8,128)} %collective-permute-done.78.refs_8_), channel_id=1, source_target_pairs={{0,4},{8,0},{16,8},{24,16},{28,24},{20,28},{12,20},{4,12},{1,5},{9... | collective-permute-start | bytes 884744 | tf_op jit(solution)/shard_map/ppermute | solution.py:181
  193.3 13.5 %collective-permute-start.39 = (f32[16,1152]{1,0:T(8,128)}, f32[16,1152]{1,0:T(8,128)S(1)}, u32[]{:S(2)}, u32[]{:S(2)}) collective-permute-start(f32[16,1152]{1,0:T(8,128)} %get-tuple-element.233), channel_id=1, source_target_pairs={{0,24},{4,28},{8,0},{12,4},{16,8},{20,12},{24,16},{28,20},{1,25},{... | collective-permute-start | bytes 221192 | tf_op jit(solution)/shard_map/ppermute | solution.py:39
  204.9 13.3 %collective-permute-start.74 = (f32[96,768]{1,0:T(8,128)S(1)}, f32[96,768]{1,0:T(8,128)S(1)}, u32[]{:S(2)}, u32[]{:S(2)}) collective-permute-start(f32[96,768]{1,0:T(8,128)S(1)} %collective-permute-done.73.refs_9_), channel_id=1, source_target_pairs={{0,8},{8,16},{16,24},{24,28},{28,20},{20,12},{12,4},{4,0},{1,9},{9... | collective-permute-start | bytes 884744 | tf_op jit(solution)/shard_map/ppermute | solution.py:181
  206.0 13.9 %collective-permute-start.80 = (f32[96,768]{1,0:T(8,128)S(1)}, f32[96,768]{1,0:T(8,128)S(1)}, u32[]{:S(2)}, u32[]{:S(2)}) collective-permute-start(f32[96,768]{1,0:T(8,128)S(1)} %collective-permute-done.79.refs_10_), channel_id=1, source_target_pairs={{0,4},{8,0},{16,8},{24,16},{28,24},{20,28},{12,20},{4,12},{1,5},{9... | collective-permute-start | bytes 884744 | tf_op jit(solution)/shard_map/ppermute | solution.py:181
  211.0 12.5 %collective-permute-start.58 = (f32[48,768]{1,0:T(8,128)}, f32[48,768]{1,0:T(8,128)S(1)}, u32[]{:S(2)}, u32[]{:S(2)}) collective-permute-start(f32[48,768]{1,0:T(8,128)} %collective-permute-done.56.refs_6_), channel_id=1, source_target_pairs={{0,8},{8,16},{16,24},{24,28},{28,20},{20,12},{12,4},{4,0},{1,9},{9... | collective-permute-start | bytes 442376 | tf_op jit(solution)/shard_map/ppermute | solution.py:181
  212.1 13.0 %collective-permute-start.59 = (f32[48,768]{1,0:T(8,128)}, f32[48,768]{1,0:T(8,128)}, u32[]{:S(2)}, u32[]{:S(2)}) collective-permute-start(f32[48,768]{1,0:T(8,128)} %collective-permute-done.57.refs_7_), channel_id=1, source_target_pairs={{0,4},{8,0},{16,8},{24,16},{28,24},{20,28},{12,20},{4,12},{1,5},{9... | collective-permute-start | bytes 442376 | tf_op jit(solution)/shard_map/ppermute | solution.py:181
  218.2 14.4 %collective-permute-start.75 = (f32[96,768]{1,0:T(8,128)S(1)}, f32[96,768]{1,0:T(8,128)S(1)}, u32[]{:S(2)}, u32[]{:S(2)}) collective-permute-start(f32[96,768]{1,0:T(8,128)S(1)} %collective-permute-done.74.refs_11_), channel_id=1, source_target_pairs={{0,8},{8,16},{16,24},{24,28},{28,20},{20,12},{12,4},{4,0},{1,9},{9... | collective-permute-start | bytes 884744 | tf_op jit(solution)/shard_map/ppermute | solution.py:181
  219.9 14.1 %collective-permute-start.81 = (f32[96,768]{1,0:T(8,128)S(1)}, f32[96,768]{1,0:T(8,128)S(1)}, u32[]{:S(2)}, u32[]{:S(2)}) collective-permute-start(f32[96,768]{1,0:T(8,128)S(1)} %collective-permute-done.80.refs_12_), channel_id=1, source_target_pairs={{0,4},{8,0},{16,8},{24,16},{28,24},{20,28},{12,20},{4,12},{1,5},{9... | collective-permute-start | bytes 884744 | tf_op jit(solution)/shard_map/ppermute | solution.py:181
  232.6 23.0 %collective-permute-start.82 = (f32[96,768]{1,0:T(8,128)S(1)}, f32[96,768]{1,0:T(8,128)S(1)}, u32[]{:S(2)}, u32[]{:S(2)}) collective-permute-start(f32[96,768]{1,0:T(8,128)S(1)} %collective-permute-done.75.refs_0_), channel_id=1, source_target_pairs={{0,8},{8,16},{16,24},{24,28},{28,20},{20,12},{12,4},{4,0},{1,9},{9... | collective-permute-start | bytes 884744 | tf_op jit(solution)/shard_map/ppermute | solution.py:181
  234.0 21.6 %collective-permute-start.83 = (f32[96,768]{1,0:T(8,128)S(1)}, f32[96,768]{1,0:T(8,128)S(1)}, u32[]{:S(2)}, u32[]{:S(2)}) collective-permute-start(f32[96,768]{1,0:T(8,128)S(1)} %collective-permute-done.81.refs_1_), channel_id=1, source_target_pairs={{0,4},{8,0},{16,8},{24,16},{28,24},{20,28},{12,20},{4,12},{1,5},{9... | collective-permute-start | bytes 884744 | tf_op jit(solution)/shard_map/ppermute | solution.py:181
  (91 other events, 856.6 us)

commit v6 on v4

--- a/solution.py
+++ b/solution.py
@@ -51,8 +51,8 @@
     return total
 
 
-VMEM_LIMIT = 20 * 1024 * 1024
-SMALL_LIMIT = 8 * 1024 * 1024
+VMEM_LIMIT = 14 * 1024 * 1024
+SMALL_LIMIT = 6 * 1024 * 1024
 GELU_SCALE = (2.0 / math.pi) ** 0.5
 IN_VMEM = pl.BlockSpec(memory_space=pltpu.VMEM)
 IN_SMEM = pl.BlockSpec(memory_space=pltpu.SMEM)

time: 255 us -> 256 us (level)
  local copies, waits for them, and re-layouts: 7.3 us -> 11.8 us
  waiting for transfers between devices: 103 us -> 100 us
    unnamed x48 -> x76, local copies, waits for them, and re-layouts: 5.07 us -> 9.56 us
    ppermute x56, waiting for transfers between devices: 63.8 us -> 60.9 us  [step(): lax.ppermute(held, 'dp', perm)]
  transfers between devices with their start and end apart: 87 -> 87, of which waited for: 37 -> 36; matrix products, arithmetic and copies ran while one was open for 4% -> 4% of each run, Pallas kernels for 17% -> 17%
where the time goes in v6:
time: 256 us
  waiting for transfers between devices  100 us (39%)
  starting transfers between devices  79.3 us (31%)
  Pallas kernels  53.4 us (21%)
  local copies, waits for them, and re-layouts  11.8 us (5%)
  matrix products  5.92 us (2%)
  other arithmetic  3.69 us (1%)
    ppermute x56, waiting for transfers between devices, step(): lax.ppermute(held, 'dp', perm)  60.9 us
    ppermute x56, starting transfers between devices, step(): lax.ppermute(held, 'dp', perm)  57.7 us
    pallas_call x33, Pallas kernels, call(): pl.pallas_call(kernel, out_shape=out_shape, in_specs=[IN_SMEM] * scalars...  42.5 us
    ppermute x27, waiting for transfers between devices, swap(): lax.ppermute(values, 'tensor', [(at, at ^ bit) for at in range(size)])  35.6 us
    ppermute x27, starting transfers between devices, swap(): lax.ppermute(values, 'tensor', [(at, at ^ bit) for at in range(size)])  15.6 us
    pallas_call x4, Pallas kernels, place_rows(): pl.pallas_call(functools.partial(place_kernel, steps, size, first, target...  10.8 us
    unnamed x76, local copies, waits for them, and re-layouts  9.56 us
    ppermute x3, starting transfers between devices, gather_latents(): lax.ppermute(pair, 'dp', [(at, (at + step) % size) for at in range(size)])  5.61 us
  transfers between devices with their start and end apart: 87, of which 36 were waited for; matrix products, arithmetic and copies ran while one was open for 4% of the time, Pallas kernels for 17%

profile of v6, /device:TPU:0, one launch (start us, length us, event | category | flops | bytes accessed | tf_op | source)
XLA Modules:
  0.0 255.9 jit_solution(16348358391767100663)
XLA Ops:
  4.2 2.6 collective-permute-start.1
  13.6 3.9 %collective-permute-done.4 = f32[2,1152]{1,0:T(2,128)S(1)} collective-permute-done((f32[2,1152]{1,0:T(2,128)S(1)}, f32[2,1152]{1,0:T(2,128)S(1)}, u32[]{:S(2)}, u32[]{:S(2)}) %collective-permute-start.4) | collective-permute-done | bytes 9248 | tf_op jit(solution)/shard_map/ppermute | solution.py:18
  17.6 3.7 %shard_map.272 = (bf16[512,768]{1,0:T(8,128)(2,1)S(1)}, bf16[512,192]{1,0:T(8,128)(2,1)S(1)}, bf16[512,192]{1,0:T(8,128)(2,1)S(1)}, bf16[512,192]{1,0:T(8,128)(2,1)S(1)}, f32[512,192]{1,0:T(8,128)S(1)}) custom-call(s32[15,2]{1,0:T(8,128)S(1)} %add_select_fusion.table_ref.spots_ref, s32[2]{0:T(128)S(1)} %pad_add_fusion.flags_ref.odd_ref, ...), custom_call_target="tpu_custom_call" | custom-call | flops 1 | bytes 1 | tf_op jit(solution)/shard_map/pallas_call | solution.py:66
  24.8 11.3 %collective-permute-done.7.across_ref = f32[512,192]{1,0:T(8,128)S(1)} collective-permute-done((f32[512,192]{1,0:T(8,128)S(1)}, f32[512,192]{1,0:T(8,128)S(1)}, u32[]{:S(2)}, u32[]{:S(2)}) %collective-permute-start.7) | collective-permute-done | bytes 393248 | tf_op jit(solution)/shard_map/ppermute | solution.py:18
  36.6 5.0 %collective-permute-done.12.mixing_5_ref = f32[96,768]{1,0:T(8,128)S(1)} collective-permute-done((f32[96,768]{1,0:T(8,128)S(1)}, f32[96,768]{1,0:T(8,128)S(1)}, u32[]{:S(2)}, u32[]{:S(2)}) %collective-permute-start.12) | collective-permute-done | bytes 294944 | tf_op jit(solution)/shard_map/ppermute | solution.py:18
  43.6 5.2 %shard_map.276 = (f32[512,768]{1,0:T(8,128)S(1)}, bf16[512,768]{1,0:T(8,128)(2,1)S(1)}, bf16[512,768]{1,0:T(8,128)(2,1)S(1)}, bf16[512,768]{1,0:T(8,128)(2,1)S(1...) custom-call(s32[2]{0:T(128)S(1)} %pad_add_fusion.flags_ref.odd_ref, ...), custom_call_target="tpu_custom_call" | custom-call | flops 1 | bytes 1 | tf_op jit(solution)/shard_map/pallas_call | solution.py:66
  48.9 2.2 collective-permute-done.15.right_ref
  51.2 2.9 %shard_map.278 = (f32[768,768]{1,0:T(8,128)S(1)}, f32[768,768]{1,0:T(8,128)S(1)}, f32[2,768]{1,0:T(2,128)S(1)}, f32[96,768]{1,0:T(8,128)S(1)}, f32[96,768]{1,0:T...) custom-call(s32[15,2]{1,0:T(8,128)S(1)} %add_select_fusion.table_ref.spots_ref, ...), custom_call_target="tpu_custom_call" | custom-call | flops 1 | bytes 1 | tf_op jit(solution)/shard_map/pallas_call | solution.py:66
  58.1 7.0 %collective-permute-done.18.refs_0_ = f32[96,768]{1,0:T(8,128)S(1)} collective-permute-done((f32[96,768]{1,0:T(8,128)S(1)}, f32[96,768]{1,0:T(8,128)S(1)}, u32[]{:S(2)}, u32[]{:S(2)}) %collective-permute-start.18) | collective-permute-done | bytes 294944 | tf_op jit(solution)/shard_map/ppermute | solution.py:180
  69.2 5.8 %collective-permute-done.20.refs_0_ = f32[96,768]{1,0:T(8,128)S(1)} collective-permute-done((f32[96,768]{1,0:T(8,128)S(1)}, f32[96,768]{1,0:T(8,128)S(1)}, u32[]{:S(2)}, u32[]{:S(2)}) %collective-permute-start.20) | collective-permute-done | bytes 294944 | tf_op jit(solution)/shard_map/ppermute | solution.py:180
  80.0 2.1 shard_map.284
  82.1 4.7 %collective-permute-done.26.refs_1_ = f32[96,768]{1,0:T(8,128)S(1)} collective-permute-done((f32[96,768]{1,0:T(8,128)S(1)}, f32[96,768]{1,0:T(8,128)S(1)}, u32[]{:S(2)}, u32[]{:S(2)}) %collective-permute-start.26) | collective-permute-done | bytes 294944 | tf_op jit(solution)/shard_map/ppermute | solution.py:180
  87.7 5.2 %shard_map.286 = (bf16[512,192]{1,0:T(8,128)(2,1)S(1)}, bf16[512,192]{1,0:T(8,128)(2,1)S(1)}, bf16[512,192]{1,0:T(8,128)(2,1)S(1)}, f32[256,768]{1,0:T(8,128)S(1)}, f32[256,768]{1,0:T(8,128)S(1)}) custom-call(s32[2]{0:T(128)S(1)} %pad_add_fusion.flags_ref.odd_ref, bf16[512,768]{1,0:T(8,128)(2,1)S(1)} %get-tuple-element.162.d_attn_ref, ...), custom_call_target="tpu_custom_call" | custom-call | flops 1 | bytes 1 | tf_op jit(solution)/shard_map/pallas_call | solution.py:66
  95.1 3.7 %collective-permute-done.22.right_ref = f32[256,768]{1,0:T(8,128)S(1)} collective-permute-done((f32[256,768]{1,0:T(8,128)S(1)}, f32[256,768]{1,0:T(8,128)S(1)}, u32[]{:S(2)}, u32[]{:S(2)}) %collective-permute-start.22) | collective-permute-done | bytes 786464 | tf_op jit(solution)/shard_map/ppermute | solution.py:18
  98.9 3.5 %collective-permute-done.29.refs_1_ = f32[96,768]{1,0:T(8,128)S(1)} collective-permute-done((f32[96,768]{1,0:T(8,128)S(1)}, f32[96,768]{1,0:T(8,128)S(1)}, u32[]{:S(2)}, u32[]{:S(2)}) %collective-permute-start.29) | collective-permute-done | bytes 294944 | tf_op jit(solution)/shard_map/ppermute | solution.py:180
  110.1 2.3 shard_map.290
  112.5 3.1 %collective-permute-done.34.refs_1_ = f32[48,768]{1,0:T(8,128)S(1)} collective-permute-done((f32[48,768]{1,0:T(8,128)S(1)}, f32[48,768]{1,0:T(8,128)S(1)}, u32[]{:S(2)}, u32[]{:S(2)}) %collective-permute-start.34) | collective-permute-done | bytes 147488 | tf_op jit(solution)/shard_map/ppermute | solution.py:180
  118.3 4.1 %collective-permute-done.30.right_ref = f32[256,768]{1,0:T(8,128)S(1)} collective-permute-done((f32[256,768]{1,0:T(8,128)S(1)}, f32[256,768]{1,0:T(8,128)S(1)}, u32[]{:S(2)}, u32[]{:S(2)}) %collective-permute-start.30) | collective-permute-done | bytes 786464 | tf_op jit(solution)/shard_map/ppermute | solution.py:18
  126.7 3.0 %shard_map.294 = (f32[512,768]{1,0:T(8,128)}, f32[2,768]{1,0:T(2,128)S(1)}, f32[2,768]{1,0:T(2,128)S(1)}) custom-call(s32[2]{0:T(128)S(1)} %pad_add_fusion.flags_ref.odd_ref, f32[256,768]{1,0:T(8,128)S(1)} %shard_map.293.full_ref, f32[256,768]{1,0:T(8,128)S(1)} %collective-permute-done.35.other_ref, bf16[512,768]{1,0:T(8,128)(2,1)S(1)} %copy-done.2, ...), custom_call_target="tpu_custom_call" | custom-call | flops 1 | bytes 1 | tf_op jit(solution)/shard_map/pallas_call | solution.py:66
  130.2 2.2 collective-permute-done.67.refs_1_
  139.6 6.3 %collective-permute-done.42.refs_0_ = f32[48,768]{1,0:T(8,128)S(1)} collective-permute-done((f32[48,768]{1,0:T(8,128)S(1)}, f32[48,768]{1,0:T(8,128)S(1)}, u32[]{:S(2)}, u32[]{:S(2)}) %collective-permute-start.42) | collective-permute-done | bytes 147488 | tf_op jit(solution)/shard_map/ppermute | solution.py:180
  158.8 2.9 %collective-permute-done.46.refs_0_ = f32[48,768]{1,0:T(8,128)S(1)} collective-permute-done((f32[48,768]{1,0:T(8,128)}, f32[48,768]{1,0:T(8,128)S(1)}, u32[]{:S(2)}, u32[]{:S(2)}) %collective-permute-start.46) | collective-permute-done | bytes 147488 | tf_op jit(solution)/shard_map/ppermute | solution.py:180
  170.1 2.2 collective-permute-done.49.refs_1_
  186.6 3.7 %collective-permute-done.37 = f32[16,1152]{1,0:T(8,128)} collective-permute-done((f32[16,1152]{1,0:T(8,128)}, f32[16,1152]{1,0:T(8,128)}, u32[]{:S(2)}, u32[]{:S(2)}) %collective-permute-start.37) | collective-permute-done | bytes 73760 | tf_op jit(solution)/shard_map/ppermute | solution.py:39
  193.3 3.0 %collective-permute-start.39 = (f32[16,1152]{1,0:T(8,128)}, f32[16,1152]{1,0:T(8,128)S(1)}, u32[]{:S(2)}, u32[]{:S(2)}) collective-permute-start(f32[16,1152]{1,0:T(8,128)} %get-tuple-element.247), channel_id=1, source_target_pairs={{0,24},{4,28},{8,0},{12,4},{16,8},{20,12},{24,16},{28,20},{1,25},{... | collective-permute-start | bytes 221192 | tf_op jit(solution)/shard_map/ppermute | solution.py:39
  199.1 3.5 %collective-permute-done.53.refs_4_ = f32[48,768]{1,0:T(8,128)S(1)} collective-permute-done((f32[48,768]{1,0:T(8,128)S(1)}, f32[48,768]{1,0:T(8,128)S(1)}, u32[]{:S(2)}, u32[]{:S(2)}) %collective-permute-start.53) | collective-permute-done | bytes 147488 | tf_op jit(solution)/shard_map/ppermute | solution.py:180
  208.4 2.6 %shard_map.296 = (f32[768,1152]{1,0:T(8,128)}, f32[1,1152]{1,0:T(1,128)S(1)}, f32[16,768]{1,0:T(8,128)S(1)}, f32[5,1152]{1,0:T(8,128)S(1)}) custom-call(f32[64,1152]{1,0:T(8,128)S(1)} %constant_dynamic-update-slice_fusion.carried_ref, bf16[16,768]{1,0:T(8,128)(2,1)S(1)} %multiply_convert_fusion.silu_ref, bf16[768,1152]{1,0:T(8,128)(2,1)S(1)} %copy-done.4), custom_call_target="tpu_custom_call" | custom-call | flops 1 | bytes 1 | tf_op jit(solution)/shard_map/pallas_call | solution.py:66
  215.5 2.8 %collective-permute-done.86 = f32[16,192]{1,0:T(8,128)} collective-permute-done((f32[16,192]{1,0:T(8,128)S(1)}, f32[16,192]{1,0:T(8,128)}, u32[]{:S(2)}, u32[]{:S(2)}) %collective-permute-start.86) | collective-permute-done | bytes 12320 | tf_op jit(solution)/shard_map/ppermute | solution.py:18
  227.2 3.8 %collective-permute-done.56.refs_10_ = f32[48,768]{1,0:T(8,128)S(1)} collective-permute-done((f32[48,768]{1,0:T(8,128)S(1)}, f32[48,768]{1,0:T(8,128)S(1)}, u32[]{:S(2)}, u32[]{:S(2)}) %collective-permute-start.56) | collective-permute-done | bytes 147488 | tf_op jit(solution)/shard_map/ppermute | solution.py:180
  244.8 2.6 %shard_map.303 = (f32[576,768]{1,0:T(8,128)}, f32[192,768]{1,0:T(8,128)}, f32[8,128]{1,0:T(8,128)}) custom-call(s32[15,2]{1,0:T(8,128)S(1)} %add_select_fusion.table_ref.spots_ref, f32[48,768]{1,0:T(8,128)S(1)} %get-tuple-element.219.refs_0_, f32[48,768]{1,0:T(8,128)S(1)} %copy-done.14, f32[48,768]{1,0:T(8,128)S(1)} %copy-done.16, f32[48,768]{1,0:T(8,128)S(1)} %copy-done.18, ...), custom_call_target="tpu_custom_call" | custom-call | flops 1 | bytes 1 | tf_op jit(solution)/shard_map/pallas_call | solution.py:130
  249.6 3.8 %shard_map.307 = (f32[768,768]{1,0:T(8,128)}, f32[768,768]{1,0:T(8,128)}, f32[8,128]{1,0:T(8,128)}) custom-call(s32[15,2]{1,0:T(8,128)S(1)} %add_select_fusion.table_ref.spots_ref, f32[96,768]{1,0:T(8,128)S(1)} %get-tuple-element.233.refs_0_, f32[96,768]{1,0:T(8,128)S(1)} %get-tuple-element.234.refs_1_, f32[96,768]{1,0:T(8,128)S(1)} %copy-done.12, ...), custom_call_target="tpu_custom_call" | custom-call | flops 1 | bytes 1 | tf_op jit(solution)/shard_map/pallas_call | solution.py:130
  253.4 2.3 shard_map.308
  (282 shorter events, 131.6 us)
Async XLA Ops:
  7.9 28.2 %collective-permute-start.11 = (f32[96,768]{1,0:T(8,128)S(1)}, f32[96,768]{1,0:T(8,128)S(1)}, u32[]{:S(2)}, u32[]{:S(2)}) collective-permute-start(f32[96,768]{1,0:T(8,128)S(1)} %shard_map.274.mixing_0_ref), channel_id=1, source_target_pairs={{0,2},{1,3},{2,0},{3,1},{4,6},{5,7},{6,4},{7,5},{8,10},{9,11},{10,... | collective-permute-start | bytes 884744 | tf_op jit(solution)/shard_map/ppermute | solution.py:18
  21.2 14.8 %collective-permute-start.7 = (f32[512,192]{1,0:T(8,128)S(1)}, f32[512,192]{1,0:T(8,128)S(1)}, u32[]{:S(2)}, u32[]{:S(2)}) collective-permute-start(f32[512,192]{1,0:T(8,128)S(1)} %get-tuple-element.129.own_ref.attended_ref), channel_id=1, source_target_pairs={{0,2},{1,3},{2,0},{3,1},{4,6},{5,7},{6,4},{7,5},{8,10},{9,11},{10,... | collective-permute-start | bytes 1179656 | tf_op jit(solution)/shard_map/ppermute | solution.py:18
  23.1 18.5 %collective-permute-start.12 = (f32[96,768]{1,0:T(8,128)S(1)}, f32[96,768]{1,0:T(8,128)S(1)}, u32[]{:S(2)}, u32[]{:S(2)}) collective-permute-start(f32[96,768]{1,0:T(8,128)S(1)} %shard_map.275.mixing_1_ref), channel_id=1, source_target_pairs={{0,2},{1,3},{2,0},{3,1},{4,6},{5,7},{6,4},{7,5},{8,10},{9,11},{10,... | collective-permute-start | bytes 884744 | tf_op jit(solution)/shard_map/ppermute | solution.py:18
  23.4 18.1 %collective-permute-start.9 = (f32[96,768]{1,0:T(8,128)S(1)}, f32[96,768]{1,0:T(8,128)S(1)}, u32[]{:S(2)}, u32[]{:S(2)}) collective-permute-start(f32[96,768]{1,0:T(8,128)S(1)} %shard_map.274.mixing_0_ref), channel_id=1, source_target_pairs={{0,1},{1,0},{2,3},{3,2},{4,5},{5,4},{6,7},{7,6},{8,9},{9,8},{10,11... | collective-permute-start | bytes 884744 | tf_op jit(solution)/shard_map/ppermute | solution.py:18
  23.4 18.6 %collective-permute-start.6 = (f32[512,192]{1,0:T(8,128)S(1)}, f32[512,192]{1,0:T(8,128)S(1)}, u32[]{:S(2)}, u32[]{:S(2)}) collective-permute-start(f32[512,192]{1,0:T(8,128)S(1)} %get-tuple-element.129.own_ref.attended_ref), channel_id=1, source_target_pairs={{0,1},{1,0},{2,3},{3,2},{4,5},{5,4},{6,7},{7,6},{8,9},{9,8},{10,11... | collective-permute-start | bytes 1179656 | tf_op jit(solution)/shard_map/ppermute | solution.py:18
  54.1 22.9 %collective-permute-start.16 = (f32[256,768]{1,0:T(8,128)S(1)}, f32[256,768]{1,0:T(8,128)S(1)}, u32[]{:S(2)}, u32[]{:S(2)}) collective-permute-start(f32[256,768]{1,0:T(8,128)S(1)} %get-tuple-element.144), channel_id=1, source_target_pairs={{0,1},{1,0},{2,3},{3,2},{4,5},{5,4},{6,7},{7,6},{8,9},{9,8},{10,11... | collective-permute-start | bytes 2359304 | tf_op jit(solution)/shard_map/ppermute | solution.py:18
  54.3 22.8 %collective-permute-start.17 = (f32[256,768]{1,0:T(8,128)S(1)}, f32[256,768]{1,0:T(8,128)S(1)}, u32[]{:S(2)}, u32[]{:S(2)}) collective-permute-start(f32[256,768]{1,0:T(8,128)S(1)} %shard_map.277.left_ref), channel_id=1, source_target_pairs={{0,2},{1,3},{2,0},{3,1},{4,6},{5,7},{6,4},{7,5},{8,10},{9,11},{10,... | collective-permute-start | bytes 2359304 | tf_op jit(solution)/shard_map/ppermute | solution.py:18
  79.4 19.3 %collective-permute-start.22 = (f32[256,768]{1,0:T(8,128)S(1)}, f32[256,768]{1,0:T(8,128)S(1)}, u32[]{:S(2)}, u32[]{:S(2)}) collective-permute-start(f32[256,768]{1,0:T(8,128)S(1)} %shard_map.279.left_ref), channel_id=1, source_target_pairs={{0,2},{1,3},{2,0},{3,1},{4,6},{5,7},{6,4},{7,5},{8,10},{9,11},{10,... | collective-permute-start | bytes 2359304 | tf_op jit(solution)/shard_map/ppermute | solution.py:18
  98.8 10.8 %collective-permute-start.23 = (f32[256,768]{1,0:T(8,128)S(1)}, f32[256,768]{1,0:T(8,128)S(1)}, u32[]{:S(2)}, u32[]{:S(2)}) collective-permute-start(f32[256,768]{1,0:T(8,128)S(1)} %shard_map.283.full_ref), channel_id=1, source_target_pairs={{0,1},{1,0},{2,3},{3,2},{4,5},{5,4},{6,7},{7,6},{8,9},{9,8},{10,11... | collective-permute-start | bytes 2359304 | tf_op jit(solution)/shard_map/ppermute | solution.py:18
  103.5 18.9 %collective-permute-start.30 = (f32[256,768]{1,0:T(8,128)S(1)}, f32[256,768]{1,0:T(8,128)S(1)}, u32[]{:S(2)}, u32[]{:S(2)}) collective-permute-start(f32[256,768]{1,0:T(8,128)S(1)} %shard_map.288.left_ref), channel_id=1, source_target_pairs={{0,2},{1,3},{2,0},{3,1},{4,6},{5,7},{6,4},{7,5},{8,10},{9,11},{10,... | collective-permute-start | bytes 2359304 | tf_op jit(solution)/shard_map/ppermute | solution.py:18
  104.4 13.1 %collective-permute-start.32 = (f32[96,768]{1,0:T(8,128)S(1)}, f32[96,768]{1,0:T(8,128)S(1)}, u32[]{:S(2)}, u32[]{:S(2)}) collective-permute-start(f32[96,768]{1,0:T(8,128)S(1)} %get-tuple-element.183), channel_id=1, source_target_pairs={{0,4},{8,0},{16,8},{24,16},{28,24},{20,28},{12,20},{4,12},{1,5},{9... | collective-permute-start | bytes 884744 | tf_op jit(solution)/shard_map/ppermute | solution.py:180
  106.0 11.6 %collective-permute-start.31 = (f32[96,768]{1,0:T(8,128)S(1)}, f32[96,768]{1,0:T(8,128)S(1)}, u32[]{:S(2)}, u32[]{:S(2)}) collective-permute-start(f32[96,768]{1,0:T(8,128)S(1)} %get-tuple-element.174), channel_id=1, source_target_pairs={{0,8},{8,16},{16,24},{24,28},{28,20},{20,12},{12,4},{4,0},{1,9},{9... | collective-permute-start | bytes 884744 | tf_op jit(solution)/shard_map/ppermute | solution.py:180
  124.6 12.2 %collective-permute-start.41 = (f32[48,768]{1,0:T(8,128)S(1)}, f32[48,768]{1,0:T(8,128)S(1)}, u32[]{:S(2)}, u32[]{:S(2)}) collective-permute-start(f32[48,768]{1,0:T(8,128)S(1)} %get-tuple-element.206), channel_id=1, source_target_pairs={{0,4},{8,0},{16,8},{24,16},{28,24},{20,28},{12,20},{4,12},{1,5},{9... | collective-permute-start | bytes 442376 | tf_op jit(solution)/shard_map/ppermute | solution.py:180
  134.7 13.9 %collective-permute-start.68 = (f32[96,768]{1,0:T(8,128)S(1)}, f32[96,768]{1,0:T(8,128)S(1)}, u32[]{:S(2)}, u32[]{:S(2)}) collective-permute-start(f32[96,768]{1,0:T(8,128)S(1)} %get-tuple-element.231), channel_id=1, source_target_pairs={{0,8},{8,16},{16,24},{24,28},{28,20},{20,12},{12,4},{4,0},{1,9},{9... | collective-permute-start | bytes 884744 | tf_op jit(solution)/shard_map/ppermute | solution.py:180
  135.3 13.4 %collective-permute-start.69 = (f32[96,768]{1,0:T(8,128)S(1)}, f32[96,768]{1,0:T(8,128)S(1)}, u32[]{:S(2)}, u32[]{:S(2)}) collective-permute-start(f32[96,768]{1,0:T(8,128)S(1)} %get-tuple-element.232), channel_id=1, source_target_pairs={{0,4},{8,0},{16,8},{24,16},{28,24},{20,28},{12,20},{4,12},{1,5},{9... | collective-permute-start | bytes 884744 | tf_op jit(solution)/shard_map/ppermute | solution.py:180
  149.4 17.0 %collective-permute-start.70 = (f32[96,768]{1,0:T(8,128)S(1)}, f32[96,768]{1,0:T(8,128)S(1)}, u32[]{:S(2)}, u32[]{:S(2)}) collective-permute-start(f32[96,768]{1,0:T(8,128)S(1)} %get-tuple-element.233.refs_0_), channel_id=1, source_target_pairs={{0,8},{8,16},{16,24},{24,28},{28,20},{20,12},{12,4},{4,0},{1,9},{9... | collective-permute-start | bytes 884744 | tf_op jit(solution)/shard_map/ppermute | solution.py:180
  151.0 17.0 %collective-permute-start.76 = (f32[96,768]{1,0:T(8,128)S(1)}, f32[96,768]{1,0:T(8,128)}, u32[]{:S(2)}, u32[]{:S(2)}) collective-permute-start(f32[96,768]{1,0:T(8,128)S(1)} %get-tuple-element.234.refs_1_), channel_id=1, source_target_pairs={{0,4},{8,0},{16,8},{24,16},{28,24},{20,28},{12,20},{4,12},{1,5},{9... | collective-permute-start | bytes 884744 | tf_op jit(solution)/shard_map/ppermute | solution.py:180
  176.6 13.9 %collective-permute-start.72 = (f32[96,768]{1,0:T(8,128)}, f32[96,768]{1,0:T(8,128)}, u32[]{:S(2)}, u32[]{:S(2)}) collective-permute-start(f32[96,768]{1,0:T(8,128)} %collective-permute-done.71.refs_4_), channel_id=1, source_target_pairs={{0,8},{8,16},{16,24},{24,28},{28,20},{20,12},{12,4},{4,0},{1,9},{9... | collective-permute-start | bytes 884744 | tf_op jit(solution)/shard_map/ppermute | solution.py:180
  178.8 13.5 %collective-permute-start.78 = (f32[96,768]{1,0:T(8,128)}, f32[96,768]{1,0:T(8,128)}, u32[]{:S(2)}, u32[]{:S(2)}) collective-permute-start(f32[96,768]{1,0:T(8,128)} %collective-permute-done.77.refs_5_), channel_id=1, source_target_pairs={{0,4},{8,0},{16,8},{24,16},{28,24},{20,28},{12,20},{4,12},{1,5},{9... | collective-permute-start | bytes 884744 | tf_op jit(solution)/shard_map/ppermute | solution.py:180
  182.1 11.2 %collective-permute-start.38 = (f32[16,1152]{1,0:T(8,128)}, f32[16,1152]{1,0:T(8,128)S(1)}, u32[]{:S(2)}, u32[]{:S(2)}) collective-permute-start(f32[16,1152]{1,0:T(8,128)} %get-tuple-element.247), channel_id=1, source_target_pairs={{0,16},{4,20},{8,24},{12,28},{16,0},{20,4},{24,8},{28,12},{1,17},{... | collective-permute-start | bytes 221192 | tf_op jit(solution)/shard_map/ppermute | solution.py:39
  184.7 11.6 %collective-permute-start.52 = (f32[48,768]{1,0:T(8,128)S(1)}, f32[48,768]{1,0:T(8,128)S(1)}, u32[]{:S(2)}, u32[]{:S(2)}) collective-permute-start(f32[48,768]{1,0:T(8,128)S(1)} %get-tuple-element.219.refs_0_), channel_id=1, source_target_pairs={{0,8},{8,16},{16,24},{24,28},{28,20},{20,12},{12,4},{4,0},{1,9},{9... | collective-permute-start | bytes 442376 | tf_op jit(solution)/shard_map/ppermute | solution.py:180
  190.4 14.4 %collective-permute-start.73 = (f32[96,768]{1,0:T(8,128)}, f32[96,768]{1,0:T(8,128)S(1)}, u32[]{:S(2)}, u32[]{:S(2)}) collective-permute-start(f32[96,768]{1,0:T(8,128)} %collective-permute-done.72.refs_6_), channel_id=1, source_target_pairs={{0,8},{8,16},{16,24},{24,28},{28,20},{20,12},{12,4},{4,0},{1,9},{9... | collective-permute-start | bytes 884744 | tf_op jit(solution)/shard_map/ppermute | solution.py:180
  192.3 13.7 %collective-permute-start.79 = (f32[96,768]{1,0:T(8,128)}, f32[96,768]{1,0:T(8,128)S(1)}, u32[]{:S(2)}, u32[]{:S(2)}) collective-permute-start(f32[96,768]{1,0:T(8,128)} %collective-permute-done.78.refs_7_), channel_id=1, source_target_pairs={{0,4},{8,0},{16,8},{24,16},{28,24},{20,28},{12,20},{4,12},{1,5},{9... | collective-permute-start | bytes 884744 | tf_op jit(solution)/shard_map/ppermute | solution.py:180
  193.3 13.5 %collective-permute-start.39 = (f32[16,1152]{1,0:T(8,128)}, f32[16,1152]{1,0:T(8,128)S(1)}, u32[]{:S(2)}, u32[]{:S(2)}) collective-permute-start(f32[16,1152]{1,0:T(8,128)} %get-tuple-element.247), channel_id=1, source_target_pairs={{0,24},{4,28},{8,0},{12,4},{16,8},{20,12},{24,16},{28,20},{1,25},{... | collective-permute-start | bytes 221192 | tf_op jit(solution)/shard_map/ppermute | solution.py:39
  204.8 14.2 %collective-permute-start.74 = (f32[96,768]{1,0:T(8,128)S(1)}, f32[96,768]{1,0:T(8,128)S(1)}, u32[]{:S(2)}, u32[]{:S(2)}) collective-permute-start(f32[96,768]{1,0:T(8,128)S(1)} %collective-permute-done.73.refs_8_), channel_id=1, source_target_pairs={{0,8},{8,16},{16,24},{24,28},{28,20},{20,12},{12,4},{4,0},{1,9},{9... | collective-permute-start | bytes 884744 | tf_op jit(solution)/shard_map/ppermute | solution.py:180
  206.0 14.1 %collective-permute-start.80 = (f32[96,768]{1,0:T(8,128)S(1)}, f32[96,768]{1,0:T(8,128)S(1)}, u32[]{:S(2)}, u32[]{:S(2)}) collective-permute-start(f32[96,768]{1,0:T(8,128)S(1)} %collective-permute-done.79.refs_9_), channel_id=1, source_target_pairs={{0,4},{8,0},{16,8},{24,16},{28,24},{20,28},{12,20},{4,12},{1,5},{9... | collective-permute-start | bytes 884744 | tf_op jit(solution)/shard_map/ppermute | solution.py:180
  211.0 12.0 %collective-permute-start.55 = (f32[48,768]{1,0:T(8,128)S(1)}, f32[48,768]{1,0:T(8,128)S(1)}, u32[]{:S(2)}, u32[]{:S(2)}) collective-permute-start(f32[48,768]{1,0:T(8,128)S(1)} %collective-permute-done.54.refs_6_), channel_id=1, source_target_pairs={{0,8},{8,16},{16,24},{24,28},{28,20},{20,12},{12,4},{4,0},{1,9},{9... | collective-permute-start | bytes 442376 | tf_op jit(solution)/shard_map/ppermute | solution.py:180
  212.2 12.5 %collective-permute-start.61 = (f32[48,768]{1,0:T(8,128)S(1)}, f32[48,768]{1,0:T(8,128)S(1)}, u32[]{:S(2)}, u32[]{:S(2)}) collective-permute-start(f32[48,768]{1,0:T(8,128)S(1)} %collective-permute-done.60.refs_7_), channel_id=1, source_target_pairs={{0,4},{8,0},{16,8},{24,16},{28,24},{20,28},{12,20},{4,12},{1,5},{9... | collective-permute-start | bytes 442376 | tf_op jit(solution)/shard_map/ppermute | solution.py:180
  219.0 14.0 %collective-permute-start.75 = (f32[96,768]{1,0:T(8,128)S(1)}, f32[96,768]{1,0:T(8,128)S(1)}, u32[]{:S(2)}, u32[]{:S(2)}) collective-permute-start(f32[96,768]{1,0:T(8,128)S(1)} %collective-permute-done.74.refs_10_), channel_id=1, source_target_pairs={{0,8},{8,16},{16,24},{24,28},{28,20},{20,12},{12,4},{4,0},{1,9},{9... | collective-permute-start | bytes 884744 | tf_op jit(solution)/shard_map/ppermute | solution.py:180
  220.1 13.0 %collective-permute-start.81 = (f32[96,768]{1,0:T(8,128)S(1)}, f32[96,768]{1,0:T(8,128)S(1)}, u32[]{:S(2)}, u32[]{:S(2)}) collective-permute-start(f32[96,768]{1,0:T(8,128)S(1)} %collective-permute-done.80.refs_11_), channel_id=1, source_target_pairs={{0,4},{8,0},{16,8},{24,16},{28,24},{20,28},{12,20},{4,12},{1,5},{9... | collective-permute-start | bytes 884744 | tf_op jit(solution)/shard_map/ppermute | solution.py:180
  233.1 20.3 %collective-permute-start.82 = (f32[96,768]{1,0:T(8,128)S(1)}, f32[96,768]{1,0:T(8,128)S(1)}, u32[]{:S(2)}, u32[]{:S(2)}) collective-permute-start(f32[96,768]{1,0:T(8,128)S(1)} %collective-permute-done.75.refs_0_), channel_id=1, source_target_pairs={{0,8},{8,16},{16,24},{24,28},{28,20},{20,12},{12,4},{4,0},{1,9},{9... | collective-permute-start | bytes 884744 | tf_op jit(solution)/shard_map/ppermute | solution.py:180
  234.1 19.3 %collective-permute-start.83 = (f32[96,768]{1,0:T(8,128)S(1)}, f32[96,768]{1,0:T(8,128)S(1)}, u32[]{:S(2)}, u32[]{:S(2)}) collective-permute-start(f32[96,768]{1,0:T(8,128)S(1)} %collective-permute-done.81.refs_1_), channel_id=1, source_target_pairs={{0,4},{8,0},{16,8},{24,16},{28,24},{20,28},{12,20},{4,12},{1,5},{9... | collective-permute-start | bytes 884744 | tf_op jit(solution)/shard_map/ppermute | solution.py:180
  (93 other events, 831.8 us)
